TPU v7x, 32 devices: a whole 2x2x4 slice. The times are simulated.
32 devices in a mesh: seq: 8 (over z, y), wt: 4 (over x, core).
Axes of the slice: x: 2, y: 2, z: 4, core: 2. Of those that a mesh axis runs over, the one named last changes fastest.
Arguments:
- inputs: bfloat16 [51200, 512], P(('seq', 'wt')), may hold values from -6 to 6
- key_mask: int32 [256, 200], P(('seq', 'wt')), may hold values from 0 to 1, as said below
- routes: int32 [51200, 2], P(('seq', 'wt')), may hold values from 0 to 7, as said below
- priority: int32 [32, 1600], P(('seq', 'wt')), may hold values from 0 to 1599, each once within a row
- capacity: int32 [8], replicated, may hold values from 200 to 400, as said below
- attention_gain: bfloat16 [512], P('wt'), may hold values from 0.5 to 1.5
- attention_shift: bfloat16 [512], P('wt'), may hold values from -2.5 to 2.5
- query_key_value: bfloat16 [512, 1536], P('wt'), may hold values from -0.25 to 0.25
- attention_out: bfloat16 [512, 512], P('wt'), may hold values from -1.5 to 1.5
- mixture_gain: bfloat16 [512], P('wt'), may hold values from 0.5 to 1.5
- mixture_shift: bfloat16 [512], P('wt'), may hold values from -2.5 to 2.5
- router_weight: bfloat16 [512, 8], P('wt'), may hold values from -0.5 to 0.5
- expert_in: bfloat16 [8, 2048, 512], P('seq', 'wt'), may hold values from -0.25 to 0.25
- expert_in_bias: bfloat16 [8, 2048], P('seq', 'wt'), may hold values from -3 to 3
- expert_out: bfloat16 [8, 2048, 512], P('seq', 'wt'), may hold values from -0.1875 to 0.1875
- expert_out_bias: bfloat16 [8, 512], P('seq', 'wt'), may hold values from -3 to 3
- cotangent: bfloat16 [51200, 512], P(('seq', 'wt')), may hold values from -6 to 6
Outputs:
- block_output: bfloat16 [51200, 512], P(('seq', 'wt'))
- input_grad: float32 [51200, 512], P(('seq', 'wt'))
- attention_gain_grad: float32 [512], P('wt')
- attention_shift_grad: float32 [512], P('wt')
- query_key_value_grad: float32 [512, 1536], P('wt')
- attention_out_grad: float32 [512, 512], P('wt')
- mixture_gain_grad: float32 [512], P('wt')
- mixture_shift_grad: float32 [512], P('wt')
- router_weight_grad: float32 [512, 8], P('wt')
- expert_in_grad: float32 [8, 2048, 512], P('seq', 'wt')
- expert_in_bias_grad: float32 [8, 2048], P('seq', 'wt')
- expert_out_grad: float32 [8, 2048, 512], P('seq', 'wt')
- expert_out_bias_grad: float32 [8, 512], P('seq', 'wt')
Inputs may be any that keep to these rules, and one draw needn't show every extreme that they name: `routes`: the two experts of a token differ. In every aligned block of 1600 rows (the tokens of one device) some expert is the first route of 400 or more tokens. `capacity`: some expert has 400 slots. `priority`: each row names each of the 1600 local rows of its block once. `key_mask`: position 0 of every image is 1; positions 197 and beyond are 0.
All inputs are finite; a program needn't handle non-finite values.
Results may differ from a plain program's by a relative error of at most 0.019.
Values may be sent and summed in bfloat16 or wider, within the bound.
No kernel may reach another device: no remote copies, remote signals or barrier semaphores. Data moves between devices by JAX's collectives and lax.ppermute only.
A program may use at most 128 MiB of HBM per device.

v0:
```python
from functools import partial

import jax
import jax.numpy as jnp
from jax import lax
from jax.sharding import PartitionSpec as P

HEADS = 8


NEGATIVE = -1e30
EPSILON = 1e-06


def layer_norm(values, norm_gain, norm_shift):
    row_mean = jnp.mean(values, axis=-1, keepdims=True)
    offsets = values - row_mean
    spread = jnp.mean(offsets * offsets, axis=-1, keepdims=True)
    return offsets * lax.rsqrt(spread + EPSILON) * norm_gain + norm_shift


def slot_tables(route_rows, order_rows, capacity, expert_count, slot_count):
    pair_tokens = route_rows.shape[0]
    ordered = jnp.take(route_rows, order_rows, axis=0)
    labels = jnp.arange(expert_count, dtype=jnp.int32)[None, :]
    first_hot = (ordered[:, 0:1] == labels).astype(jnp.int32)
    second_hot = (ordered[:, 1:2] == labels).astype(jnp.int32)
    first_seen = jnp.cumsum(first_hot, axis=0, dtype=jnp.int32) - first_hot
    second_seen = (
        jnp.cumsum(second_hot, axis=0, dtype=jnp.int32)
        - second_hot
        + jnp.sum(first_hot, axis=0, keepdims=True, dtype=jnp.int32)
    )
    places = jnp.stack(
        [
            jnp.sum(first_seen * first_hot, axis=1, dtype=jnp.int32),
            jnp.sum(second_seen * second_hot, axis=1, dtype=jnp.int32),
        ],
        axis=1,
    )
    limits = jnp.stack(
        [
            jnp.sum(first_hot * capacity[None, :], axis=1, dtype=jnp.int32),
            jnp.sum(second_hot * capacity[None, :], axis=1, dtype=jnp.int32),
        ],
        axis=1,
    )
    sorted_kept = (places < limits).astype(jnp.int32)
    sorted_slot = places * expert_count + ordered
    kept_flags = jnp.zeros((pair_tokens, 2), jnp.int32).at[order_rows].set(sorted_kept)
    slot_index = (
        jnp.zeros((pair_tokens, 2), jnp.int32).at[order_rows].set(sorted_slot * sorted_kept)
    )
    pair_ids = jnp.arange(2, dtype=jnp.int32)[None, :] * pair_tokens + order_rows[:, None]
    target = jnp.where(sorted_kept > 0, sorted_slot, slot_count * expert_count)
    slot_table = (
        jnp.full((slot_count * expert_count,), 2 * pair_tokens, jnp.int32)
        .at[target.reshape(-1)]
        .set(pair_ids.reshape(-1), mode="drop")
    )
    return (kept_flags, slot_index, slot_table)


def row_block(row_total):
    block_size = row_total
    while block_size > 1024 and block_size % 2 == 0:
        block_size = block_size // 2
    return block_size


def unpack_weights(gathered):
    return (
        gathered[0].astype(jnp.float32),
        gathered[1].astype(jnp.float32),
        gathered[2].astype(jnp.float32),
        gathered[3].astype(jnp.float32),
        gathered[4],
        gathered[5],
        gathered[6],
        gathered[7][0],
        gathered[8][0].astype(jnp.float32),
        gathered[9][0],
        gathered[10][0].astype(jnp.float32),
    )


def expert_apply(block_rows, weight_in, bias_in, weight_out, bias_out):
    before = (
        jnp.einsum("rd,fd->rf", block_rows, weight_in, preferred_element_type=jnp.float32) + bias_in
    )
    hidden = jax.nn.gelu(before, approximate=True).astype(jnp.bfloat16)
    return (jnp.dot(hidden, weight_out, preferred_element_type=jnp.float32) + bias_out).astype(
        jnp.bfloat16
    )


def local(
    inputs,
    key_mask,
    routes,
    priority,
    capacity,
    attention_gain,
    attention_shift,
    query_key_value,
    attention_out,
    mixture_gain,
    mixture_shift,
    router_weight,
    expert_in,
    expert_in_bias,
    expert_out,
    expert_out_bias,
    cotangent,
):
    token_count, model_width = inputs.shape
    image_count, seq_length = key_mask.shape
    head_count = HEADS
    head_width = model_width // head_count
    expert_count = capacity.shape[0]
    slot_count = 8 * max(1, token_count // (4 * expert_count))
    peer_count = lax.axis_size("seq")
    scale_factor = head_width ** (-0.5)
    gathered = (
        lax.all_gather(attention_gain, "wt", axis=0, tiled=True),
        lax.all_gather(attention_shift, "wt", axis=0, tiled=True),
        lax.all_gather(mixture_gain, "wt", axis=0, tiled=True),
        lax.all_gather(mixture_shift, "wt", axis=0, tiled=True),
        lax.all_gather(query_key_value, "wt", axis=0, tiled=True),
        lax.all_gather(attention_out, "wt", axis=0, tiled=True),
        lax.all_gather(router_weight, "wt", axis=0, tiled=True),
        lax.all_gather(expert_in, "wt", axis=1, tiled=True),
        lax.all_gather(expert_in_bias, "wt", axis=1, tiled=True),
        lax.all_gather(expert_out, "wt", axis=1, tiled=True),
        lax.all_gather(expert_out_bias, "wt", axis=1, tiled=True),
    )
    forward_weights = unpack_weights(gathered)
    (
        first_gain,
        first_shift,
        second_gain,
        second_shift,
        triple_weight,
        output_weight,
        router_full,
        weight_in,
        bias_in,
        weight_out,
        bias_out,
    ) = forward_weights
    inputs_wide = inputs.astype(jnp.float32)
    normed_first = layer_norm(inputs_wide, first_gain, first_shift)
    normed_first_low = normed_first.astype(jnp.bfloat16)
    triple = jnp.dot(normed_first_low, triple_weight, preferred_element_type=jnp.float32).astype(
        jnp.bfloat16
    )
    shaped = triple.reshape(image_count, seq_length, 3, head_count, head_width)
    queries = shaped[:, :, 0]
    keys_part = shaped[:, :, 1]
    values_part = shaped[:, :, 2]
    visible = key_mask[:, None, None, :] > 0
    scores = jnp.where(
        visible,
        jnp.einsum("iqhd,ikhd->ihqk", queries, keys_part, preferred_element_type=jnp.float32)
        * scale_factor,
        NEGATIVE,
    )
    row_peak = jnp.max(scores, axis=-1, keepdims=True)
    raised = jnp.exp(scores - row_peak)
    totals = jnp.sum(raised, axis=-1, keepdims=True)
    log_total = row_peak + jnp.log(totals)
    softmax_low = (raised / totals).astype(jnp.bfloat16)
    context = (
        jnp.einsum("ihqk,ikhd->iqhd", softmax_low, values_part, preferred_element_type=jnp.float32)
        .reshape(token_count, model_width)
        .astype(jnp.bfloat16)
    )
    residual = inputs_wide + jnp.dot(context, output_weight, preferred_element_type=jnp.float32)
    normed_second = layer_norm(residual, second_gain, second_shift)
    normed_second_low = normed_second.astype(jnp.bfloat16)
    logits = jnp.dot(normed_second_low, router_full, preferred_element_type=jnp.float32)
    labels = jnp.arange(expert_count, dtype=jnp.int32)[None, :]
    first_hot = (routes[:, 0:1] == labels).astype(jnp.float32)
    second_hot = (routes[:, 1:2] == labels).astype(jnp.float32)
    route_logits = jnp.stack(
        [jnp.sum(logits * first_hot, axis=1), jnp.sum(logits * second_hot, axis=1)], axis=1
    )
    gate_values = jax.nn.softmax(route_logits, axis=1)
    kept_flags, slot_index, slot_table = slot_tables(
        routes, priority[0], capacity, expert_count, slot_count
    )
    kept_float = kept_flags.astype(jnp.float32)
    padded_rows = jnp.concatenate(
        [normed_second_low, jnp.zeros((1, model_width), jnp.bfloat16)], axis=0
    )
    row_of_slot = jnp.where(slot_table < 2 * token_count, slot_table % token_count, token_count)
    send_buffer = jnp.take(padded_rows, row_of_slot, axis=0).reshape(
        slot_count, expert_count, model_width
    )

    def apply_block(block_rows):
        return expert_apply(block_rows, weight_in, bias_in, weight_out, bias_out)

    arrived = lax.all_to_all(send_buffer, "seq", split_axis=1, concat_axis=1, tiled=True)
    item_count = arrived.shape[0]
    flat_rows = arrived.reshape(item_count * peer_count, model_width)
    block_size = row_block(flat_rows.shape[0])
    produced = lax.map(apply_block, flat_rows.reshape(-1, block_size, model_width)).reshape(
        item_count, peer_count, model_width
    )
    returned = lax.all_to_all(produced, "seq", split_axis=1, concat_axis=1, tiled=True)
    back_flat = returned.reshape(slot_count * expert_count, model_width)
    picked_first = jnp.take(back_flat, slot_index[:, 0], axis=0).astype(jnp.float32)
    picked_second = jnp.take(back_flat, slot_index[:, 1], axis=0).astype(jnp.float32)
    weight_first = kept_float[:, 0] * gate_values[:, 0]
    weight_second = kept_float[:, 1] * gate_values[:, 1]
    mixture = weight_first[:, None] * picked_first + weight_second[:, None] * picked_second
    block_output = (residual + mixture).astype(jnp.bfloat16)
    regathered = (
        lax.all_gather(attention_gain, "wt", axis=0, tiled=True),
        lax.all_gather(attention_shift, "wt", axis=0, tiled=True),
        lax.all_gather(mixture_gain, "wt", axis=0, tiled=True),
        lax.all_gather(mixture_shift, "wt", axis=0, tiled=True),
        lax.all_gather(query_key_value, "wt", axis=0, tiled=True),
        lax.all_gather(attention_out, "wt", axis=0, tiled=True),
        lax.all_gather(router_weight, "wt", axis=0, tiled=True),
        lax.all_gather(expert_in, "wt", axis=1, tiled=True),
        lax.all_gather(expert_in_bias, "wt", axis=1, tiled=True),
        lax.all_gather(expert_out, "wt", axis=1, tiled=True),
        lax.all_gather(expert_out_bias, "wt", axis=1, tiled=True),
    )
    back_weights = unpack_weights(regathered)
    (
        first_gain_b,
        first_shift_b,
        second_gain_b,
        second_shift_b,
        triple_weight_b,
        output_weight_b,
        router_full_b,
        weight_in_b,
        bias_in_b,
        weight_out_b,
        bias_out_b,
    ) = back_weights
    upstream = cotangent.astype(jnp.float32)
    gate_grad = jnp.stack(
        [
            kept_float[:, 0] * jnp.sum(picked_first * upstream, axis=1),
            kept_float[:, 1] * jnp.sum(picked_second * upstream, axis=1),
        ],
        axis=1,
    )
    route_grad = gate_values * (gate_grad - jnp.sum(gate_values * gate_grad, axis=1, keepdims=True))
    logit_grad = (route_grad[:, 0:1] * first_hot + route_grad[:, 1:2] * second_hot).astype(
        jnp.bfloat16
    )
    router_grad = jnp.einsum(
        "td,te->de", normed_second_low, logit_grad, preferred_element_type=jnp.float32
    )
    gate_of_slot = jnp.take(
        jnp.concatenate([gate_values[:, 0], gate_values[:, 1], jnp.zeros((1,), jnp.float32)]),
        slot_table,
    )
    padded_upstream = jnp.concatenate([upstream, jnp.zeros((1, model_width), jnp.float32)], axis=0)
    produced_grad = (
        (gate_of_slot[:, None] * jnp.take(padded_upstream, row_of_slot, axis=0))
        .astype(jnp.bfloat16)
        .reshape(slot_count, expert_count, model_width)
    )
    arrived_grad = lax.all_to_all(produced_grad, "seq", split_axis=1, concat_axis=1, tiled=True)
    slot_rows = arrived.reshape(-1, model_width)
    grad_rows = arrived_grad.reshape(-1, model_width)
    block_size = row_block(slot_rows.shape[0])
    hidden_width = weight_in_b.shape[0]
    gelu_tanh = partial(jax.nn.gelu, approximate=True)

    def expert_back(carried, pieces):
        in_grad, in_bias_grad, out_grad, out_bias_grad = carried
        block_rows, block_grad = pieces
        before = (
            jnp.einsum("rd,fd->rf", block_rows, weight_in_b, preferred_element_type=jnp.float32)
            + bias_in_b
        )
        activated, gelu_back = jax.vjp(gelu_tanh, before)
        hidden = activated.astype(jnp.bfloat16)
        out_grad = out_grad + jnp.einsum(
            "rf,rd->fd", hidden, block_grad, preferred_element_type=jnp.float32
        )
        out_bias_grad = out_bias_grad + jnp.sum(block_grad.astype(jnp.float32), axis=0)
        hidden_grad = jnp.einsum(
            "rd,fd->rf", block_grad, weight_out_b, preferred_element_type=jnp.float32
        )
        before_grad = gelu_back(hidden_grad)[0].astype(jnp.bfloat16)
        in_grad = in_grad + jnp.einsum(
            "rf,rd->fd", before_grad, block_rows, preferred_element_type=jnp.float32
        )
        in_bias_grad = in_bias_grad + jnp.sum(before_grad.astype(jnp.float32), axis=0)
        rows_back = jnp.dot(before_grad, weight_in_b, preferred_element_type=jnp.float32).astype(
            jnp.bfloat16
        )
        return ((in_grad, in_bias_grad, out_grad, out_bias_grad), rows_back)

    initial = (
        jnp.zeros((hidden_width, model_width), jnp.float32),
        jnp.zeros((hidden_width,), jnp.float32),
        jnp.zeros((hidden_width, model_width), jnp.float32),
        jnp.zeros((model_width,), jnp.float32),
    )
    expert_sums, rows_back = lax.scan(
        expert_back,
        initial,
        (
            slot_rows.reshape(-1, block_size, model_width),
            grad_rows.reshape(-1, block_size, model_width),
        ),
    )
    in_grad, in_bias_grad, out_grad, out_bias_grad = expert_sums
    returned_grad = lax.all_to_all(
        rows_back.reshape(slot_count, peer_count, model_width),
        "seq",
        split_axis=1,
        concat_axis=1,
        tiled=True,
    )
    back_all = returned_grad.reshape(slot_count * expert_count, model_width)
    normed_second_grad = jnp.einsum(
        "te,de->td", logit_grad, router_full_b, preferred_element_type=jnp.float32
    )
    normed_second_grad = normed_second_grad + kept_float[:, 0:1] * jnp.take(
        back_all, slot_index[:, 0], axis=0
    ).astype(jnp.float32)
    normed_second_grad = normed_second_grad + kept_float[:, 1:2] * jnp.take(
        back_all, slot_index[:, 1], axis=0
    ).astype(jnp.float32)
    _, second_back = jax.vjp(layer_norm, residual, second_gain_b, second_shift_b)
    residual_part, second_gain_grad, second_shift_grad = second_back(normed_second_grad)
    residual_grad = upstream + residual_part
    residual_low = residual_grad.astype(jnp.bfloat16)
    output_weight_grad = jnp.einsum(
        "td,te->de", context, residual_low, preferred_element_type=jnp.float32
    )
    context_grad = (
        jnp.einsum("te,de->td", residual_low, output_weight_b, preferred_element_type=jnp.float32)
        .astype(jnp.bfloat16)
        .reshape(image_count, seq_length, head_count, head_width)
    )
    scores_again = jnp.where(
        visible,
        jnp.einsum("iqhd,ikhd->ihqk", queries, keys_part, preferred_element_type=jnp.float32)
        * scale_factor,
        NEGATIVE,
    )
    probabilities = jnp.exp(scores_again - log_total)
    probabilities_low = probabilities.astype(jnp.bfloat16)
    prob_grad = jnp.einsum(
        "iqhd,ikhd->ihqk", context_grad, values_part, preferred_element_type=jnp.float32
    )
    values_grad = jnp.einsum(
        "ihqk,iqhd->ikhd", probabilities_low, context_grad, preferred_element_type=jnp.float32
    )
    score_grad = (
        probabilities * (prob_grad - jnp.sum(probabilities * prob_grad, axis=-1, keepdims=True))
    ).astype(jnp.bfloat16)
    queries_grad = (
        jnp.einsum("ihqk,ikhd->iqhd", score_grad, keys_part, preferred_element_type=jnp.float32)
        * scale_factor
    )
    keys_grad = (
        jnp.einsum("ihqk,iqhd->ikhd", score_grad, queries, preferred_element_type=jnp.float32)
        * scale_factor
    )
    triple_grad = (
        jnp.stack([queries_grad, keys_grad, values_grad], axis=2)
        .astype(jnp.bfloat16)
        .reshape(token_count, 3 * model_width)
    )
    triple_weight_grad = jnp.einsum(
        "td,te->de", normed_first_low, triple_grad, preferred_element_type=jnp.float32
    )
    normed_first_grad = jnp.einsum(
        "te,de->td", triple_grad, triple_weight_b, preferred_element_type=jnp.float32
    )
    _, first_back = jax.vjp(layer_norm, inputs_wide, first_gain_b, first_shift_b)
    input_part, first_gain_grad, first_shift_grad = first_back(normed_first_grad)
    input_grad = residual_grad + input_part
    reduced = (
        lax.psum_scatter(
            first_gain_grad.astype(jnp.bfloat16), "wt", scatter_dimension=0, tiled=True
        ).astype(jnp.float32),
        lax.psum_scatter(
            first_shift_grad.astype(jnp.bfloat16), "wt", scatter_dimension=0, tiled=True
        ).astype(jnp.float32),
        lax.psum_scatter(
            second_gain_grad.astype(jnp.bfloat16), "wt", scatter_dimension=0, tiled=True
        ).astype(jnp.float32),
        lax.psum_scatter(
            second_shift_grad.astype(jnp.bfloat16), "wt", scatter_dimension=0, tiled=True
        ).astype(jnp.float32),
        lax.psum_scatter(
            triple_weight_grad.astype(jnp.bfloat16), "wt", scatter_dimension=0, tiled=True
        ).astype(jnp.float32),
        lax.psum_scatter(
            output_weight_grad.astype(jnp.bfloat16), "wt", scatter_dimension=0, tiled=True
        ).astype(jnp.float32),
        lax.psum_scatter(
            router_grad.astype(jnp.bfloat16), "wt", scatter_dimension=0, tiled=True
        ).astype(jnp.float32),
        lax.psum_scatter(
            in_grad[None].astype(jnp.bfloat16), "wt", scatter_dimension=1, tiled=True
        ).astype(jnp.float32),
        lax.psum_scatter(
            in_bias_grad[None].astype(jnp.bfloat16), "wt", scatter_dimension=1, tiled=True
        ).astype(jnp.float32),
        lax.psum_scatter(
            out_grad[None].astype(jnp.bfloat16), "wt", scatter_dimension=1, tiled=True
        ).astype(jnp.float32),
        lax.psum_scatter(
            out_bias_grad[None].astype(jnp.bfloat16), "wt", scatter_dimension=1, tiled=True
        ).astype(jnp.float32),
    )
    shared = (
        lax.psum(reduced[0].astype(jnp.bfloat16), "seq").astype(jnp.float32),
        lax.psum(reduced[1].astype(jnp.bfloat16), "seq").astype(jnp.float32),
        lax.psum(reduced[2].astype(jnp.bfloat16), "seq").astype(jnp.float32),
        lax.psum(reduced[3].astype(jnp.bfloat16), "seq").astype(jnp.float32),
        lax.psum(reduced[4].astype(jnp.bfloat16), "seq").astype(jnp.float32),
        lax.psum(reduced[5].astype(jnp.bfloat16), "seq").astype(jnp.float32),
        lax.psum(reduced[6].astype(jnp.bfloat16), "seq").astype(jnp.float32),
    )
    return (
        block_output,
        input_grad,
        shared[0],
        shared[1],
        shared[4],
        shared[5],
        shared[2],
        shared[3],
        shared[6],
        reduced[7],
        reduced[8],
        reduced[9],
        reduced[10],
    )


def solution(mesh):
    placed = (
        P(("seq", "wt"), None),
        P(("seq", "wt"), None),
        P(("seq", "wt"), None),
        P(("seq", "wt"), None),
        P(),
        P("wt"),
        P("wt"),
        P("wt", None),
        P("wt", None),
        P("wt"),
        P("wt"),
        P("wt", None),
        P("seq", "wt", None),
        P("seq", "wt"),
        P("seq", "wt", None),
        P("seq", "wt"),
        P(("seq", "wt"), None),
    )
    return jax.shard_map(
        local,
        mesh=mesh,
        in_specs=placed,
        out_specs=(
            P(("seq", "wt"), None),
            P(("seq", "wt"), None),
            P("wt"),
            P("wt"),
            P("wt", None),
            P("wt", None),
            P("wt"),
            P("wt"),
            P("wt", None),
            P("seq", "wt", None),
            P("seq", "wt"),
            P("seq", "wt", None),
            P("seq", "wt"),
        ),
        check_vma=False,
    )
```

profile of v0, /device:TPU:0, one launch (start us, length us, event | category | flops | bytes accessed | tf_op | source)
XLA Modules:
  0.0 898.3 jit_solution(9003227922511913830)
XLA Ops:
  9.4 6.1 all-gather
  15.5 5.4 all-gather.1
  20.9 5.2 all-gather.2
  26.1 5.2 all-gather.3
  35.9 7.9 all_gather.44
  55.5 16.0 %scatter_custom_fusion.1 = s32[3200]{0:T(1024)S(1)} fusion(s32[3200]{0:T(1024)S(1)} %fusion.101, s32[3200]{0:T(1024)S(1)} %reshape.423, s32[]{:T(128)} %constant.196.clone.1), kind=kCustom, calls=%fused_computation.209 | custom fusion | bytes 12804 | tf_op jit(solution)/shard_map/scatter | solution.py:59
  71.9 6.2 convolution_convert_fusion.1
  78.1 12.9 %reshape.472 = bf16[8,200,3,8,64]{4,3,2,1,0:T(8,128)(2,1)} reshape(bf16[1600,1536]{1,0:T(8,128)(2,1)} %convolution_convert_fusion.1) | data formatting | bytes 9830400 | tf_op jit(solution)/shard_map/reshape | solution.py:157
  91.0 7.1 fusion.115
  98.1 4.8 copy.250
  102.9 4.8 copy.251
  107.6 4.8 copy.252
  112.4 5.4 fusion.116
  123.4 5.1 convert_bitcast_fusion.3
  131.1 4.6 convert_element_type.254
  142.3 10.3 %gather_fusion.1 = bf16[3200,512]{1,0:T(8,128)(2,1)} fusion(bf16[1601,512]{1,0:T(8,128)(2,1)S(1)} %concatenate.9, s32[4096]{0:T(1024)S(1)} %pad_clamp_fusion.1), kind=kCustom, calls=%fused_computation.5 | custom fusion | bytes 6566400 | tf_op jit(solution)/shard_map/jit(_take)/gather | solution.py:197
  152.5 6.4 copy_select_fusion.1
  158.9 6.1 all-to-all-start
  165.7 5.2 all_gather.51
  170.9 5.4 all_gather.49
  176.3 62.7 %all-to-all-done = bf16[400,8,512]{2,0,1:T(8,128)(2,1)S(1)} async-done(((bf16[400,8,512]{2,0,1:T(8,128)(2,1)}), bf16[400,8,512]{2,0,1:T(8,128)(2,1)S(1)}, u32[]{:S(2)}, u32[]{:S(2)}) %all-to-all-start) | async-done | bytes 3276832 | tf_op jit(solution)/shard_map/all_to_all | solution.py:204
  242.8 25.2 %while.31 = (s32[]{:T(128)}, bf16[4,800,512]{2,1,0:T(8,128)(2,1)S(1)}, bf16[4,800,512]{2,1,0:T(8,128)(2,1)}, bf16[2048,512]{1,0:T(8,128)(2,1)}, f32[2048]{0:T(10...) while((s32[]{:T(128)}, bf16[4,800,512]{2,1,0:T(8,128)(2,1)S(1)}, ...), condition=%wide.region_21.22_spmd, body=%wide.region_20.21_spmd.sunk | while | flops 3372646400 | bytes 5844061 | solution.py:208
  243.2 6.2 fusion.160
  249.4 6.2 fusion.160
  255.6 6.2 fusion.160
  261.8 6.2 fusion.160
  270.9 4.5 all-to-all-start.1
  275.8 8.0 scatter_custom_fusion
  284.4 8.7 scatter_custom_fusion.2
  295.0 9.5 %gather_fusion.3 = f32[3200,512]{1,0:T(8,128)} fusion(f32[1601,512]{1,0:T(8,128)S(1)} %concatenate.11, s32[4096]{0:T(1024)S(1)} %pad_clamp_fusion.1), kind=kCustom, calls=%fused_computation.7 | custom fusion | bytes 13120000 | tf_op jit(solution)/shard_map/jit(_take)/gather | solution.py:267
  304.5 5.5 all_gather.47
  314.4 34.2 %all-to-all-done.1 = bf16[400,8,512]{2,0,1:T(8,128)(2,1)} async-done(((bf16[400,8,512]{2,0,1:T(8,128)(2,1)}), bf16[400,8,512]{2,0,1:T(8,128)(2,1)}, u32[]{:S(2)}, u32[]{:S(2)}) %all-to-all-start.1) | async-done | bytes 3276832 | tf_op jit(solution)/shard_map/all_to_all | solution.py:211
  352.4 6.0 gather_fusion.5
  358.4 6.0 gather_fusion.4
  370.2 16.9 %gather_fusion.2 = f32[3200]{0:T(1024)S(1)} fusion(f32[3201]{0:T(1024)S(1)} %concatenate.10, s32[4096]{0:T(1024)S(1)} %pad_clamp_fusion), kind=kCustom, calls=%fused_computation.6 | custom fusion | bytes 38400 | tf_op jit(solution)/shard_map/jit(_take)/gather | solution.py:261
  387.5 8.5 fusion.52
  400.5 72.9 %all-to-all-done.2 = bf16[400,8,512]{2,0,1:T(8,128)(2,1)} async-done(((bf16[400,8,512]{2,0,1:T(8,128)(2,1)}), bf16[400,8,512]{2,0,1:T(8,128)(2,1)}, u32[]{:S(2)}, u32[]{:S(2)}) %all-to-all-start.2) | async-done | bytes 3276832 | tf_op jit(solution)/shard_map/all_to_all | solution.py:271
  479.2 100.0 %while.32 = (s32[]{:T(128)}, f32[2048,512]{1,0:T(8,128)}, f32[2048]{0:T(1024)S(1)}, f32[2048,512]{1,0:T(8,128)}, f32[512]{0:T(512)S(1)}, /*index=5*/bf16[4,800,5...) while((s32[]{:T(128)}, f32[2048,512]{1,0:T(8,128)}, ...), condition=%wide.region_29.31_spmd.clone, body=%wide.region_26.30_spmd.clone.sunk | while | flops 8448100864 | bytes 141418832 | solution.py:310
  483.7 6.1 convert_reduce_fusion.6
  489.8 4.5 select_add_fusion.10
  508.5 6.1 convert_reduce_fusion.6
  514.7 4.5 select_add_fusion.10
  533.4 6.1 convert_reduce_fusion.6
  539.6 4.5 select_add_fusion.10
  558.3 6.1 convert_reduce_fusion.6
  564.4 4.5 select_add_fusion.10
  579.2 4.7 copy.227
  584.0 4.6 all-to-all-start.3
  600.0 61.6 %all-to-all-done.3 = bf16[400,8,512]{2,0,1:T(8,128)(2,1)} async-done(((bf16[400,8,512]{2,0,1:T(8,128)(2,1)}), bf16[400,8,512]{2,0,1:T(8,128)(2,1)}, u32[]{:S(2)}, u32[]{:S(2)}) %all-to-all-start.3) | async-done | bytes 3276832 | tf_op jit(solution)/shard_map/all_to_all | solution.py:319
  665.3 6.0 gather_fusion.7
  671.4 6.0 gather_fusion.6
  677.6 8.2 multiply_reduce_fusion.1
  699.8 11.9 %multiply_reduce_fusion = (f32[8,8,200]{2,1,0:T(8,128)S(1)}, f32[8,8,200,200]{2,3,1,0:T(8,128)}) fusion(f32[8,8,200,200]{2,3,1,0:T(8,128)} %copy-done, f32[8,8,200]{2,1,0:T(8,128)S(1)} %log_add_fusion, bf16[8,200,8,64]{1,3,2,0:T(8,128)(2,1)S(1)} %copy.230, bf16[8,200,1,8,64]{1,4,3,0,2:T(8,128)(2,1)} %copy.250), kind=kOutput, calls=%fused_computation.68 | convolution fusion | flops 335347200 | bytes 23859200 | tf_op jit(solution)/shard_map/iqhd,ikhd->ihqk/dot_general | solution.py:356
  713.7 11.8 %multiply_convert_fusion.4 = bf16[8,8,200,200]{2,3,1,0:T(8,128)(2,1)S(1)} fusion(f32[8,8,200,200]{2,3,1,0:T(8,128)} %get-tuple-element.335, f32[8,8,200,200]{2,3,1,0:T(8,128)} %copy-done, f32[8,8,200]{2,1,0:T(8,128)S(1)} %get-tuple-element.334, f32[8,8,200]{2,1,0:T(8,128)S(1)} %log_add_fusion), kind=kLoop, calls=%fused_computation.67 | loop fusion | flops 10240000 | bytes 25702400 | tf_op jit(solution)/shard_map/convert_element_type | solution.py:364
  725.4 5.2 fusion.87
  735.1 5.1 convert_bitcast_fusion.2
  744.5 7.2 copy.235
  751.7 11.8 %convert_element_type.278 = bf16[1600,1536]{0,1:T(8,128)(2,1)} reshape(bf16[8,200,3,8,64]{1,0,4,3,2:T(8,128)(2,1)} %copy.235) | data formatting | bytes 9830400 | tf_op jit(solution)/shard_map/convert_element_type | solution.py:375
  763.5 7.3 convolution_convert_fusion.3
  780.4 6.1 fusion.113
  789.7 6.2 all-reduce.10
  796.2 20.4 %all-reduce.8 = (bf16[128]{0:T(256)(128)(2,1)S(1)}, bf16[128]{0:T(256)(128)(2,1)S(1)}, bf16[128]{0:T(256)(128)(2,1)S(1)}, bf16[128]{0:T(256)(128)(2,1)S(1)}, bf16[128,8]{0,1:T(8,128)(2,1)S(1)}) all-reduce(bf16[128]{0:T(256)(128)(2,1)S(1)} %dynamic-slice.1, ...), channel_id=1, replica_groups=mesh['seq'=8,'wt'=4] {'seq'}, use_global_device_ids=true, to_apply=%region_37.39 | all-reduce | flops 1536 | bytes 6144 | tf_op jit(solution)/shard_map/psum | solution.py:423
  819.2 6.1 add_add_fusion.2
  825.3 62.7 %all-reduce.13.cloned.1.call-done = (bf16[128,1536]{1,0:T(8,128)(2,1)}, bf16[128,512]{1,0:T(8,128)(2,1)}) async-done(((bf16[128,1536]{1,0:T(8,128)(2,1)}, bf16[128,512]{1,0:T(8,128)(2,1)}), (bf16[128,1536]{1,0:T(8,128)(2,1)}, bf16[128,512]{1,0:T(8,128)(2,1)})) %all-reduce.13.cloned.1.call-update) | async-done | bytes 524304 | tf_op jit(solution)/shard_map/psum | solution.py:427
  (406 shorter events, 182.4 us)
Async XLA Ops:
  7.2 27.3 %copy-start.3 = (bf16[1600,512]{1,0:T(8,128)(2,1)S(1)}, bf16[1600,512]{1,0:T(8,128)(2,1)}, u32[]{:S(2)}) copy-start(bf16[1600,512]{1,0:T(8,128)(2,1)} %param.23) | copy-start | bytes 4915204
  7.2 28.7 %copy-start.31 = (bf16[128,512]{1,0:T(8,128)(2,1)S(1)}, bf16[128,512]{1,0:T(8,128)(2,1)}, u32[]{:S(2)}) copy-start(bf16[128,512]{1,0:T(8,128)(2,1)} %param.31) | copy-start | bytes 393220
  7.2 37.3 %copy-start.54 = (s32[1600,2]{0,1:T(2,128)S(1)}, s32[1600,2]{0,1:T(2,128)}, u32[]{:S(2)}) copy-start(s32[1600,2]{0,1:T(2,128)} %param.25) | copy-start | bytes 38404
  7.2 64.6 %all-gather.8.cloned.1.call-start = ((), (), s32[]{:S(2)}) async-start(), calls=%async_computation.11 | async-start | bytes 1966080 | tf_op jit(solution)/shard_map/all_gather | solution.py:129
  7.9 234.6 %all-gather.10.cloned.1.call-start = ((), (), s32[]{:S(2)}) async-start(), calls=%async_computation.12 | async-start | bytes 2621440 | tf_op jit(solution)/shard_map/all_gather | solution.py:132
  15.5 56.3 %copy-start.60 = (f32[4,1,128]{2,1,0:T(1,128)}, f32[4,1,128]{2,1,0:T(1,128)S(1)}, u32[]{:S(2)}) copy-start(f32[4,1,128]{2,1,0:T(1,128)S(1)} %convert_element_type.307) | copy-start | bytes 6148
  20.9 50.9 %copy-start.73 = (f32[4,1,128]{2,1,0:T(1,128)}, f32[4,1,128]{2,1,0:T(1,128)S(1)}, u32[]{:S(2)}) copy-start(f32[4,1,128]{2,1,0:T(1,128)S(1)} %convert_element_type.308) | copy-start | bytes 6148
  26.1 113.8 %copy-start.66 = (f32[4,1,128]{2,1,0:T(1,128)}, f32[4,1,128]{2,1,0:T(1,128)S(1)}, u32[]{:S(2)}) copy-start(f32[4,1,128]{2,1,0:T(1,128)S(1)} %convert_element_type.309) | copy-start | bytes 6148
  34.5 37.4 %copy-start.27 = (f32[1600]{0:T(1024)}, f32[1600]{0:T(1024)S(1)}, u32[]{:S(2)}) copy-start(f32[1600]{0:T(1024)S(1)} %broadcast_multiply_fusion.1) | copy-start | bytes 19204
  35.9 35.9 %copy-start.34 = (f32[1600]{0:T(1024)}, f32[1600]{0:T(1024)S(1)}, u32[]{:S(2)}) copy-start(f32[1600]{0:T(1024)S(1)} %fusion.104) | copy-start | bytes 19204
  44.8 9.4 %copy-start.70 = (s32[8]{0:T(128)S(1)}, s32[8]{0:T(128)}, u32[]{:S(2)}) copy-start(s32[8]{0:T(128)} %param.27) | copy-start | bytes 100
  128.5 7.2 copy-start.19
  158.9 6.8 copy-start.75
  158.9 12.0 %copy-start.71 = (bf16[1,512]{1,0:T(2,128)(2,1)S(1)}, bf16[1,512]{1,0:T(2,128)(2,1)}, u32[]{:S(2)}) copy-start(bf16[1,512]{1,0:T(2,128)(2,1)} %param.36) | copy-start | bytes 3076
  158.9 80.1 %all-to-all-start = ((bf16[400,8,512]{2,0,1:T(8,128)(2,1)}), bf16[400,8,512]{2,0,1:T(8,128)(2,1)S(1)}, u32[]{:S(2)}, u32[]{:S(2)}) async-start(bf16[400,8,512]{2,0,1:T(8,128)(2,1)} %copy_select_fusion.1), calls=%async_computation | async-start | bytes 6553600 | tf_op jit(solution)/shard_map/all_to_all | solution.py:204
  165.0 77.5 %all-gather.12.cloned.1.call-start = ((), (), s32[]{:S(2)}) async-start(), calls=%async_computation.13 | async-start | bytes 2621440 | tf_op jit(solution)/shard_map/all_gather | solution.py:134
  270.9 77.7 %all-to-all-start.1 = ((bf16[400,8,512]{2,0,1:T(8,128)(2,1)}), bf16[400,8,512]{2,0,1:T(8,128)(2,1)}, u32[]{:S(2)}, u32[]{:S(2)}) async-start(bf16[400,8,512]{2,0,1:T(8,128)(2,1)} %copy.222), calls=%async_computation.1 | async-start | bytes 6553600 | tf_op jit(solution)/shard_map/all_to_all | solution.py:211
  295.0 9.5 %copy-start.72 = (bf16[128,8]{0,1:T(8,128)(2,1)S(1)}, bf16[128,8]{0,1:T(8,128)(2,1)}, u32[]{:S(2)}) copy-start(bf16[128,8]{0,1:T(8,128)(2,1)} %param.34) | copy-start | bytes 6148
  312.2 40.2 %copy-start.38 = (s32[2048]{0:T(1024)}, s32[2048]{0:T(1024)S(1)}, u32[]{:S(2)}) copy-start(s32[2048]{0:T(1024)S(1)} %pad_clamp_fusion.2) | copy-start | bytes 24580
  312.2 46.2 %copy-start.40 = (s32[2048]{0:T(1024)}, s32[2048]{0:T(1024)S(1)}, u32[]{:S(2)}) copy-start(s32[2048]{0:T(1024)S(1)} %pad_clamp_fusion.3) | copy-start | bytes 24580
  312.3 40.1 %copy-start.42 = (s32[1600]{0:T(1024)}, s32[1600]{0:T(1024)S(1)}, u32[]{:S(2)}) copy-start(s32[1600]{0:T(1024)S(1)} %get-tuple-element.259) | copy-start | bytes 19204
  312.3 40.1 %copy-start.44 = (s32[1600]{0:T(1024)}, s32[1600]{0:T(1024)S(1)}, u32[]{:S(2)}) copy-start(s32[1600]{0:T(1024)S(1)} %get-tuple-element.260) | copy-start | bytes 19204
  312.3 52.1 %copy-start.62 = (pred[1600]{0:T(1024)(128)(4,1)}, pred[1600]{0:T(1024)(128)(4,1)S(1)}, u32[]{:S(2)}) copy-start(pred[1600]{0:T(1024)(128)(4,1)S(1)} %compare_and_fusion.1) | copy-start | bytes 4804
  312.4 52.1 %copy-start.64 = (pred[1600]{0:T(1024)(128)(4,1)}, pred[1600]{0:T(1024)(128)(4,1)S(1)}, u32[]{:S(2)}) copy-start(pred[1600]{0:T(1024)(128)(4,1)S(1)} %compare_and_fusion.2) | copy-start | bytes 4804
  368.8 18.4 %copy-start.50 = (f32[1600,1]{0,1:T(1,128)}, f32[1600,1]{0,1:T(1,128)S(1)}, u32[]{:S(2)}) copy-start(f32[1600,1]{0,1:T(1,128)S(1)} %get-tuple-element.327) | copy-start | bytes 19204
  368.8 18.4 %copy-start.52 = (f32[1600,1]{0,1:T(1,128)}, f32[1600,1]{0,1:T(1,128)S(1)}, u32[]{:S(2)}) copy-start(f32[1600,1]{0,1:T(1,128)S(1)} %get-tuple-element.328) | copy-start | bytes 19204
  396.0 77.4 %all-to-all-start.2 = ((bf16[400,8,512]{2,0,1:T(8,128)(2,1)}), bf16[400,8,512]{2,0,1:T(8,128)(2,1)}, u32[]{:S(2)}, u32[]{:S(2)}) async-start(bf16[400,8,512]{2,0,1:T(8,128)(2,1)} %fusion.52), calls=%async_computation.2 | async-start | bytes 6553600 | tf_op jit(solution)/shard_map/all_to_all | solution.py:271
  483.7 6.2 copy-start.15
  508.5 6.2 copy-start.15
  533.4 6.2 copy-start.15
  558.3 6.2 copy-start.15
  584.0 77.6 %all-to-all-start.3 = ((bf16[400,8,512]{2,0,1:T(8,128)(2,1)}), bf16[400,8,512]{2,0,1:T(8,128)(2,1)}, u32[]{:S(2)}, u32[]{:S(2)}) async-start(bf16[400,8,512]{2,0,1:T(8,128)(2,1)} %copy.227), calls=%async_computation.3 | async-start | bytes 6553600 | tf_op jit(solution)/shard_map/all_to_all | solution.py:319
  588.6 183.6 %reduce-scatter.22.cloned.1.call-start = ((), (), s32[]{:S(2)}) async-start(), calls=%async_computation.18 | async-start | bytes 163840
  590.0 183.1 %reduce-scatter.26.cloned.1.call-start = ((), (), s32[]{:S(2)}) async-start(), calls=%async_computation.20 | async-start | bytes 163840
  590.8 183.6 %reduce-scatter.24.cloned.1.call-start = ((), (), s32[]{:S(2)}) async-start(), calls=%async_computation.19 | async-start | bytes 655360
  592.0 184.0 %reduce-scatter.18.cloned.1.call-start = ((), (), s32[]{:S(2)}) async-start(), calls=%async_computation.16 | async-start | bytes 2621440 | tf_op jit(solution)/shard_map/reduce_scatter | solution.py:409
  596.0 182.2 %reduce-scatter.20.cloned.1.call-start = ((), (), s32[]{:S(2)}) async-start(), calls=%async_computation.17 | async-start | bytes 2621440 | tf_op jit(solution)/shard_map/reduce_scatter | solution.py:415
  599.9 65.4 %copy-start.39 = (s32[2048]{0:T(1024)S(1)}, s32[2048]{0:T(1024)}, u32[]{:S(2)}) copy-start(s32[2048]{0:T(1024)} %copy-done.38) | copy-start | bytes 24580
  599.9 219.3 %reduce-scatter.16.cloned.1.call-start = ((), (), s32[]{:S(2)}) async-start(), calls=%async_computation.15 | async-start | bytes 655360 | tf_op jit(solution)/shard_map/reduce_scatter | solution.py:403
  671.4 6.1 copy-start.30
  671.4 6.1 copy-start.37
  671.4 6.1 copy-start.58
  677.5 8.3 copy-start.49
  677.5 8.3 copy-start.2
  677.6 8.3 copy-start.11
  677.6 8.3 copy-start.12
  677.6 8.3 copy-start.55
  677.6 8.3 copy-start.56
  699.8 12.0 %copy-start.10 = (bf16[8,200,8,64]{1,3,2,0:T(8,128)(2,1)}, bf16[8,200,8,64]{1,3,2,0:T(8,128)(2,1)S(1)}, u32[]{:S(2)}) copy-start(bf16[8,200,8,64]{1,3,2,0:T(8,128)(2,1)S(1)} %copy.230) | copy-start | bytes 4915204
  699.8 11.9 %copy-start.14 = (bf16[1600,512]{0,1:T(8,128)(2,1)S(1)}, bf16[1600,512]{0,1:T(8,128)(2,1)}, u32[]{:S(2)}) copy-start(bf16[1600,512]{0,1:T(8,128)(2,1)} %convert_element_type.254) | copy-start | bytes 4915204
  699.8 11.9 %copy-start.22 = (bf16[1600,512]{1,0:T(8,128)(2,1)S(1)}, bf16[1600,512]{1,0:T(8,128)(2,1)}, u32[]{:S(2)}) copy-start(bf16[1600,512]{1,0:T(8,128)(2,1)} %copy-done.21) | copy-start | bytes 4915204
  713.7 21.4 %slice-start = ((s8[13107200]{0:T(1024)(128)(4,1)}), s8[4194304]{0:T(1024)(128)(4,1)S(1)}, s32[]{:S(2)}) async-start(s8[13107200]{0:T(1024)(128)(4,1)} %bitcast.192), calls=%async_computation.22 | async-start | bytes 8388608
  713.7 21.4 %slice-start.1 = ((s8[13107200]{0:T(1024)(128)(4,1)}), s8[4194304]{0:T(1024)(128)(4,1)S(1)}, s32[]{:S(2)}) async-start(s8[13107200]{0:T(1024)(128)(4,1)} %bitcast.192), calls=%async_computation.23 | async-start | bytes 8388608
  713.7 21.4 %slice-start.2 = ((s8[13107200]{0:T(1024)(128)(4,1)}), s8[4194304]{0:T(1024)(128)(4,1)S(1)}, s32[]{:S(2)}) async-start(s8[13107200]{0:T(1024)(128)(4,1)} %bitcast.192), calls=%async_computation.24 | async-start | bytes 8388608
  740.2 79.0 %reduce-scatter.14.cloned.1.call-start = ((), (), s32[]{:S(2)}) async-start(), calls=%async_computation.14 | async-start | bytes 1966080 | tf_op jit(solution)/shard_map/reduce_scatter | solution.py:400
  751.7 11.8 %copy-start.4 = (bf16[1600,512]{1,0:T(8,128)(2,1)S(1)}, bf16[1600,512]{1,0:T(8,128)(2,1)}, u32[]{:S(2)}) copy-start(bf16[1600,512]{1,0:T(8,128)(2,1)} %param.23) | copy-start | bytes 4915204
  751.7 11.8 %copy-start.28 = (f32[1600]{0:T(1024)S(1)}, f32[1600]{0:T(1024)}, u32[]{:S(2)}) copy-start(f32[1600]{0:T(1024)} %copy-done.27) | copy-start | bytes 19204
  751.7 11.8 %copy-start.35 = (f32[1600]{0:T(1024)S(1)}, f32[1600]{0:T(1024)}, u32[]{:S(2)}) copy-start(f32[1600]{0:T(1024)} %copy-done.34) | copy-start | bytes 19204
  751.7 11.8 %copy-start.61 = (f32[4,1,128]{2,1,0:T(1,128)S(1)}, f32[4,1,128]{2,1,0:T(1,128)}, u32[]{:S(2)}) copy-start(f32[4,1,128]{2,1,0:T(1,128)} %copy-done.60) | copy-start | bytes 6148
  751.7 11.8 %copy-start.74 = (f32[4,1,128]{2,1,0:T(1,128)S(1)}, f32[4,1,128]{2,1,0:T(1,128)}, u32[]{:S(2)}) copy-start(f32[4,1,128]{2,1,0:T(1,128)} %copy-done.73) | copy-start | bytes 6148
  763.5 7.4 copy-start.79
  770.9 9.6 %copy-start.78 = (bf16[512,1536]{1,0:T(8,128)(2,1)S(1)}, bf16[512,1536]{1,0:T(8,128)(2,1)}, u32[]{:S(2)}) copy-start(bf16[512,1536]{1,0:T(8,128)(2,1)} %all-gather.8.cloned.1.call-done) | copy-start | bytes 4718596
  770.9 117.1 %all-reduce.13.cloned.1.call-start = ((), (), s32[]{:S(2)}) async-start(), calls=%async_computation.21 | async-start | bytes 1048576 | tf_op jit(solution)/shard_map/psum | solution.py:427
  786.5 32.7 %copy-start.7 = (bf16[1600,512]{1,0:T(8,128)(2,1)S(1)}, bf16[1600,512]{1,0:T(8,128)(2,1)}, u32[]{:S(2)}) copy-start(bf16[1600,512]{1,0:T(8,128)(2,1)} %param.39) | copy-start | bytes 4915204
  (53 other events, 192.5 us)
Sparse Core Ops, SparseCore 0:
  9.6 22.3 all-gather.7
  33.6 22.5 all-gather.9
  167.4 24.6 all-gather.11
  592.1 21.4 reduce-scatter.21
  616.6 19.5 reduce-scatter.25
  639.2 21.6 reduce-scatter.23
  663.5 31.4 reduce-scatter.17
  697.5 31.4 reduce-scatter.19
  740.3 20.4 reduce-scatter.15
  771.0 27.1 reduce-scatter.13
  819.3 68.6 all-reduce.12
where the time goes:
time: 906 us; the launch traced here: 898 us
  waiting for transfers between devices  296 us (33%)
  local copies, waits for them, and re-layouts  225 us (25%)
  matrix products  183 us (20%)
  other arithmetic  83.5 us (9%)
  blocking collectives  72.3 us (8%)
  starting transfers between devices  20.1 us (2%)
  between operations  16.2 us (2%)
    all_to_all x1, waiting for transfers between devices, local(): lax.all_to_all(produced_grad, 'seq', split_axis=1, concat_axis=1, tiled=T...  72.9 us
    psum x1, waiting for transfers between devices, local(): lax.psum(reduced[4].astype(jnp.bfloat16), 'seq').astype(jnp.float32)  62.7 us
    all_to_all x1, waiting for transfers between devices, local(): lax.all_to_all(send_buffer, 'seq', split_axis=1, concat_axis=1, tiled=True)  62.7 us
    all_to_all x1, waiting for transfers between devices, local(): lax.all_to_all(rows_back.reshape(slot_count, peer_count, model_width), 's...  61.6 us
    all_to_all x1, waiting for transfers between devices, local(): lax.all_to_all(produced, 'seq', split_axis=1, concat_axis=1, tiled=True)  34.2 us
    unnamed x173, local copies, waits for them, and re-layouts  30.5 us
    dot_general x4, matrix products, expert_apply(): jnp.dot(hidden, weight_out, preferred_element_type=jnp.float32) + bias_out  24.7 us
    dot_general x4, matrix products, expert_back(): jnp.einsum('rd,fd->rf', block_grad, weight_out_b, preferred_element_type=...  24.6 us
  transfers between devices with their start and end apart: 15, of which 5 were waited for; matrix products, arithmetic and copies ran while one was open for 33% of the time, Pallas kernels for 0%

commit v1 on v0

v1 whole, which is shorter than its diff:
```python
from functools import partial

import jax
import jax.numpy as jnp
from jax import lax
from jax.experimental import pallas as pl
from jax.experimental.pallas import tpu as pltpu
from jax.sharding import PartitionSpec as P

HEADS = 8
NEGATIVE = -1e30
EPSILON = 1e-06
LANES = 128
CHUNK = 256
VMEM_BYTES = 60 * 1024 * 1024
F32 = jnp.float32
BF16 = jnp.bfloat16
ROOT = 0.7978845608028654
CUBIC = 0.044715

NT = (((1,), (1,)), ((), ()))
TN = (((0,), (0,)), ((), ()))


def mm(a, b):
    return jnp.dot(a, b, preferred_element_type=F32)


def mm_nt(a, b):
    return lax.dot_general(a, b, NT, preferred_element_type=F32)


def mm_tn(a, b):
    return lax.dot_general(a, b, TN, preferred_element_type=F32)


def params(steps=0):
    return pltpu.CompilerParams(
        dimension_semantics=("arbitrary",) * steps if steps else None,
        vmem_limit_bytes=VMEM_BYTES,
    )


def whole(shape):
    zeros = (0,) * len(shape)
    return pl.BlockSpec(shape, lambda *_: zeros, pipeline_mode=pl.Buffered(1))


def lane_iota(rows, width):
    return lax.broadcasted_iota(jnp.int32, (rows, width), 1)


def norm_stats(values):
    row_mean = jnp.mean(values, axis=-1, keepdims=True)
    offsets = values - row_mean
    spread = jnp.mean(offsets * offsets, axis=-1, keepdims=True)
    scale = lax.rsqrt(spread + EPSILON)
    return offsets * scale, scale


def norm_back(grad, unit, scale, gain):
    weighted = grad * gain
    first = jnp.mean(weighted, axis=-1, keepdims=True)
    second = jnp.mean(weighted * unit, axis=-1, keepdims=True)
    return scale * (weighted - first - unit * second)


def slots_kernel(cap, block, prow, pcol, routes, limits, out, posrow):
    total = routes.shape[0]
    steps = total // block
    lane_t = lane_iota(1, total)

    def row_step(i, acc):
        rows = pl.ds(pl.multiple_of(i * block, block), block)
        rank = (lax.broadcasted_iota(jnp.int32, (block, 1), 0) + i * block).astype(F32)
        hit = pcol[rows, :] == lane_t
        return acc + jnp.sum(jnp.where(hit, rank, 0.0), axis=0, keepdims=True)

    posrow[...] = lax.fori_loop(0, steps, row_step, jnp.zeros((1, total), F32))
    lane = lane_iota(1, LANES)
    half = LANES // 2
    first_all = routes[:, 0:1]
    second_all = routes[:, 1:2]
    hot_all = jnp.where((first_all == lane) | (second_all + half == lane), 1.0, 0.0).astype(BF16)
    seen_first = jnp.sum(
        jnp.where(first_all + half == lane, 1.0, 0.0), axis=0, keepdims=True
    )
    rank_row = lane_t.astype(F32)

    def step(i, carry):
        rows = pl.ds(pl.multiple_of(i * block, block), block)
        token = lax.broadcasted_iota(jnp.int32, (block, 1), 0) + i * block
        poscol = jnp.sum(jnp.where(prow[...] == token, rank_row, 0.0), axis=1, keepdims=True)
        earlier = jnp.where(posrow[...] < poscol, 1.0, 0.0).astype(BF16)
        counts = mm(earlier, hot_all)
        first = routes[rows, 0:1]
        second = routes[rows, 1:2]
        first_hot = jnp.where(first == lane, 1.0, 0.0)
        second_hot = jnp.where(second + half == lane, 1.0, 0.0)
        place_a = jnp.sum(counts * first_hot, axis=1, keepdims=True)
        place_b = jnp.sum((counts + seen_first) * second_hot, axis=1, keepdims=True)
        limit_a = jnp.sum(limits[...] * first_hot, axis=1, keepdims=True)
        limit_b = jnp.sum(limits[...] * second_hot, axis=1, keepdims=True)
        slot_a = jnp.where(place_a < limit_a, first * cap + place_a.astype(jnp.int32), -1)
        slot_b = jnp.where(place_b < limit_b, second * cap + place_b.astype(jnp.int32), -1)
        out[rows, :] = jnp.where(lane_iota(block, 2) == 0, slot_a, slot_b)
        return carry

    lax.fori_loop(0, steps, step, 0)


def make_slots(routes, priority, capacity, cap):
    total = routes.shape[0]
    experts = capacity.shape[0]
    half = LANES // 2
    padded = jnp.pad(capacity.astype(F32), (0, half - experts))
    limits = jnp.concatenate([padded, padded])[None, :]
    return pl.pallas_call(
        partial(slots_kernel, cap, 200),
        out_shape=jax.ShapeDtypeStruct((total, 2), jnp.int32),
        scratch_shapes=[pltpu.VMEM((1, total), F32)],
        compiler_params=params(),
        name="slots",
    )(priority, priority.reshape(total, 1), routes, limits)


def dispatch_kernel(cap, with_other, slot_rows, route_rows, rows, out, *other):
    base = pl.program_id(0) * cap
    place = lax.broadcasted_iota(jnp.int32, (cap, 1), 0) + base
    hit_a = slot_rows[0:1, :] == place
    hit_b = slot_rows[1:2, :] == place
    pick = jnp.where(hit_a | hit_b, 1.0, 0.0).astype(BF16)
    out[...] = mm(pick, rows[...]).astype(BF16)
    if with_other:
        named = route_rows[...] + 1.0
        found = jnp.where(hit_a, named[1:2, :], jnp.where(hit_b, named[0:1, :], 0.0))
        other[0][...] = jnp.sum(found, axis=1, keepdims=True) - 1.0


def dispatch(slot_rows, route_rows, rows, experts, cap, with_other):
    total, width = rows.shape
    out_shape = [jax.ShapeDtypeStruct((experts * cap, width), BF16)]
    out_specs = [pl.BlockSpec((cap, width), lambda e: (e, 0))]
    if with_other:
        out_shape.append(jax.ShapeDtypeStruct((experts * cap, 1), F32))
        out_specs.append(pl.BlockSpec((cap, 1), lambda e: (e, 0)))
    return pl.pallas_call(
        partial(dispatch_kernel, cap, with_other),
        grid=(experts,),
        in_specs=[whole((2, total)), whole((2, total)), whole((total, width))],
        out_specs=out_specs,
        out_shape=out_shape,
        compiler_params=params(1),
        name="dispatch",
        cost_estimate=pl.CostEstimate(
            flops=2 * experts * cap * total * width, bytes_accessed=6000000, transcendentals=0
        ),
    )(slot_rows, route_rows, rows)


def attention_kernel(x, mask, gains, wqkv, wout, triple, context, logs, residual, normed):
    width = x.shape[1]
    length = x.shape[0]
    x_wide = x[...].astype(F32)
    unit, _ = norm_stats(x_wide)
    low = (unit * gains[0:1, :] + gains[1:2, :]).astype(BF16)
    mixed = mm(low, wqkv[...]).astype(BF16)
    triple[...] = mixed
    bias = jnp.where(mask[0] > 0, 0.0, NEGATIVE)
    lane = lane_iota(1, LANES)
    head_width = width // HEADS
    scale = head_width ** (-0.5)
    per = LANES // head_width
    gathered = jnp.zeros((length, LANES), F32)
    lanes_all = lane_iota(length, LANES)
    for group in range(HEADS // per):
        begin = group * LANES
        queries = mixed[:, begin : begin + LANES]
        keys = mixed[:, width + begin : width + begin + LANES]
        values = mixed[:, 2 * width + begin : 2 * width + begin + LANES]
        merged = jnp.zeros((length, LANES), F32)
        for inner in range(per):
            inside = (lane >= inner * head_width) & (lane < (inner + 1) * head_width)
            chosen = queries * jnp.where(inside, scale, 0.0).astype(BF16)
            scores = mm_nt(chosen, keys) + bias
            peak = jnp.max(scores, axis=-1, keepdims=True)
            raised = jnp.exp(scores - peak)
            sums = jnp.sum(raised, axis=-1, keepdims=True)
            found = mm(raised.astype(BF16), values) * (1.0 / sums)
            merged = jnp.where(inside, found, merged)
            gathered = jnp.where(
                lanes_all == group * per + inner, peak + jnp.log(sums), gathered
            )
        context[:, begin : begin + LANES] = merged.astype(BF16)
    logs[0] = jnp.transpose(gathered)[:HEADS, :]
    after = x_wide + mm(context[...], wout[...])
    residual[...] = after
    unit_b, _ = norm_stats(after)
    normed[...] = (unit_b * gains[2:3, :] + gains[3:4, :]).astype(BF16)


def attention_forward(x, mask, gains, dense):
    total, width = x.shape
    images, length = mask.shape
    rows = lambda i: (i, 0)
    return pl.pallas_call(
        attention_kernel,
        grid=(images,),
        in_specs=[
            pl.BlockSpec((length, width), rows),
            pl.BlockSpec((1, 1, length), lambda i: (i, 0, 0)),
            whole(gains.shape),
            pl.BlockSpec((width, 3 * width), lambda i: (0, 0), pipeline_mode=pl.Buffered(1)),
            pl.BlockSpec((width, width), lambda i: (0, 3), pipeline_mode=pl.Buffered(1)),
        ],
        out_specs=[
            pl.BlockSpec((length, 3 * width), rows),
            pl.BlockSpec((length, width), rows),
            pl.BlockSpec((1, HEADS, length), lambda i: (i, 0, 0)),
            pl.BlockSpec((length, width), rows),
            pl.BlockSpec((length, width), rows),
        ],
        out_shape=[
            jax.ShapeDtypeStruct((total, 3 * width), BF16),
            jax.ShapeDtypeStruct((total, width), BF16),
            jax.ShapeDtypeStruct((images, HEADS, length), F32),
            jax.ShapeDtypeStruct((total, width), F32),
            jax.ShapeDtypeStruct((total, width), BF16),
        ],
        compiler_params=params(1),
        name="attention_forward",
    )(x, mask.reshape(images, 1, length), gains, dense, dense)


def experts_kernel(
    block, rows, ups, other, own, router, w_in, w_out, b_in, b_out,
    sent, back, dw_in, dw_out, db_in, db_out, drouter,
    gate, weighted, rows_t, weighted_t, made, pushed, hid, pre_g,
):
    f = pl.program_id(0)
    last = pl.num_programs(0) - 1
    total, width = rows.shape
    steps = total // block
    lane = lane_iota(1, LANES)
    tile = 512

    def spans():
        return [(s, min(tile, total - s)) for s in range(0, total, tile)]

    @pl.when(f == 0)
    def _():
        own_hot = own[...] > 0.0

        def step(i, acc):
            at = pl.ds(pl.multiple_of(i * block, block), block)
            logits = mm(rows[at, :], router[...])
            mine = jnp.sum(jnp.where(own_hot, logits, 0.0), axis=1, keepdims=True)
            rival = other[at, :].astype(jnp.int32)
            theirs = jnp.sum(jnp.where(lane == rival, logits, 0.0), axis=1, keepdims=True)
            share = 1.0 / (1.0 + jnp.exp(theirs - mine))
            gate[at, 0:1] = share
            gate[at, 1:2] = 1.0 / (1.0 + jnp.exp(mine - theirs))
            scaled = (share * ups[at, :].astype(F32)).astype(BF16)
            weighted[at, :] = scaled
            return acc + jnp.sum(scaled.astype(F32), axis=0, keepdims=True)

        db_out[...] = lax.fori_loop(0, steps, step, jnp.zeros((1, width), F32))
        for s, n in spans():
            rows_t[:, s : s + n] = jnp.transpose(rows[s : s + n, :])
            weighted_t[:, s : s + n] = jnp.transpose(weighted[s : s + n, :])

    bias = b_in[0]

    def body(i, acc):
        at = pl.ds(pl.multiple_of(i * block, block), block)
        here = rows[at, :]
        u = mm_nt(here, w_in[0]) + bias
        square = u * u
        t = jnp.tanh(ROOT * (u * (1.0 + CUBIC * square)))
        up_half = 0.5 + 0.5 * t
        hidden = (u * up_half).astype(BF16)
        slope = up_half + (0.5 * ROOT) * (u * (1.0 - t * t)) * (1.0 + (3.0 * CUBIC) * square)
        hid[at, :] = hidden
        grad = mm_nt(weighted[at, :], w_out[0]) * slope
        low = grad.astype(BF16)
        pre_g[at, :] = low
        part = mm(hidden, w_out[0])
        part_b = mm(low, w_in[0])

        @pl.when(f == 0)
        def _():
            made[at, :] = part
            pushed[at, :] = part_b

        @pl.when(f > 0)
        def _():
            made[at, :] += part
            pushed[at, :] += part_b

        return acc + jnp.sum(grad, axis=0, keepdims=True)

    db_in[0] = lax.fori_loop(0, steps, body, jnp.zeros((1, w_in.shape[1]), F32))
    dw_out[0] = jnp.transpose(mm(weighted_t[...], hid[...])).astype(BF16)
    dw_in[0] = jnp.transpose(mm(rows_t[...], pre_g[...])).astype(BF16)

    @pl.when(f == last)
    def _():
        own_row = own[...]

        def step(i, carry):
            at = pl.ds(pl.multiple_of(i * block, block), block)
            produced = (made[at, :] + b_out[...]).astype(BF16).astype(F32)
            share = gate[at, 0:1]
            sent[at, :] = (share * produced).astype(BF16)
            inner = jnp.sum(produced * ups[at, :].astype(F32), axis=1, keepdims=True)
            pull = share * gate[at, 1:2] * inner
            rival = other[at, :].astype(jnp.int32)
            spread = (pull * (own_row - jnp.where(lane == rival, 1.0, 0.0))).astype(BF16)
            back[at, :] = (pushed[at, :] + mm_nt(spread, router[...])).astype(BF16)
            hid[at, 0:LANES] = spread
            return carry

        lax.fori_loop(0, steps, step, 0)
        drouter[...] = mm(rows_t[...], hid[:, 0:LANES])


def run_experts(rows, ups, other, own, dense, weights, b_in, b_out, block):
    total, width = rows.shape
    quarters, double, _ = weights.shape
    per = double // 2 // CHUNK
    hidden = quarters * per * CHUNK
    views = weights.reshape(quarters * 2 * per, CHUNK, width)
    in_at = lambda f: ((f // per) * 2 * per + f % per, 0, 0)
    out_at = lambda f: ((f // per) * 2 * per + per + f % per, 0, 0)
    small = dense.shape[1] // LANES - 1
    steps = hidden // CHUNK
    dw_shape = jax.ShapeDtypeStruct((steps, CHUNK, width), BF16)
    outs = pl.pallas_call(
        partial(experts_kernel, block),
        grid=(steps,),
        in_specs=[
            whole((total, width)),
            whole((total, width)),
            whole((total, 1)),
            whole((1, LANES)),
            pl.BlockSpec((width, LANES), lambda f: (0, small), pipeline_mode=pl.Buffered(1)),
            pl.BlockSpec((1, CHUNK, width), in_at),
            pl.BlockSpec((1, CHUNK, width), out_at),
            pl.BlockSpec((1, 1, CHUNK), lambda f: (f, 0, 0)),
            whole((1, width)),
        ],
        out_specs=[
            whole((total, width)),
            whole((total, width)),
            pl.BlockSpec((1, CHUNK, width), lambda f: (f, 0, 0)),
            pl.BlockSpec((1, CHUNK, width), lambda f: (f, 0, 0)),
            pl.BlockSpec((1, 1, CHUNK), lambda f: (f, 0, 0)),
            whole((1, width)),
            whole((width, LANES)),
        ],
        out_shape=[
            jax.ShapeDtypeStruct((total, width), BF16),
            jax.ShapeDtypeStruct((total, width), BF16),
            dw_shape,
            dw_shape,
            jax.ShapeDtypeStruct((steps, 1, CHUNK), F32),
            jax.ShapeDtypeStruct((1, width), F32),
            jax.ShapeDtypeStruct((width, LANES), F32),
        ],
        scratch_shapes=[
            pltpu.VMEM((total, 2), F32),
            pltpu.VMEM((total, width), BF16),
            pltpu.VMEM((width, total), BF16),
            pltpu.VMEM((width, total), BF16),
            pltpu.VMEM((total, width), F32),
            pltpu.VMEM((total, width), F32),
            pltpu.VMEM((total, CHUNK), BF16),
            pltpu.VMEM((total, CHUNK), BF16),
        ],
        compiler_params=params(1),
        name="experts",
        cost_estimate=pl.CostEstimate(
            flops=12 * total * width * hidden, bytes_accessed=20000000, transcendentals=0
        ),
    )(rows, ups, other, own, dense, views, views, b_in.reshape(steps, 1, CHUNK), b_out)
    return outs


def backward_kernel(
    x, kbias, gains, wqkv, wout, triple, context, logs, residual, up, slot, ret,
    input_grad, dqkv, dwout, dgains,
    tg,
):
    step = pl.program_id(0)
    length, width = x.shape
    total = ret.shape[0]
    lanes_total = lane_iota(1, total)

    @pl.when(step == 0)
    def _():
        dqkv[...] = jnp.zeros_like(dqkv)
        dwout[...] = jnp.zeros_like(dwout)
        dgains[...] = jnp.zeros_like(dgains)

    pick = jnp.where(
        (lanes_total == slot[:, 0:1]) | (lanes_total == slot[:, 1:2]), 1.0, 0.0
    ).astype(BF16)
    second_grad = mm(pick, ret[...])
    unit_b, scale_b = norm_stats(residual[...])
    dgains[2:3, :] += jnp.sum(second_grad * unit_b, axis=0, keepdims=True)
    dgains[3:4, :] += jnp.sum(second_grad, axis=0, keepdims=True)
    residual_grad = up[...].astype(F32) + norm_back(second_grad, unit_b, scale_b, gains[2:3, :])
    residual_low = residual_grad.astype(BF16)
    dwout[...] += mm_tn(context[...], residual_low)
    context_grad = mm_nt(residual_low, wout[...]).astype(BF16)

    lane = lane_iota(1, LANES)
    head_width = width // HEADS
    scale = head_width ** (-0.5)
    per = LANES // head_width
    hide = kbias[...]
    for group in range(HEADS // per):
        begin = group * LANES
        queries = triple[:, begin : begin + LANES]
        keys = triple[:, width + begin : width + begin + LANES]
        values = triple[:, 2 * width + begin : 2 * width + begin + LANES]
        pulled = context_grad[:, begin : begin + LANES]
        dq = jnp.zeros((length, LANES), F32)
        dk = jnp.zeros((length, LANES), F32)
        dv = jnp.zeros((length, LANES), F32)
        for inner in range(per):
            head = group * per + inner
            inside = (lane >= inner * head_width) & (lane < (inner + 1) * head_width)
            chosen = queries * jnp.where(inside, scale, 0.0).astype(BF16)
            log_row = logs[0, head : head + 1, :]
            probs = jnp.exp(mm_nt(keys, chosen) + hide - log_row)
            picked = pulled * jnp.where(inside, 1.0, 0.0).astype(BF16)
            prob_grad = mm_nt(values, picked)
            inner_sum = jnp.sum(probs * prob_grad, axis=0, keepdims=True)
            score_grad = (probs * (prob_grad - inner_sum)).astype(BF16)
            dq = jnp.where(inside, mm_tn(score_grad, keys), dq)
            dk = jnp.where(inside, mm(score_grad, queries), dk)
            dv = jnp.where(inside, mm(probs.astype(BF16), pulled), dv)
        tg[:, begin : begin + LANES] = (dq * scale).astype(BF16)
        tg[:, width + begin : width + begin + LANES] = (dk * scale).astype(BF16)
        tg[:, 2 * width + begin : 2 * width + begin + LANES] = dv.astype(BF16)
    unit, scale_a = norm_stats(x[...].astype(F32))
    low = (unit * gains[0:1, :] + gains[1:2, :]).astype(BF16)
    dqkv[...] += mm_tn(low, tg[...])
    first_grad = mm_nt(tg[...], wqkv[...])
    dgains[0:1, :] += jnp.sum(first_grad * unit, axis=0, keepdims=True)
    dgains[1:2, :] += jnp.sum(first_grad, axis=0, keepdims=True)
    input_grad[...] = residual_grad + norm_back(first_grad, unit, scale_a, gains[0:1, :])


def attention_backward(x, mask, gains, dense, triple, context, logs, residual, up, slot, ret):
    total, width = x.shape
    images, length = mask.shape
    rows = lambda i: (i, 0)
    kbias = jnp.where(mask > 0, 0.0, NEGATIVE).reshape(total, 1)
    return pl.pallas_call(
        backward_kernel,
        grid=(images,),
        in_specs=[
            pl.BlockSpec((length, width), rows),
            pl.BlockSpec((length, 1), rows),
            whole(gains.shape),
            pl.BlockSpec((width, 3 * width), lambda i: (0, 0), pipeline_mode=pl.Buffered(1)),
            pl.BlockSpec((width, width), lambda i: (0, 3), pipeline_mode=pl.Buffered(1)),
            pl.BlockSpec((length, 3 * width), rows),
            pl.BlockSpec((length, width), rows),
            pl.BlockSpec((1, HEADS, length), lambda i: (i, 0, 0)),
            pl.BlockSpec((length, width), rows),
            pl.BlockSpec((length, width), rows),
            pl.BlockSpec((length, 2), rows),
            whole(ret.shape),
        ],
        out_specs=[
            pl.BlockSpec((length, width), rows),
            whole((width, 3 * width)),
            whole((width, width)),
            whole((8, width)),
        ],
        out_shape=[
            jax.ShapeDtypeStruct((total, width), F32),
            jax.ShapeDtypeStruct((width, 3 * width), F32),
            jax.ShapeDtypeStruct((width, width), F32),
            jax.ShapeDtypeStruct((8, width), F32),
        ],
        scratch_shapes=[pltpu.VMEM((length, 3 * width), BF16)],
        compiler_params=params(1),
        name="attention_backward",
        cost_estimate=pl.CostEstimate(
            flops=40000000000, bytes_accessed=20000000, transcendentals=0
        ),
    )(x, kbias, gains, dense, dense, triple, context, logs, residual, up, slot, ret)


def combine_kernel(slot, residual, ret, out):
    lanes_total = lane_iota(1, ret.shape[0])
    pick = jnp.where(
        (lanes_total == slot[:, 0:1]) | (lanes_total == slot[:, 1:2]), 1.0, 0.0
    ).astype(BF16)
    out[...] = (residual[...] + mm(pick, ret[...])).astype(BF16)


def combine(slot, residual, ret, block):
    total, width = residual.shape
    rows = lambda i: (i, 0)
    return pl.pallas_call(
        combine_kernel,
        grid=(total // block,),
        in_specs=[
            pl.BlockSpec((block, 2), rows),
            pl.BlockSpec((block, width), rows),
            whole(ret.shape),
        ],
        out_specs=pl.BlockSpec((block, width), rows),
        out_shape=jax.ShapeDtypeStruct((total, width), BF16),
        compiler_params=params(1),
        name="combine",
        cost_estimate=pl.CostEstimate(
            flops=2 * total * ret.shape[0] * width, bytes_accessed=9000000, transcendentals=0
        ),
    )(slot, residual, ret)


def local(
    inputs,
    key_mask,
    routes,
    priority,
    capacity,
    attention_gain,
    attention_shift,
    query_key_value,
    attention_out,
    mixture_gain,
    mixture_shift,
    router_weight,
    expert_in,
    expert_in_bias,
    expert_out,
    expert_out_bias,
    cotangent,
):
    total, width = inputs.shape
    experts = capacity.shape[0]
    cap = 8 * max(1, total // (4 * experts))
    share = query_key_value.shape[0]

    def exchange(a):
        return lax.all_to_all(
            a.reshape(experts, cap, a.shape[-1]), "seq", split_axis=0, concat_axis=0, tiled=True
        ).reshape(a.shape)

    small = jnp.concatenate(
        [
            router_weight,
            jnp.stack([attention_gain, attention_shift, mixture_gain, mixture_shift], axis=1),
            jnp.zeros((share, LANES - experts - 4), BF16),
        ],
        axis=1,
    )
    packed = jnp.concatenate([query_key_value, attention_out, small], axis=1)
    dense = lax.all_gather(packed, "wt", axis=0, tiled=True)
    weights = lax.all_gather(
        jnp.concatenate([expert_in[0], expert_out[0]], axis=0), "wt", axis=0
    )
    biases = lax.all_gather(
        jnp.concatenate([expert_in_bias[0], expert_out_bias[0]]), "wt", axis=0
    ).astype(F32)
    b_in = biases[:, : expert_in_bias.shape[1]].reshape(-1)
    b_out = biases[:, expert_in_bias.shape[1] :].reshape(1, width)
    own_id = lax.axis_index("seq")
    own = (jnp.arange(LANES) == own_id).astype(F32)[None, :]

    slot = make_slots(routes, priority, capacity, cap)
    slot_rows = slot.T
    route_rows = routes.T.astype(F32)
    ups_out, other_out = dispatch(slot_rows, route_rows, cotangent, experts, cap, True)
    ups = exchange(ups_out)
    other = lax.all_to_all(
        other_out.reshape(experts, cap), "seq", split_axis=0, concat_axis=0, tiled=True
    ).reshape(experts * cap, 1)

    gains = dense[:, 4 * width + experts : 4 * width + experts + 4].T.astype(F32)
    gains = jnp.pad(gains, ((0, 4), (0, 0)))
    triple, context, logs, residual, normed = attention_forward(inputs, key_mask, gains, dense)
    (rows_out,) = dispatch(slot_rows, route_rows, normed, experts, cap, False)
    rows = exchange(rows_out)
    sent, back, dw_in, dw_out, db_in, db_out, drouter = run_experts(
        rows, ups, other, own, dense, weights, b_in, b_out, cap
    )
    ret_back = exchange(back)
    ret_sent = exchange(sent)
    input_grad, dqkv, dwout, dgains = attention_backward(
        inputs, key_mask, gains, dense, triple, context, logs, residual, cotangent, slot, ret_back
    )
    block_output = combine(slot, residual, ret_sent, 400)

    tail = jnp.concatenate(
        [drouter[:, :experts], dgains[:4].T, jnp.zeros((width, LANES - experts - 4), F32)], axis=1
    )
    grads = jnp.concatenate([dqkv, dwout, tail], axis=1).astype(BF16)
    part = lax.psum_scatter(grads, "wt", scatter_dimension=0, tiled=True)
    done = lax.psum(part, "seq").astype(F32)
    hidden_share = expert_in.shape[1]
    in_grad = lax.psum_scatter(
        dw_in.reshape(-1, width), "wt", scatter_dimension=0, tiled=True
    ).astype(F32)[None]
    out_grad = lax.psum_scatter(
        dw_out.reshape(-1, width), "wt", scatter_dimension=0, tiled=True
    ).astype(F32)[None]
    in_bias = lax.psum_scatter(
        db_in.reshape(-1).astype(BF16), "wt", scatter_dimension=0, tiled=True
    ).astype(F32)[None]
    out_bias = lax.psum_scatter(
        db_out.reshape(-1).astype(BF16), "wt", scatter_dimension=0, tiled=True
    ).astype(F32)[None]
    base = 4 * width
    return (
        block_output,
        input_grad,
        done[:, base + experts],
        done[:, base + experts + 1],
        done[:, : 3 * width],
        done[:, 3 * width : base],
        done[:, base + experts + 2],
        done[:, base + experts + 3],
        done[:, base : base + experts],
        in_grad,
        in_bias,
        out_grad,
        out_bias,
    )


def solution(mesh):
    both = P(("seq", "wt"), None)
    placed = (
        both,
        both,
        both,
        both,
        P(),
        P("wt"),
        P("wt"),
        P("wt", None),
        P("wt", None),
        P("wt"),
        P("wt"),
        P("wt", None),
        P("seq", "wt", None),
        P("seq", "wt"),
        P("seq", "wt", None),
        P("seq", "wt"),
        both,
    )
    return jax.shard_map(
        local,
        mesh=mesh,
        in_specs=placed,
        out_specs=(
            both,
            both,
            P("wt"),
            P("wt"),
            P("wt", None),
            P("wt", None),
            P("wt"),
            P("wt"),
            P("wt", None),
            P("seq", "wt", None),
            P("seq", "wt"),
            P("seq", "wt", None),
            P("seq", "wt"),
        ),
        check_vma=False,
    )
```

time: 906 us -> 603 us (0.67)
  Pallas kernels: 0 us -> 212 us
  local copies, waits for them, and re-layouts: 225 us -> 32.1 us
  matrix products: 183 us -> 0 us
  other arithmetic: 83.5 us -> 16.3 us
  blocking collectives: 72.3 us -> 25.9 us
  waiting for transfers between devices: 296 us -> 284 us
    pallas_call x0 -> x7, Pallas kernels: none -> 212 us  [the longest x1 104 us: run_experts(): pl.pallas_call(partial(experts_kernel, block), grid=(steps,), in_specs=[w...]
    dot_general x39 -> x0, matrix products: 183 us -> none  [the longest x4 24.7 us: expert_apply(): jnp.dot(hidden, weight_out, preferred_element_type=jnp.float32) + bias_out]
    all_to_all x4, waiting for transfers between devices: 231 us -> 159 us  [exchange(): lax.all_to_all(a.reshape(experts, cap, a.shape[-1]), 'seq', split_axis=0,...]
    gather x9 -> x0, local copies, waits for them, and re-layouts: 64.3 us -> none  [the longest x1 16.9 us: local(): jnp.take(jnp.concatenate([gate_values[:, 0], gate_values[:, 1], jnp.zeros...]
    reduce_scatter x4 -> x3, waiting for transfers between devices: 0.01 us -> 48.5 us  [the longest x1 33.8 us: local(): lax.psum_scatter(dw_in.reshape(-1, width), 'wt', scatter_dimension=0, til...]
    all_gather x8 -> x1, blocking collectives: 45.7 us -> 5.35 us  [local(): lax.all_gather(jnp.concatenate([expert_in_bias[0], expert_out_bias[0]]),...]
    convert_element_type x27 -> x6, other arithmetic: 41.1 us -> 3.73 us  [the longest x1 1.31 us: local(): route_rows = routes.T.astype(F32)]
    scatter x4 -> x0, local copies, waits for them, and re-layouts: 33 us -> none  [the longest x1 16 us: slot_tables(): slot_table = jnp.full((slot_count * expert_count,), 2 * pair_tokens, jnp....]
  transfers between devices with their start and end apart: 15 -> 10, of which waited for: 5 -> 8; matrix products, arithmetic and copies ran while one was open for 33% -> 5% of each run, Pallas kernels for 0% -> 14%
where the time goes in v1:
time: 603 us; the launch traced here: 602 us
  waiting for transfers between devices  284 us (47%)
  Pallas kernels  212 us (35%)
  local copies, waits for them, and re-layouts  32.1 us (5%)
  blocking collectives  25.9 us (4%)
  other arithmetic  16.3 us (3%)
  starting transfers between devices  16.2 us (3%)
  between operations  15.7 us (3%)
    all_to_all x4, waiting for transfers between devices, exchange(): lax.all_to_all(a.reshape(experts, cap, a.shape[-1]), 'seq', split_axis=0,...  159 us
    pallas_call x1, Pallas kernels, run_experts(): pl.pallas_call(partial(experts_kernel, block), grid=(steps,), in_specs=[w...  104 us
    psum x1, waiting for transfers between devices, local(): done = lax.psum(part, 'seq').astype(F32)  52.9 us
    pallas_call x1, Pallas kernels, attention_backward(): pl.pallas_call(backward_kernel, grid=(images,), in_specs=[pl.BlockSpec((l...  50.8 us
    reduce_scatter x1, waiting for transfers between devices, local(): lax.psum_scatter(dw_in.reshape(-1, width), 'wt', scatter_dimension=0, til...  33.8 us
    all_gather x1, waiting for transfers between devices, local(): dense = lax.all_gather(packed, 'wt', axis=0, tiled=True)  21.9 us
    pallas_call x2, Pallas kernels, dispatch(): pl.pallas_call(partial(dispatch_kernel, cap, with_other), grid=(experts,)...  19.8 us
    pallas_call x1, Pallas kernels, attention_forward(): pl.pallas_call(attention_kernel, grid=(images,), in_specs=[pl.BlockSpec((...  16.5 us
  transfers between devices with their start and end apart: 10, of which 8 were waited for; matrix products, arithmetic and copies ran while one was open for 5% of the time, Pallas kernels for 14%

profile of v1, /device:TPU:0, one launch (start us, length us, event | category | flops | bytes accessed | tf_op | source)
XLA Modules:
  0.0 601.7 jit_solution(5655385144922764934)
XLA Ops:
  7.2 1.9 copy.71.routes
  9.1 1.3 convert_bitcast_fusion.route_rows
  10.4 1.9 copy.70.pcol
  12.3 0.7 convert_element_type.49
  13.0 0.6 maximum_bitcast_fusion.limits
  13.5 11.1 %slots.1.slot = s32[1600,2]{1,0:T(8,128)} custom-call(s32[1,1600]{1,0:T(1,128)} %prow.1, s32[1600,1]{1,0:T(8,128)} %copy.70.pcol, s32[1600,2]{1,0:T(8,128)} %copy.71.routes, f32[1,128]{1,0:T(1,128)} %maximum_bitcast_fusion.limits), custom_call_target="tpu_custom_call" | custom-call | tf_op jit(solution)/shard_map/slots/pallas_call | solution.py:118
  24.6 2.0 copy.78
  26.7 10.2 %dispatch.3 = (bf16[3200,512]{1,0:T(8,128)(2,1)}, f32[3200,1]{1,0:T(8,128)}) custom-call(s32[2,1600]{1,0:T(2,128)} %bitcast.61, f32[2,1600]{1,0:T(2,128)} %convert_bitcast_fusion.route_rows, bf16[1600,512]{1,0:T(8,128)(2,1)} %up.1), custom_call_target="tpu_custom_call" | custom-call | flops 5242880000 | bytes 6000000 | tf_op jit(solution)/shard_map/dispatch/pallas_call | solution.py:147
  36.9 1.9 reduce
  38.9 13.6 %all_to_all.30 = f32[8,1,400]{2,1,0:T(1,128)S(1)} all-to-all(f32[8,1,400]{2,1,0:T(1,128)S(1)} %all_to_all.24), channel_id=1, replica_groups=mesh['seq'=8,'wt'=4] {'seq'}, dimensions={0} | all-to-all | bytes 25600 | tf_op jit(solution)/shard_map/all_to_all | solution.py:583
  52.6 3.8 all-to-all-start.1
  56.8 0.8 copy.75
  57.6 1.4 copy.76
  59.0 0.6 broadcast_in_dim.43
  59.6 1.9 concatenate.17
  61.6 2.2 pad_maximum_fusion
  63.9 0.6 reshape.94.mask
  64.5 21.9 %all-gather.6.cloned.1.call-done.wqkv.wout.router = bf16[512,2176]{1,0:T(8,128)(2,1)} async-done(((bf16[128,2176]{1,0:T(8,128)(2,1)}), bf16[512,2176]{1,0:T(8,128)(2,1)}) %all-gather.6.cloned.1.call-update) | async-done | bytes 2228240 | tf_op jit(solution)/shard_map/all_gather | solution.py:566
  86.3 1.0 slice_bitcast_fusion
  87.4 0.7 copy.77.gains
  88.1 16.5 %attention_forward.1 = (bf16[1600,1536]{1,0:T(8,128)(2,1)}, bf16[1600,512]{1,0:T(8,128)(2,1)}, f32[8,8,200]{2,1,0:T(8,128)}, f32[1600,512]{1,0:T(8,128)}, bf16[1600,512]{1,0:T(8,128)(2,1)}) custom-call(bf16[1600,512]{1,0:T(8,128)(2,1)} %x.7, s32[8,1,200]{2,1,0:T(1,128)} %reshape.94.mask, f32[8,512]{1,0:T(8,128)} %copy.77.gains, ...), custom_call_target="tpu_custom_call" | custom-call | tf_op jit(solution)/shard_map/attention_forward/pallas_call | solution.py:206
  104.6 9.6 %dispatch.2 = bf16[3200,512]{1,0:T(8,128)(2,1)} custom-call(s32[2,1600]{1,0:T(2,128)} %bitcast.62, f32[2,1600]{1,0:T(2,128)} %convert_bitcast_fusion.route_rows, bf16[1600,512]{1,0:T(8,128)(2,1)} %get-tuple-element.32.rows), custom_call_target="tpu_custom_call" | custom-call | flops 5242880000 | bytes 6000000 | tf_op jit(solution)/shard_map/dispatch/pallas_call | solution.py:147
  114.3 14.4 %all-to-all-done.1 = bf16[8,400,512]{2,1,0:T(8,128)(2,1)S(1)} async-done(((bf16[8,400,512]{2,1,0:T(8,128)(2,1)}), bf16[8,400,512]{2,1,0:T(8,128)(2,1)S(1)}, u32[]{:S(2)}, u32[]{:S(2)}) %all-to-all-start.1) | async-done | bytes 3276832 | tf_op jit(solution)/shard_map/all_to_all | solution.py:553
  128.7 1.7 copy-done.1
  130.4 4.5 all-to-all-start
  134.9 5.3 all-gather.2
  140.3 0.6 slice.52
  140.9 0.6 reshape_reshape.3.b_in
  141.5 0.5 compare_convert_fusion.own
  142.0 1.9 reshape.123.other
  143.9 63.9 %all-to-all-done = bf16[8,400,512]{2,1,0:T(8,128)(2,1)} async-done(((bf16[8,400,512]{2,1,0:T(8,128)(2,1)}), bf16[8,400,512]{2,1,0:T(8,128)(2,1)}, u32[]{:S(2)}, u32[]{:S(2)}) %all-to-all-start) | async-done | bytes 3276832 | tf_op jit(solution)/shard_map/all_to_all | solution.py:553
  207.8 103.8 %experts.1 = (bf16[3200,512]{1,0:T(8,128)(2,1)}, bf16[3200,512]{1,0:T(8,128)(2,1)}, bf16[8,256,512]{2,1,0:T(8,128)(2,1)}, bf16[8,256,512]{2,1,0:T(8,128)(2,1)}, ...) custom-call(bf16[3200,512]{1,0:T(8,128)(2,1)} %bitcast.10.rows, bf16[3200,512]{1,0:T(8,128)(2,1)} %bitcast.46, ...), custom_call_target="tpu_custom_call" | custom-call | flops 40265318400 | bytes 20000000 | tf_op jit(solution)/shard_map/experts/pallas_call | solution.py:338
  311.7 3.7 all-to-all-start.4
  315.4 0.7 reduce-scatter.8.cloned.1.call-update
  316.1 0.3 reduce-scatter.4.cloned.1.call-start
  316.4 1.2 reshape.124.kbias
  317.5 1.0 slice.71
  318.5 70.5 %all-to-all-done.4 = bf16[8,400,512]{2,1,0:T(8,128)(2,1)S(1)} async-done(((bf16[8,400,512]{2,1,0:T(8,128)(2,1)}), bf16[8,400,512]{2,1,0:T(8,128)(2,1)S(1)}, u32[]{:S(2)}, u32[]{:S(2)}) %all-to-all-start.4) | async-done | bytes 3276832 | tf_op jit(solution)/shard_map/all_to_all | solution.py:553
  389.0 1.7 copy-done.3
  390.7 50.8 %attention_backward.1 = (f32[1600,512]{1,0:T(8,128)}, f32[512,1536]{1,0:T(8,128)}, f32[512,512]{1,0:T(8,128)}, f32[8,512]{1,0:T(8,128)}) custom-call(bf16[1600,512]{1,0:T(8,128)(2,1)} %x.7, f32[1600,1]{1,0:T(8,128)} %reshape.124.kbias, f32[8,512]{1,0:T(8,128)} %copy.77.gains, bf16[512,2176]{1,0:T(8,128)(2,1)} %all-gather.6.cloned.1.call-done.wqkv.wout.router, ...), custom_call_target="tpu_custom_call" | custom-call | flops 40000000000 | bytes 20000000 | tf_op jit(solution)/shard_map/attention_backward/pallas_call | solution.py:461
  441.5 2.2 convert.24
  443.7 0.7 fusion
  444.4 0.2 copy.83
  444.7 3.0 concatenate.20
  447.7 3.8 all-to-all-start.3
  451.6 0.5 reduce-scatter.6.cloned.1.call-update
  452.2 0.6 dynamic-slice
  454.2 6.9 %all-reduce.4 = (bf16[2048]{0:T(1024)(128)(2,1)S(1)}, bf16[512]{0:T(512)(128)(2,1)S(1)}) all-reduce(bf16[2048]{0:T(1024)(128)(2,1)S(1)} %bitcast.60, bf16[512]{0:T(512)(128)(2,1)S(1)} %convert_reduce_fusion.1), channel_id=6, replica_groups=mesh['seq'=8,'wt'=4] {'wt'}, use_global_device_ids=true, to_apply=%region_3.4.clone | all-reduce | flops 2560 | bytes 10240
  461.0 0.6 bitcast_convert_fusion.2
  461.6 0.7 dynamic-slice_convert_fusion
  462.3 2.1 bitcast_convert_fusion
  464.4 14.7 %reduce-scatter.4.cloned.1.call-done = bf16[128,2176]{1,0:T(8,128)(2,1)} async-done(((bf16[512,2176]{1,0:T(8,128)(2,1)}), bf16[128,2176]{1,0:T(8,128)(2,1)}) %reduce-scatter.4.cloned.1.call-update) | async-done | bytes 557072 | tf_op jit(solution)/shard_map/reduce_scatter | solution.py:606
  479.2 33.8 %reduce-scatter.6.cloned.1.call-done = bf16[512,512]{1,0:T(8,128)(2,1)} async-done(((bf16[2048,512]{1,0:T(8,128)(2,1)}), bf16[512,512]{1,0:T(8,128)(2,1)}) %reduce-scatter.6.cloned.1.call-update) | async-done | bytes 524304 | tf_op jit(solution)/shard_map/reduce_scatter | solution.py:609
  513.0 2.1 bitcast_convert_fusion.1
  515.2 10.3 %all-to-all-done.3 = bf16[8,400,512]{2,1,0:T(8,128)(2,1)S(1)} async-done(((bf16[8,400,512]{2,1,0:T(8,128)(2,1)}), bf16[8,400,512]{2,1,0:T(8,128)(2,1)S(1)}, u32[]{:S(2)}, u32[]{:S(2)}) %all-to-all-start.3) | async-done | bytes 3276832 | tf_op jit(solution)/shard_map/all_to_all | solution.py:553
  525.4 1.7 copy-done.2
  527.1 9.7 %combine.1 = bf16[1600,512]{1,0:T(8,128)(2,1)} custom-call(s32[1600,2]{1,0:T(8,128)} %slots.1.slot, f32[1600,512]{1,0:T(8,128)} %get-tuple-element.31.residual, bf16[3200,512]{1,0:T(8,128)(2,1)} %bitcast.47), custom_call_target="tpu_custom_call" | custom-call | flops 5242880000 | bytes 9000000 | tf_op jit(solution)/shard_map/combine/pallas_call | solution.py:510
  536.8 52.9 %all-reduce.7.cloned.1.call-done = bf16[128,2176]{1,0:T(8,128)(2,1)} async-done(((bf16[128,2176]{1,0:T(8,128)(2,1)}), bf16[128,2176]{1,0:T(8,128)(2,1)}) %all-reduce.7.cloned.1.call-update) | async-done | bytes 557072 | tf_op jit(solution)/shard_map/psum | solution.py:607
  589.7 1.2 convert_element_type.55
  590.9 0.8 slice_reduce_fusion
  591.7 0.8 slice.61
  592.5 0.7 copy.84
  593.1 1.0 slice.57
  594.1 0.7 slice.58
  (58 shorter events, 1.1 us)
Async XLA Ops:
  52.5 3.9 copy-start.9
  52.5 4.0 copy-start.12
  52.6 4.1 copy-start.13
  52.6 7.1 %copy-start.5 = (bf16[128,512]{1,0:T(8,128)(2,1)S(1)}, bf16[128,512]{1,0:T(8,128)(2,1)}, u32[]{:S(2)}) copy-start(bf16[128,512]{1,0:T(8,128)(2,1)} %param.25) | copy-start | bytes 393220
  52.6 76.1 %all-to-all-start.1 = ((bf16[8,400,512]{2,1,0:T(8,128)(2,1)}), bf16[8,400,512]{2,1,0:T(8,128)(2,1)S(1)}, u32[]{:S(2)}, u32[]{:S(2)}) async-start(bf16[8,400,512]{2,1,0:T(8,128)(2,1)} %bitcast.48), calls=%async_computation.1 | async-start | bytes 6553600 | tf_op jit(solution)/shard_map/all_to_all | solution.py:553
  56.4 30.0 %all-gather.6.cloned.1.call-start = ((), (), s32[]{:S(2)}) async-start(), calls=%async_computation.8 | async-start | bytes 2785280 | tf_op jit(solution)/shard_map/all_gather | solution.py:566
  61.5 2.3 copy-start.6
  61.5 82.4 %all-gather.8.cloned.1.call-start = ((), (), s32[]{:S(2)}) async-start(), calls=%async_computation.13 | async-start | bytes 5242880 | tf_op jit(solution)/shard_map/all_gather | solution.py:567
  128.7 1.7 copy-start.1
  128.7 6.2 %copy-start.10 = (bf16[1,512]{1,0:T(2,128)(2,1)S(1)}, bf16[1,512]{1,0:T(2,128)(2,1)}, u32[]{:S(2)}) copy-start(bf16[1,512]{1,0:T(2,128)(2,1)} %param.30) | copy-start | bytes 3076
  128.7 6.2 %copy-start.14 = (bf16[1,128]{1,0:T(2,128)(2,1)S(1)}, bf16[1,128]{1,0:T(2,128)(2,1)}, u32[]{:S(2)}) copy-start(bf16[1,128]{1,0:T(2,128)(2,1)} %param.32) | copy-start | bytes 772
  130.4 77.4 %all-to-all-start = ((bf16[8,400,512]{2,1,0:T(8,128)(2,1)}), bf16[8,400,512]{2,1,0:T(8,128)(2,1)}, u32[]{:S(2)}, u32[]{:S(2)}) async-start(bf16[8,400,512]{2,1,0:T(8,128)(2,1)} %bitcast.49), calls=%async_computation | async-start | bytes 6553600 | tf_op jit(solution)/shard_map/all_to_all | solution.py:553
  311.7 4.7 copy-start.7
  311.7 77.3 %all-to-all-start.4 = ((bf16[8,400,512]{2,1,0:T(8,128)(2,1)}), bf16[8,400,512]{2,1,0:T(8,128)(2,1)S(1)}, u32[]{:S(2)}, u32[]{:S(2)}) async-start(bf16[8,400,512]{2,1,0:T(8,128)(2,1)} %bitcast.51), calls=%async_computation.4 | async-start | bytes 6553600 | tf_op jit(solution)/shard_map/all_to_all | solution.py:553
  315.3 146.9 %reduce-scatter.8.cloned.1.call-start = ((), (), s32[]{:S(2)}) async-start(), calls=%async_computation.12 | async-start | bytes 2621440 | tf_op jit(solution)/shard_map/reduce_scatter | solution.py:612
  316.1 163.1 %reduce-scatter.4.cloned.1.call-start = ((), (), s32[]{:S(2)}) async-start(), calls=%async_computation.9 | async-start | bytes 2785280 | tf_op jit(solution)/shard_map/reduce_scatter | solution.py:606
  389.0 1.7 copy-start.3
  441.5 2.2 copy-start.4
  447.7 4.5 copy-start.15
  447.7 6.4 %copy-start.8 = (f32[8,1,256]{2,1,0:T(1,128)S(1)}, f32[8,1,256]{2,1,0:T(1,128)}, u32[]{:S(2)}) copy-start(f32[8,1,256]{2,1,0:T(1,128)} %get-tuple-element.46) | copy-start | bytes 24580
  447.7 6.4 %copy-start.11 = (f32[1,512]{1,0:T(1,128)S(1)}, f32[1,512]{1,0:T(1,128)}, u32[]{:S(2)}) copy-start(f32[1,512]{1,0:T(1,128)} %get-tuple-element.48) | copy-start | bytes 6148
  447.7 77.7 %all-to-all-start.3 = ((bf16[8,400,512]{2,1,0:T(8,128)(2,1)}), bf16[8,400,512]{2,1,0:T(8,128)(2,1)S(1)}, u32[]{:S(2)}, u32[]{:S(2)}) async-start(bf16[8,400,512]{2,1,0:T(8,128)(2,1)} %bitcast.45), calls=%async_computation.3 | async-start | bytes 6553600 | tf_op jit(solution)/shard_map/all_to_all | solution.py:553
  451.6 61.5 %reduce-scatter.6.cloned.1.call-start = ((), (), s32[]{:S(2)}) async-start(), calls=%async_computation.11 | async-start | bytes 2621440 | tf_op jit(solution)/shard_map/reduce_scatter | solution.py:609
  452.1 137.6 %all-reduce.7.cloned.1.call-start = ((), (), s32[]{:S(2)}) async-start(), calls=%async_computation.10 | async-start | bytes 1114112 | tf_op jit(solution)/shard_map/psum | solution.py:607
  525.4 1.7 copy-start.2
  589.7 3.4 copy-start
Sparse Core Ops, SparseCore 0:
  61.7 24.6 all-gather.5
  88.5 34.4 all-gather.7
  318.7 32.7 reduce-scatter.7
  447.8 31.3 reduce-scatter.3
  481.6 31.4 reduce-scatter.5
  516.7 73.0 all-reduce.6

commit v2 on v1

v2 whole, which is shorter than its diff:
```python
from functools import partial

import jax
import jax.numpy as jnp
from jax import lax
from jax.experimental import pallas as pl
from jax.experimental.pallas import tpu as pltpu
from jax.sharding import PartitionSpec as P

HEADS = 8
NEGATIVE = -1e30
EPSILON = 1e-06
LANES = 128
BIG_STEPS = 2
VMEM_BYTES = 60 * 1024 * 1024
F32 = jnp.float32
BF16 = jnp.bfloat16
ROOT = 0.7978845608028654
CUBIC = 0.044715

NT = (((1,), (1,)), ((), ()))
TN = (((0,), (0,)), ((), ()))


def mm(a, b):
    return jnp.dot(a, b, preferred_element_type=F32)


def mm_nt(a, b):
    return lax.dot_general(a, b, NT, preferred_element_type=F32)


def mm_tn(a, b):
    return lax.dot_general(a, b, TN, preferred_element_type=F32)


def params(steps=0):
    return pltpu.CompilerParams(
        dimension_semantics=("arbitrary",) * steps if steps else None,
        vmem_limit_bytes=VMEM_BYTES,
    )


def cost(micros):
    return pl.CostEstimate(
        flops=int(micros * 1.0e7), bytes_accessed=int(micros * 1.0e4), transcendentals=0
    )


def gain_rows(small, experts):
    turned = jnp.transpose(small[...].astype(F32))
    return turned[experts : experts + 4, :]


def whole(shape):
    zeros = (0,) * len(shape)
    return pl.BlockSpec(shape, lambda *_: zeros, pipeline_mode=pl.Buffered(1))


def gather_slots(slot, parts):
    found = None
    start = 0
    for piece in parts:
        rows = piece[...].reshape(-1, piece.shape[-1])
        lanes = lane_iota(1, rows.shape[0]) + start
        start += rows.shape[0]
        pick = jnp.where((lanes == slot[:, 0:1]) | (lanes == slot[:, 1:2]), 1.0, 0.0)
        piece = jnp.dot(pick.astype(BF16), rows, preferred_element_type=F32)
        found = piece if found is None else found + piece
    return found


def returned_specs(ret, which):
    both, alone = ret
    experts, _, size, width = both.shape
    spot = lambda *_: (0, which, 0, 0)
    return [
        pl.BlockSpec((experts, None, size, width), spot, pipeline_mode=pl.Buffered(1)),
        whole(alone.shape),
    ]


def lane_iota(rows, width):
    return lax.broadcasted_iota(jnp.int32, (rows, width), 1)


def norm_stats(values):
    row_mean = jnp.mean(values, axis=-1, keepdims=True)
    offsets = values - row_mean
    spread = jnp.mean(offsets * offsets, axis=-1, keepdims=True)
    scale = lax.rsqrt(spread + EPSILON)
    return offsets * scale, scale


def norm_back(grad, unit, scale, gain):
    weighted = grad * gain
    first = jnp.mean(weighted, axis=-1, keepdims=True)
    second = jnp.mean(weighted * unit, axis=-1, keepdims=True)
    return scale * (weighted - first - unit * second)


EXTRA = 16


def pack_kernel(wqkv, wout, router, ga, sa, gm, sm, w_in, w_out, b_in, b_out, dense, first, second, tail):
    width = wout.shape[1]
    experts = router.shape[1]
    share = wout.shape[0]
    hidden = w_in.shape[0]
    dense[:, : 3 * width] = wqkv[...]
    dense[:, 3 * width : 4 * width] = wout[...]
    tail[...] = jnp.zeros_like(tail)
    for k, row in enumerate((ga, sa, gm, sm)):
        tail[experts + k : experts + k + 1, 0:share] = row[...].astype(F32)
    columns = jnp.transpose(tail[0:LANES, 0:LANES])[:share, :]
    dense[:, 4 * width :] = columns.astype(BF16)
    dense[:, 4 * width : 4 * width + experts] = router[...]
    first[...] = w_in[...]
    second[0:hidden, :] = w_out[...]
    tail[0:EXTRA, :] = jnp.zeros((EXTRA, width), F32)
    tail[0:1, 0:hidden] = b_in[...].astype(F32)
    tail[1:2, 0:share] = b_out[...].astype(F32)
    second[hidden:, :] = tail[0:EXTRA, :].astype(BF16)


def pack(wqkv, wout, router, gains, w_in, w_out, b_in, b_out):
    share, width = wout.shape
    hidden = w_in.shape[0]
    return pl.pallas_call(
        pack_kernel,
        out_shape=[
            jax.ShapeDtypeStruct((share, 4 * width + LANES), BF16),
            jax.ShapeDtypeStruct((hidden, width), BF16),
            jax.ShapeDtypeStruct((hidden + EXTRA, width), BF16),
        ],
        scratch_shapes=[pltpu.VMEM((LANES, width), F32)],
        compiler_params=params(),
        name="pack",
        cost_estimate=cost(3),
    )(wqkv, wout, router, *[g[None, :] for g in gains], w_in, w_out, b_in, b_out)


def slots_kernel(parts, block, prow, routes, capacity, out, out_rows, poscol, hot, limits, wide):
    total = routes.shape[1]
    experts = capacity.shape[1]
    steps = total // block
    half = LANES // 2
    sub = lax.broadcasted_iota(jnp.int32, (LANES, 1), 0)
    hot_t = jnp.where((routes[0:1, :] == sub) | (routes[1:2, :] + half == sub), 1.0, 0.0)
    hot[...] = jnp.transpose(hot_t).astype(BF16)
    limits[...] = jnp.zeros_like(limits)
    limits[:, 0:experts] = capacity[...].astype(F32)
    limits[:, half : half + experts] = capacity[...].astype(F32)
    lane = lane_iota(1, LANES)
    index = lax.broadcasted_iota(jnp.int32, (total, LANES), 0)
    digits = jnp.where(
        lane_iota(total, LANES) == 0, index // 8, jnp.where(lane_iota(total, LANES) == 1, index % 8, 0)
    ).astype(F32).astype(BF16)

    def find(i, carry):
        at = pl.ds(pl.multiple_of(i * block, block), block)
        token = lax.broadcasted_iota(jnp.int32, (block, 1), 0) + i * block
        hit = jnp.where(prow[...] == token, 1.0, 0.0).astype(BF16)
        poscol[at, :] = mm(hit, digits)
        return carry

    lax.fori_loop(0, steps, find, 0)
    turned = jnp.transpose(poscol[...])
    posrow = turned[0:1, :] * 8.0 + turned[1:2, :]
    low_lanes = lane < half
    seen = jnp.sum(hot[...].astype(F32), axis=0, keepdims=True)
    seen_b = jnp.where(low_lanes, 0.0, pltpu.roll(jnp.broadcast_to(seen, (8, LANES)), half, 1)[0:1, :])
    expert = jnp.where(low_lanes, lane, lane - half)
    front, rest = parts
    base = (expert * front + 1).astype(F32)
    base_b = (experts * front + expert * rest - front + 1).astype(F32)

    def step(i, carry):
        at = pl.ds(pl.multiple_of(i * block, block), block)
        mine = poscol[at, 0:1] * 8.0 + poscol[at, 1:2]
        earlier = jnp.where(posrow < mine, 1.0, 0.0).astype(BF16)
        own = hot[at, :].astype(F32)
        place = mm(earlier, hot[...]) + seen_b
        number = place + jnp.where(place < front, base, base_b)
        value = jnp.where(place < limits[...], number, 0.0) * own
        slot_a = jnp.sum(jnp.where(low_lanes, value, 0.0), axis=1, keepdims=True) - 1.0
        slot_b = jnp.sum(jnp.where(low_lanes, 0.0, value), axis=1, keepdims=True) - 1.0
        wide[at, :] = jnp.where(lane == 0, slot_a, slot_b)
        out[at, :] = jnp.where(lane_iota(1, 2) == 0, slot_a, slot_b).astype(jnp.int32)
        return carry

    lax.fori_loop(0, steps, step, 0)
    out_rows[...] = jnp.transpose(wide[...])[0:2, :].astype(jnp.int32)


def make_slots(route_rows, priority, capacity, parts):
    total = route_rows.shape[1]
    return pl.pallas_call(
        partial(slots_kernel, parts, 400),
        out_shape=[
            jax.ShapeDtypeStruct((total, 2), jnp.int32),
            jax.ShapeDtypeStruct((2, total), jnp.int32),
        ],
        scratch_shapes=[
            pltpu.VMEM((total, LANES), F32),
            pltpu.VMEM((total, LANES), BF16),
            pltpu.VMEM((1, LANES), F32),
            pltpu.VMEM((total, LANES), F32),
        ],
        compiler_params=params(),
        name="slots",
        cost_estimate=cost(8),
    )(priority, route_rows, capacity[None, :])


def dispatch_kernel(parts, with_other, slot_rows, route_rows, rows, *outs):
    e = pl.program_id(0)
    if not with_other:
        carry, *outs = outs
        outs[-1][0, parts[-1] :, :] = carry[0]
    start = 0
    for size, out in zip(parts, outs):
        place = lax.broadcasted_iota(jnp.int32, (size, 1), 0) + (start + e * size)
        start += pl.num_programs(0) * size
        hit_a = slot_rows[0:1, :] == place
        hit_b = slot_rows[1:2, :] == place
        pick = jnp.where(hit_a | hit_b, 1.0, 0.0).astype(BF16)
        out[0, 0:size, :] = mm(pick, rows[...]).astype(BF16)
        if with_other:
            named = route_rows[...].astype(F32) + 1.0
            found = jnp.where(hit_a, named[1:2, :], jnp.where(hit_b, named[0:1, :], 0.0))
            column = jnp.sum(found, axis=1, keepdims=True) - 1.0
            turned = jnp.transpose(jnp.broadcast_to(column, (size, LANES)))
            out[0, size : size + EXTRA, 0:size] = turned[0:EXTRA, :].astype(BF16)


def dispatch(slot_rows, route_rows, rows, experts, parts, carry=None):
    total, width = rows.shape
    with_other = carry is None
    if with_other:
        tall = [size + EXTRA for size in parts]
        extra, extra_spec = (), ()
    else:
        tall = [parts[0], parts[1] + carry.shape[1]]
        extra = (carry,)
        extra_spec = (pl.BlockSpec((1,) + carry.shape[1:], lambda e: (e, 0, 0)),)
    return pl.pallas_call(
        partial(dispatch_kernel, parts, with_other),
        grid=(experts,),
        in_specs=[whole((2, total)), whole((2, total)), whole((total, width)), *extra_spec],
        out_specs=[pl.BlockSpec((1, t, width), lambda e: (e, 0, 0)) for t in tall],
        out_shape=[jax.ShapeDtypeStruct((experts, t, width), BF16) for t in tall],
        compiler_params=params(1),
        name="dispatch",
        cost_estimate=cost(10),
    )(slot_rows, route_rows, rows, *extra)


def attention_kernel(
    experts, x, mask, small, wqkv, wout, triple, context, logs, residual, normed, gains
):
    @pl.when(pl.program_id(0) == 0)
    def _():
        gains[0:4, :] = gain_rows(small, experts)

    width = x.shape[1]
    length = x.shape[0]
    x_wide = x[...].astype(F32)
    unit, _ = norm_stats(x_wide)
    low = (unit * gains[0:1, :] + gains[1:2, :]).astype(BF16)
    mixed = mm(low, wqkv[...]).astype(BF16)
    triple[...] = mixed
    bias = jnp.where(mask[0] > 0, 0.0, NEGATIVE)
    lane = lane_iota(1, LANES)
    head_width = width // HEADS
    scale = head_width ** (-0.5)
    per = LANES // head_width
    gathered = jnp.zeros((length, LANES), F32)
    lanes_all = lane_iota(length, LANES)
    for group in range(HEADS // per):
        begin = group * LANES
        queries = mixed[:, begin : begin + LANES]
        keys = mixed[:, width + begin : width + begin + LANES]
        values = mixed[:, 2 * width + begin : 2 * width + begin + LANES]
        merged = jnp.zeros((length, LANES), F32)
        for inner in range(per):
            inside = (lane >= inner * head_width) & (lane < (inner + 1) * head_width)
            chosen = queries * jnp.where(inside, scale, 0.0).astype(BF16)
            scores = mm_nt(chosen, keys) + bias
            peak = jnp.max(scores, axis=-1, keepdims=True)
            raised = jnp.exp(scores - peak)
            sums = jnp.sum(raised, axis=-1, keepdims=True)
            found = mm(raised.astype(BF16), values) * (1.0 / sums)
            merged = jnp.where(inside, found, merged)
            gathered = jnp.where(
                lanes_all == group * per + inner, peak + jnp.log(sums), gathered
            )
        context[:, begin : begin + LANES] = merged.astype(BF16)
    logs[0] = jnp.transpose(gathered)[:HEADS, :]
    after = x_wide + mm(context[...], wout[...])
    residual[...] = after
    unit_b, _ = norm_stats(after)
    normed[...] = (unit_b * gains[2:3, :] + gains[3:4, :]).astype(BF16)


def small_spec(width):
    last = 4 * width // LANES
    return pl.BlockSpec((width, LANES), lambda i: (0, last), pipeline_mode=pl.Buffered(1))


def attention_forward(x, mask, dense, experts):
    total, width = x.shape
    images, length = mask.shape
    rows = lambda i: (i, 0)
    return pl.pallas_call(
        partial(attention_kernel, experts),
        grid=(images,),
        in_specs=[
            pl.BlockSpec((length, width), rows),
            pl.BlockSpec((1, 1, length), lambda i: (i, 0, 0)),
            small_spec(width),
            pl.BlockSpec((width, 3 * width), lambda i: (0, 0), pipeline_mode=pl.Buffered(1)),
            pl.BlockSpec((width, width), lambda i: (0, 3), pipeline_mode=pl.Buffered(1)),
        ],
        out_specs=[
            pl.BlockSpec((length, 3 * width), rows),
            pl.BlockSpec((length, width), rows),
            pl.BlockSpec((1, HEADS, length), lambda i: (i, 0, 0)),
            pl.BlockSpec((length, width), rows),
            pl.BlockSpec((length, width), rows),
        ],
        out_shape=[
            jax.ShapeDtypeStruct((total, 3 * width), BF16),
            jax.ShapeDtypeStruct((total, width), BF16),
            jax.ShapeDtypeStruct((images, HEADS, length), F32),
            jax.ShapeDtypeStruct((total, width), F32),
            jax.ShapeDtypeStruct((total, width), BF16),
        ],
        scratch_shapes=[pltpu.VMEM((8, width), F32)],
        compiler_params=params(1),
        name="attention_forward",
        cost_estimate=cost(17),
    )(x, mask.reshape(images, 1, length), dense, dense, dense)


def experts_kernel(block, more, *refs):
    if more:
        mixed, own, router, w_in, w_out, b_in, b_out, *rest = refs
        old_mine, old_mate, old_router, back, sent, dw_mine, dw_mate, drouter, *rest = rest
        *rest, rows = rest
        ups, shift = mixed, block

        @pl.when(pl.program_id(0) == 0)
        def _():
            for i in range(mixed.shape[0]):
                rows[i * block : (i + 1) * block, :] = mixed[i, 0:block, :]

        outs = (back, sent, 0)
        old = (old_mine, old_mate, old_router)
    else:
        rows, ups, own, router, w_in, w_out, b_in, b_out, *rest = refs
        ret, dw_mine, dw_mate, drouter, *rest = rest
        outs = (ret, ret, block)
        shift, old = 0, None
    experts_body(
        block, rows, ups, shift, own, router, w_in, w_out, b_in, b_out, old,
        outs, dw_mine, dw_mate, drouter, *rest,
    )


def experts_body(
    block, rows, ups, shift, own, router, w_in, w_out, b_in, b_out, old,
    outs, dw_mine, dw_mate, drouter,
    gate, weighted, made, pushed, hid, pre_g, other, db,
):
    f = pl.program_id(0)
    last = pl.num_programs(0) - 1
    total, width = rows.shape
    steps = total // block
    lane = lane_iota(1, LANES)

    @pl.when(f == 0)
    def _():
        own_hot = own[...] > 0.0

        def step(i, acc):
            at = pl.ds(pl.multiple_of(i * block, block), block)
            logits = mm(rows[at, :], router[...])
            mine = jnp.sum(jnp.where(own_hot, logits, 0.0), axis=1, keepdims=True)
            named = ups[i, shift + block : shift + block + EXTRA, 0:block].astype(F32)
            rival = jnp.transpose(named)[:, 0:1].astype(jnp.int32)
            other[at, :] = rival
            theirs = jnp.sum(jnp.where(lane == rival, logits, 0.0), axis=1, keepdims=True)
            share = 1.0 / (1.0 + jnp.exp(theirs - mine))
            gate[at, 0:1] = share
            gate[at, 1:2] = 1.0 / (1.0 + jnp.exp(mine - theirs))
            scaled = (share * ups[i, shift : shift + block, :].astype(F32)).astype(BF16)
            weighted[at, :] = scaled
            return acc + jnp.sum(scaled.astype(F32), axis=0, keepdims=True)

        db[...] = jnp.zeros_like(db)
        db[1:2, :] = lax.fori_loop(0, steps, step, jnp.zeros((1, width), F32))

    chunk = w_in.shape[1]
    hidden_share = (dw_mine.shape[1] - EXTRA) // 2
    per = hidden_share // chunk
    place = f % per
    biases = b_in[0, 0:1, :].astype(F32)
    bias = biases[:, 0:chunk]
    for k in range(1, per):
        bias = jnp.where(place == k, biases[:, k * chunk : (k + 1) * chunk], bias)

    big = total // BIG_STEPS

    def body(i, acc):
        at = pl.ds(pl.multiple_of(i * big, big), big)
        here = rows[at, :]
        u = mm_nt(here, w_in[0]) + bias
        inner = ROOT + (ROOT * CUBIC) * (u * u)
        share = 0.5 + 0.5 * jnp.tanh(u * inner)
        raised = u * share
        hidden = raised.astype(BF16)
        slope = share + raised * (1.0 - share) * (6.0 * inner - 4.0 * ROOT)
        hid[at, :] = hidden
        grad = mm_nt(weighted[at, :], w_out[0]) * slope
        low = grad.astype(BF16)
        pre_g[at, :] = low
        part = mm(hidden, w_out[0])
        part_b = mm(low, w_in[0])

        @pl.when(f == 0)
        def _():
            made[at, :] = part
            pushed[at, :] = part_b

        @pl.when(f > 0)
        def _():
            made[at, :] += part
            pushed[at, :] += part_b

        return acc + jnp.sum(grad, axis=0, keepdims=True)

    db_here = lax.fori_loop(0, BIG_STEPS, body, jnp.zeros((1, chunk), F32))
    for k in range(per):

        @pl.when(place == k)
        def _():
            db[0:1, k * chunk : (k + 1) * chunk] = db_here

    dw_out_here = mm_tn(hid[...], weighted[...])
    dw_in_here = mm_tn(pre_g[...], rows[...])

    def put(target, prior):
        spots = (
            (pl.ds(pl.multiple_of(place * chunk, chunk), chunk), dw_in_here),
            (pl.ds(pl.multiple_of(hidden_share + place * chunk, chunk), chunk), dw_out_here),
            (pl.ds(2 * hidden_share, EXTRA), db[...]),
        )
        for spot, value in spots:
            if prior is not None:
                value = value + prior[0, spot, :].astype(F32)
            target[0, spot, :] = value.astype(BF16)

    quarters = (last + 1) // per

    @pl.when(f // per < quarters // 2)
    def _():
        put(dw_mine, old and old[0])

    @pl.when(f // per >= quarters // 2)
    def _():
        put(dw_mate, old and old[1])

    @pl.when(f == last)
    def _():
        own_row = own[...]
        back, sent, after = outs

        def step(i, carry):
            at = pl.ds(pl.multiple_of(i * block, block), block)
            produced = (made[at, :] + b_out[...]).astype(BF16).astype(F32)
            share = gate[at, 0:1]
            sent[i, after : after + block, :] = (share * produced).astype(BF16)
            inner = jnp.sum(produced * ups[i, shift : shift + block, :].astype(F32), axis=1, keepdims=True)
            pull = share * gate[at, 1:2] * inner
            rival = other[at, :]
            spread = (pull * (own_row - jnp.where(lane == rival, 1.0, 0.0))).astype(BF16)
            back[i, 0:block, :] = (pushed[at, :] + mm_nt(spread, router[...])).astype(BF16)
            hid[at, 0:LANES] = spread
            return carry

        lax.fori_loop(0, steps, step, 0)
        drouter[...] = mm_tn(rows[...], hid[:, 0:LANES]) + (0.0 if old is None else old[2][...])


def run_experts(given, block, own, dense, weights, b_out, old):
    experts, _, width = given[0].shape
    total = experts * block
    first, second = weights
    quarters, share, _ = first.shape
    chunk = min(share, 512)
    per = share // chunk
    half = quarters // 2
    at = lambda f: (f // per, f % per, 0)
    bias_at = lambda f: (f // per, share // EXTRA, 0)
    mine_at = lambda f: (jnp.minimum(f // per, half - 1), 0, 0)
    mate_at = lambda f: (jnp.maximum(f // per - half, 0), 0, 0)
    double = 2 * share + EXTRA
    steps = quarters * per
    dw_shape = jax.ShapeDtypeStruct((half, double, width), BF16)
    sums = [
        pl.BlockSpec((1, double, width), mine_at),
        pl.BlockSpec((1, double, width), mate_at),
        whole((width, LANES)),
    ]
    if old:
        given_specs = [whole(given[0].shape)]
        ret_shapes = [(experts, block, width)] * 2
        more_scratch = [pltpu.VMEM((total, width), BF16)]
    else:
        given = (given[0].reshape(total, width), given[1])
        given_specs = [whole(given[0].shape), whole(given[1].shape)]
        ret_shapes = [(experts, 2 * block, width)]
        more_scratch = []
    return pl.pallas_call(
        partial(experts_kernel, block, bool(old)),
        grid=(steps,),
        in_specs=given_specs
        + [
            whole((1, LANES)),
            small_spec(width),
            pl.BlockSpec((1, chunk, width), at),
            pl.BlockSpec((1, chunk, width), at),
            pl.BlockSpec((1, EXTRA, width), bias_at),
            whole((1, width)),
        ]
        + (sums if old else []),
        out_specs=[whole(r) for r in ret_shapes] + sums,
        out_shape=[jax.ShapeDtypeStruct(r, BF16) for r in ret_shapes]
        + [dw_shape, dw_shape, jax.ShapeDtypeStruct((width, LANES), F32)],
        scratch_shapes=[
            pltpu.VMEM((total, 2), F32),
            pltpu.VMEM((total, width), BF16),
            pltpu.VMEM((total, width), F32),
            pltpu.VMEM((total, width), F32),
            pltpu.VMEM((total, chunk), BF16),
            pltpu.VMEM((total, chunk), BF16),
            pltpu.VMEM((total, 1), jnp.int32),
            pltpu.VMEM((EXTRA, width), F32),
        ]
        + more_scratch,
        compiler_params=params(1),
        name="experts",
        cost_estimate=cost(50),
    )(*given, own, dense, first, second, second, b_out, *old)


def backward_kernel(
    experts, x, mask, small, wqkv, wout, triple, context, logs, residual, up, slot, ret_a, ret_b, drouter,
    input_grad, packed,
    tg, gains, dqkv, dwout, dgains,
):
    step = pl.program_id(0)
    length, width = x.shape

    @pl.when(step == 0)
    def _():
        dqkv[...] = jnp.zeros_like(dqkv)
        dwout[...] = jnp.zeros_like(dwout)
        dgains[...] = jnp.zeros_like(dgains)
        gains[0:4, :] = gain_rows(small, experts)

    second_grad = gather_slots(slot, (ret_a, ret_b))
    unit_b, scale_b = norm_stats(residual[...])
    dgains[experts + 2 : experts + 3, :] += jnp.sum(second_grad * unit_b, axis=0, keepdims=True)
    dgains[experts + 3 : experts + 4, :] += jnp.sum(second_grad, axis=0, keepdims=True)
    residual_grad = up[...].astype(F32) + norm_back(second_grad, unit_b, scale_b, gains[2:3, :])
    residual_low = residual_grad.astype(BF16)
    dwout[...] += mm_tn(context[...], residual_low)
    context_grad = mm_nt(residual_low, wout[...]).astype(BF16)

    lane = lane_iota(1, LANES)
    head_width = width // HEADS
    scale = head_width ** (-0.5)
    per = LANES // head_width
    hide_row = jnp.where(mask[0] > 0, 0.0, NEGATIVE)
    hide = jnp.transpose(jnp.broadcast_to(hide_row, (LANES, length)))[:, 0:1]
    for group in range(HEADS // per):
        begin = group * LANES
        queries = triple[:, begin : begin + LANES]
        keys = triple[:, width + begin : width + begin + LANES]
        values = triple[:, 2 * width + begin : 2 * width + begin + LANES]
        pulled = context_grad[:, begin : begin + LANES]
        dq = jnp.zeros((length, LANES), F32)
        dk = jnp.zeros((length, LANES), F32)
        dv = jnp.zeros((length, LANES), F32)
        for inner in range(per):
            head = group * per + inner
            inside = (lane >= inner * head_width) & (lane < (inner + 1) * head_width)
            chosen = queries * jnp.where(inside, scale, 0.0).astype(BF16)
            log_row = logs[0, head : head + 1, :]
            probs = jnp.exp(mm_nt(keys, chosen) + hide - log_row)
            picked = pulled * jnp.where(inside, 1.0, 0.0).astype(BF16)
            prob_grad = mm_nt(values, picked)
            inner_sum = jnp.sum(probs * prob_grad, axis=0, keepdims=True)
            score_grad = (probs * (prob_grad - inner_sum)).astype(BF16)
            dq = jnp.where(inside, mm_tn(score_grad, keys), dq)
            dk = jnp.where(inside, mm(score_grad, queries), dk)
            dv = jnp.where(inside, mm(probs.astype(BF16), pulled), dv)
        tg[:, begin : begin + LANES] = (dq * scale).astype(BF16)
        tg[:, width + begin : width + begin + LANES] = (dk * scale).astype(BF16)
        tg[:, 2 * width + begin : 2 * width + begin + LANES] = dv.astype(BF16)
    unit, scale_a = norm_stats(x[...].astype(F32))
    low = (unit * gains[0:1, :] + gains[1:2, :]).astype(BF16)
    dqkv[...] += mm_tn(low, tg[...])
    first_grad = mm_nt(tg[...], wqkv[...])
    dgains[experts + 0 : experts + 1, :] += jnp.sum(first_grad * unit, axis=0, keepdims=True)
    dgains[experts + 1 : experts + 2, :] += jnp.sum(first_grad, axis=0, keepdims=True)
    input_grad[...] = residual_grad + norm_back(first_grad, unit, scale_a, gains[0:1, :])

    @pl.when(step == pl.num_programs(0) - 1)
    def _():
        packed[:, : 3 * width] = dqkv[...].astype(BF16)
        packed[:, 3 * width : 4 * width] = dwout[...].astype(BF16)
        packed[:, 4 * width :] = (drouter[...] + jnp.transpose(dgains[...])).astype(BF16)


def attention_backward(
    x, mask, dense, triple, context, logs, residual, up, slot, ret, drouter, experts
):
    total, width = x.shape
    images, length = mask.shape
    rows = lambda i: (i, 0)
    return pl.pallas_call(
        partial(backward_kernel, experts),
        grid=(images,),
        in_specs=[
            pl.BlockSpec((length, width), rows),
            pl.BlockSpec((1, 1, length), lambda i: (i, 0, 0)),
            small_spec(width),
            pl.BlockSpec((width, 3 * width), lambda i: (0, 0), pipeline_mode=pl.Buffered(1)),
            pl.BlockSpec((width, width), lambda i: (0, 3), pipeline_mode=pl.Buffered(1)),
            pl.BlockSpec((length, 3 * width), rows),
            pl.BlockSpec((length, width), rows),
            pl.BlockSpec((1, HEADS, length), lambda i: (i, 0, 0)),
            pl.BlockSpec((length, width), rows),
            pl.BlockSpec((length, width), rows),
            pl.BlockSpec((length, 2), rows),
            *returned_specs(ret, 0),
            whole((width, LANES)),
        ],
        out_specs=[
            pl.BlockSpec((length, width), rows),
            whole((width, 4 * width + LANES)),
        ],
        out_shape=[
            jax.ShapeDtypeStruct((total, width), F32),
            jax.ShapeDtypeStruct((width, 4 * width + LANES), BF16),
        ],
        scratch_shapes=[
            pltpu.VMEM((length, 3 * width), BF16),
            pltpu.VMEM((8, width), F32),
            pltpu.VMEM((width, 3 * width), F32),
            pltpu.VMEM((width, width), F32),
            pltpu.VMEM((LANES, width), F32),
        ],
        compiler_params=params(1),
        name="attention_backward",
        cost_estimate=cost(50),
    )(
        x, mask.reshape(images, 1, length), dense, dense, dense, triple, context, logs, residual,
        up, slot, *ret, drouter,
    )


def combine_kernel(slot, residual, ret_a, ret_b, out):
    out[...] = (residual[...] + gather_slots(slot, (ret_a, ret_b))).astype(BF16)


def combine(slot, residual, ret, block):
    total, width = residual.shape
    rows = lambda i: (i, 0)
    return pl.pallas_call(
        combine_kernel,
        grid=(total // block,),
        in_specs=[
            pl.BlockSpec((block, 2), rows),
            pl.BlockSpec((block, width), rows),
            *returned_specs(ret, 1),
        ],
        out_specs=pl.BlockSpec((block, width), rows),
        out_shape=jax.ShapeDtypeStruct((total, width), BF16),
        compiler_params=params(1),
        name="combine",
        cost_estimate=cost(10),
    )(slot, residual, *ret)


class PlainPlan:
    def __init__(self, seq, wt):
        self.seq, self.wt = seq, wt

    def own_id(self):
        return lax.axis_index("seq")

    def exchange(self, a):
        return lax.all_to_all(a, "seq", split_axis=0, concat_axis=0, tiled=True)

    def begin_dense(self, packed):
        return packed

    def gather_dense(self, packed, begun):
        return lax.all_gather(begun, "wt", axis=0, tiled=True)

    def begin_fetch(self, packed):
        return (packed,)

    def fetch(self, packed, begun):
        return lax.all_gather(begun[0], "wt", axis=0)

    def spread_out_bias(self, quarters):
        return quarters

    def begin_reduce(self, mine, mate):
        return (jnp.concatenate([mine, mate]).reshape(-1, mine.shape[-1]),)

    def reduce_expert(self, parts):
        (parts,) = parts
        return lax.psum_scatter(parts, "wt", scatter_dimension=0, tiled=True)

    def finish_expert(self, parts, received):
        return received.astype(F32)

    def begin_dense_sum(self, grads):
        return lax.psum_scatter(grads, "wt", scatter_dimension=0, tiled=True)

    def reduce_dense(self, part):
        return lax.psum(part, "seq").astype(F32)


class CubePlan:
    AXES = ("seq", "wt")

    def __init__(self, seq, wt):
        self.seq, self.wt = seq, wt
        self.levels = seq // 2
        places = [
            (z, y, x, c)
            for z in range(self.levels)
            for y in range(2)
            for x in range(2)
            for c in range(2)
        ]
        flat = self.flat
        self.cross = [(flat(*p), flat(p[0], p[1], 1 - p[2], p[3])) for p in places]
        self.core = [(flat(*p), flat(p[0], p[1], p[2], 1 - p[3])) for p in places]
        swap = lambda p: (p[0] ^ 2, p[1], 1, p[3]) if p[2] == 0 else (p[0], p[1], 0, p[3])
        self.first = [(flat(*p), flat(*swap(p))) for p in places]
        self.second = [
            (flat(*p), flat(p[0] ^ 2, p[1], 1, p[3])) for p in places if p[2] == 1
        ]
        self.groups = [
            [self.host(half, e, c) for e in range(seq)] for half in range(2) for c in range(2)
        ]

    def flat(self, z, y, x, c):
        return (z * 2 + y) * self.wt + x * 2 + c

    def host(self, half, expert, c):
        z, y = expert // 2, expert % 2
        if z // 2 == half:
            return self.flat(z, y, 0, c)
        return self.flat(z ^ 2, y, 1, c)

    def send(self, a, pairs):
        return lax.ppermute(a, self.AXES, pairs)

    def x_zero(self):
        return lax.axis_index("wt") < 2

    def core_zero(self):
        return lax.axis_index("wt") % 2 == 0

    def own_id(self):
        rank = lax.axis_index("seq")
        return jnp.where(self.x_zero(), rank, rank ^ 4)

    def exchange(self, a):
        return lax.all_to_all(
            a, self.AXES, split_axis=0, concat_axis=0, axis_index_groups=self.groups, tiled=True
        )

    def begin_dense(self, packed):
        return self.send(packed, self.cross)

    def gather_dense(self, packed, far):
        mate = self.send(packed, self.core)
        far_mate = self.send(far, self.core)
        flip = self.x_zero()
        low, high = jnp.where(flip, packed, far), jnp.where(flip, far, packed)
        low_mate, high_mate = jnp.where(flip, mate, far_mate), jnp.where(flip, far_mate, mate)
        first = self.core_zero()
        return jnp.concatenate(
            [
                jnp.where(first, low, low_mate),
                jnp.where(first, low_mate, low),
                jnp.where(first, high, high_mate),
                jnp.where(first, high_mate, high),
            ],
            axis=0,
        )

    def begin_fetch(self, packed):
        return self.send(packed, self.first), self.send(packed, self.second)

    def fetch(self, packed, begun):
        got, got_b = begun
        flip = self.x_zero()
        low = jnp.where(flip, packed, got)
        high = jnp.where(flip, got, got_b)
        return jnp.stack([low, high, self.send(low, self.core), self.send(high, self.core)])

    def spread_out_bias(self, quarters):
        a, b, c, d = (quarters[i] for i in range(4))
        return jnp.where(
            self.core_zero(), jnp.stack([a, c, b, d]), jnp.stack([c, a, d, b])
        )

    def begin_reduce(self, mine, mate):
        got = self.send(mate, self.core)
        low = (mine[0].astype(F32) + got[0].astype(F32)).astype(BF16)
        high = (mine[1].astype(F32) + got[1].astype(F32)).astype(BF16)
        return low, high, jnp.where(self.x_zero(), high, low)

    def reduce_expert(self, parts):
        low, high, give = parts
        return self.send(give, self.first_back()), self.send(high, self.second)

    def finish_expert(self, parts, received):
        far, far_b = received
        return jnp.where(self.x_zero(), parts[0], far_b).astype(F32) + far.astype(F32)

    def first_back(self):
        return [(b, a) for a, b in self.first]

    def begin_dense_sum(self, grads):
        share = grads.shape[0] // 4
        width = grads.shape[1]
        parts = [grads[i * share : (i + 1) * share] for i in range(4)]
        first = self.core_zero()
        keep = [jnp.where(first, parts[0], parts[1]), jnp.where(first, parts[2], parts[3])]
        give = [jnp.where(first, parts[1], parts[0]), jnp.where(first, parts[3], parts[2])]
        got = [self.send(v.astype(BF16), self.core).astype(F32) for v in give]
        low, high = keep[0].astype(F32) + got[0], keep[1].astype(F32) + got[1]
        flip = self.x_zero()
        out = self.send(jnp.where(flip, high, low).astype(BF16), self.cross)
        mine = jnp.where(flip, low, high) + out.astype(F32)
        return mine.astype(BF16)

    def reduce_dense(self, mine):
        share, width = mine.shape
        pieces = mine.reshape(self.seq, share // self.seq, width)
        swap = lambda v: lax.all_to_all(v, "seq", split_axis=0, concat_axis=0, tiled=True)
        total = jnp.sum(swap(pieces).astype(F32), axis=0, keepdims=True).astype(BF16)
        spread = swap(jnp.broadcast_to(total, pieces.shape))
        return spread.reshape(share, width).astype(F32)


def plan_of(seq, wt):
    return CubePlan(seq, wt) if (seq, wt) == (8, 4) else PlainPlan(seq, wt)


def local(
    inputs,
    key_mask,
    routes,
    priority,
    capacity,
    attention_gain,
    attention_shift,
    query_key_value,
    attention_out,
    mixture_gain,
    mixture_shift,
    router_weight,
    expert_in,
    expert_in_bias,
    expert_out,
    expert_out_bias,
    cotangent,
):
    total, width = inputs.shape
    experts = capacity.shape[0]
    cap = 8 * max(1, total // (4 * experts))
    share = query_key_value.shape[0]
    hidden_share = expert_in.shape[1]
    plan = plan_of(lax.axis_size("seq"), lax.axis_size("wt"))

    tie = lax.optimization_barrier
    front = (cap // 2 + EXTRA - 1) // EXTRA * EXTRA
    parts = (front, cap - front)
    packed, *shards = pack(
        query_key_value, attention_out, router_weight,
        (attention_gain, attention_shift, mixture_gain, mixture_shift),
        expert_in[0], expert_out[0], expert_in_bias, expert_out_bias,
    )
    fetched = [plan.begin_fetch(shard) for shard in shards]
    far = plan.begin_dense(packed)
    own = (jnp.arange(LANES) == plan.own_id()).astype(F32)[None, :]
    route_rows = routes.T
    slot, slot_rows = make_slots(route_rows, priority, capacity, parts)
    slot_rows, far = tie((slot_rows, far))
    ups_a, ups_b = dispatch(slot_rows, route_rows, cotangent, experts, parts)
    dense = plan.gather_dense(packed, far)
    dense, ups_a, fetched[0] = tie((dense, ups_a, fetched[0]))
    ups_a = plan.exchange(ups_a)

    triple, context, logs, residual, normed = attention_forward(inputs, key_mask, dense, experts)
    rows_a, mixed_b = dispatch(slot_rows, route_rows, normed, experts, parts, ups_b)
    rows_a, ups_a, fetched[1] = tie((rows_a, ups_a, fetched[1]))
    weights = [plan.fetch(*pair) for pair in zip(shards, fetched)]
    b_out = plan.spread_out_bias(
        weights[1][:, hidden_share + 1, :share].astype(F32)
    ).reshape(1, width)
    rows_a = plan.exchange(rows_a)
    rows_a, mixed_b = tie((rows_a, mixed_b))
    mixed_b = plan.exchange(mixed_b)
    ret_a, *sums = run_experts((rows_a, ups_a), parts[0], own, dense, weights, b_out, ())
    ret_a, mixed_b = tie((ret_a, mixed_b))
    ret_a = plan.exchange(ret_a)
    back_b, sent_b, *sums = run_experts(
        (mixed_b,), parts[1], own, dense, weights, b_out, tuple(sums)
    )
    back_b, ret_a = tie((back_b, ret_a))
    back_b = plan.exchange(back_b)
    halves = plan.begin_reduce(*sums[:2])
    back_b, sent_b, halves = tie((back_b, sent_b, halves))
    sent_b = plan.exchange(sent_b)
    received = plan.reduce_expert(halves)
    ret_a = ret_a.reshape(experts, 2, front, width)
    input_grad, grads = attention_backward(
        inputs, key_mask, dense, triple, context, logs, residual, cotangent, slot,
        (ret_a, back_b), sums[2], experts,
    )
    grads, sent_b, received = tie((grads, sent_b, received))
    mine = plan.begin_dense_sum(grads)
    shard = plan.finish_expert(halves, received)
    done = plan.reduce_dense(mine)
    block_output = combine(slot, residual, (ret_a, sent_b), 400)
    base = 4 * width
    rank = lax.axis_index("wt")
    return (
        block_output,
        input_grad,
        done[:, base + experts],
        done[:, base + experts + 1],
        done[:, : 3 * width],
        done[:, 3 * width : base],
        done[:, base + experts + 2],
        done[:, base + experts + 3],
        done[:, base : base + experts],
        shard[None, :hidden_share],
        shard[2 * hidden_share, :hidden_share][None],
        shard[None, hidden_share : 2 * hidden_share],
        lax.dynamic_slice(shard[2 * hidden_share + 1], (rank * share,), (share,))[None],
    )


def solution(mesh):
    both = P(("seq", "wt"), None)
    placed = (
        both,
        both,
        both,
        both,
        P(),
        P("wt"),
        P("wt"),
        P("wt", None),
        P("wt", None),
        P("wt"),
        P("wt"),
        P("wt", None),
        P("seq", "wt", None),
        P("seq", "wt"),
        P("seq", "wt", None),
        P("seq", "wt"),
        both,
    )
    return jax.shard_map(
        local,
        mesh=mesh,
        in_specs=placed,
        out_specs=(
            both,
            both,
            P("wt"),
            P("wt"),
            P("wt", None),
            P("wt", None),
            P("wt"),
            P("wt"),
            P("wt", None),
            P("seq", "wt", None),
            P("seq", "wt"),
            P("seq", "wt", None),
            P("seq", "wt"),
        ),
        check_vma=False,
    )
```

time: 603 us -> 423 us (0.70)
  waiting for transfers between devices: 284 us -> 80.9 us
  starting transfers between devices: 16.2 us -> 84.8 us
  local copies, waits for them, and re-layouts: 32.1 us -> 10.2 us
  Pallas kernels: 212 us -> 196 us
  between operations: 15.7 us -> 0.9 us
    all_to_all x4 -> x7, waiting for transfers between devices: 159 us -> 39.4 us  [the longest x5 23.4 us: exchange(): lax.all_to_all(a, self.AXES, split_axis=0, concat_axis=0, axis_index_grou...]
    psum x1 -> x0, waiting for transfers between devices: 52.9 us -> none  [local(): done = lax.psum(part, 'seq').astype(F32)]
    reduce_scatter x3 -> x0, waiting for transfers between devices: 48.5 us -> none  [the longest x1 33.8 us: local(): lax.psum_scatter(dw_in.reshape(-1, width), 'wt', scatter_dimension=0, til...]
    ppermute x0 -> x17, waiting for transfers between devices: none -> 41.5 us  [send(): return lax.ppermute(a, self.AXES, pairs)]
    ppermute x0 -> x17, starting transfers between devices: none -> 40.8 us  [send(): return lax.ppermute(a, self.AXES, pairs)]
    all_to_all x4 -> x7, starting transfers between devices: 15.7 us -> 44.1 us  [the longest x5 35.3 us: exchange(): lax.all_to_all(a, self.AXES, split_axis=0, concat_axis=0, axis_index_grou...]
    all_gather x2 -> x0, waiting for transfers between devices: 21.9 us -> none  [the longest x1 21.9 us: local(): dense = lax.all_gather(packed, 'wt', axis=0, tiled=True)]
    pallas_call x6 -> x8, Pallas kernels: 202 us -> 186 us  [the longest x2 86.7 us: run_experts(): pl.pallas_call(partial(experts_kernel, block, bool(old)), grid=(steps,),...]
  transfers between devices with their start and end apart: 10 -> 24, of which waited for: 8 -> 11; matrix products, arithmetic and copies ran while one was open for 5% -> 4% of each run, Pallas kernels for 14% -> 46%
where the time goes in v2:
time: 423 us; the launch traced here: 422 us
  Pallas kernels  196 us (46%)
  starting transfers between devices  84.8 us (20%)
  waiting for transfers between devices  80.9 us (19%)
  blocking collectives  27.9 us (7%)
  other arithmetic  20.6 us (5%)
  local copies, waits for them, and re-layouts  10.2 us (2%)
    pallas_call x2, Pallas kernels, run_experts(): pl.pallas_call(partial(experts_kernel, block, bool(old)), grid=(steps,),...  86.7 us
    pallas_call x1, Pallas kernels, attention_backward(): pl.pallas_call(partial(backward_kernel, experts), grid=(images,), in_spec...  51.5 us
    ppermute x17, waiting for transfers between devices, send(): return lax.ppermute(a, self.AXES, pairs)  41.5 us
    ppermute x17, starting transfers between devices, send(): return lax.ppermute(a, self.AXES, pairs)  40.8 us
    all_to_all x5, starting transfers between devices, exchange(): lax.all_to_all(a, self.AXES, split_axis=0, concat_axis=0, axis_index_grou...  35.3 us
    all_to_all x1, blocking collectives, exchange(): lax.all_to_all(a, self.AXES, split_axis=0, concat_axis=0, axis_index_grou...  27.9 us
    all_to_all x5, waiting for transfers between devices, exchange(): lax.all_to_all(a, self.AXES, split_axis=0, concat_axis=0, axis_index_grou...  23.4 us
    pallas_call x2, Pallas kernels, dispatch(): pl.pallas_call(partial(dispatch_kernel, parts, with_other), grid=(experts...  20.9 us
  transfers between devices with their start and end apart: 24, of which 11 were waited for; matrix products, arithmetic and copies ran while one was open for 4% of the time, Pallas kernels for 46%

profile of v2, /device:TPU:0, one launch (start us, length us, event | category | flops | bytes accessed | tf_op | source)
XLA Modules:
  0.0 421.5 jit_solution(8581260695438517052)
XLA Ops:
  0.6 1.4 copy.35.router
  2.0 2.7 pack.1
  4.7 2.9 collective-permute-start
  7.7 7.9 %slots.1 = (s32[1600,2]{1,0:T(8,128)}, s32[2,1600]{1,0:T(2,128)}) custom-call(s32[1,1600]{1,0:T(1,128)} %prow.1, s32[2,1600]{1,0:T(2,128)} %bitcast.52, s32[1,8]{1,0:T(1,128)} %bitcast.61), custom_call_target="tpu_custom_call" | custom-call | flops 80000000 | bytes 80000 | tf_op jit(solution)/shard_map/slots/pallas_call | solution.py:198
  15.5 5.0 %collective-permute-done = bf16[128,2176]{1,0:T(8,128)(2,1)S(1)} collective-permute-done((bf16[128,2176]{1,0:T(8,128)(2,1)}, bf16[128,2176]{1,0:T(8,128)(2,1)S(1)}, u32[]{:S(2)}, u32[]{:S(2)}) %collective-permute-start) | collective-permute-done | bytes 557088 | tf_op jit(solution)/shard_map/ppermute | solution.py:776
  20.6 0.7 collective-permute-start.4
  21.3 5.3 %collective-permute-start.3 = (bf16[512,512]{1,0:T(8,128)(2,1)}, bf16[512,512]{1,0:T(8,128)(2,1)}, u32[]{:S(2)}, u32[]{:S(2)}) collective-permute-start(bf16[512,512]{1,0:T(8,128)(2,1)} %get-tuple-element.69), channel_id=1, source_target_pairs={{0,18},{1,19},{2,0},{3,1},{4,22},{5,23},{6,4},{7,5},{8,26},{9,27},... | collective-permute-start | bytes 1572872 | tf_op jit(solution)/shard_map/ppermute | solution.py:776
  26.6 10.5 %dispatch.2 = (bf16[8,224,512]{2,1,0:T(8,128)(2,1)}, bf16[8,208,512]{2,1,0:T(8,128)(2,1)}) custom-call(s32[2,1600]{1,0:T(2,128)} %get-tuple-element.67.slot_rows, s32[2,1600]{1,0:T(2,128)} %bitcast.53, bf16[1600,512]{1,0:T(8,128)(2,1)} %up.1), custom_call_target="tpu_custom_call" | custom-call | flops 100000000 | bytes 100000 | tf_op jit(solution)/shard_map/dispatch/pallas_call | solution.py:247
  37.3 1.5 pad_maximum_fusion.small.wqkv.wout.refs_3_.refs_2_
  38.9 0.6 collective-permute-done.3
  39.4 17.0 %all-to-all-start = ((bf16[8,224,512]{2,1,0:T(8,128)(2,1)}), bf16[8,224,512]{2,1,0:T(8,128)(2,1)S(1)}, u32[]{:S(2)}, u32[]{:S(2)}) async-start(bf16[8,224,512]{2,1,0:T(8,128)(2,1)} %get-tuple-element.75), calls=%async_computation | async-start | bytes 3670016 | tf_op jit(solution)/shard_map/all_to_all | solution.py:789
  56.4 0.7 collective-permute-start.6
  57.1 5.6 %collective-permute-start.5 = (bf16[528,512]{1,0:T(8,128)(2,1)S(1)}, bf16[528,512]{1,0:T(8,128)(2,1)}, u32[]{:S(2)}, u32[]{:S(2)}) collective-permute-start(bf16[528,512]{1,0:T(8,128)(2,1)S(1)} %copy-done.9), channel_id=1, source_target_pairs={{0,18},{1,19},{2,0},{3,1},{4,22},{5,23},{6,4},{7,5},{8,26},{9,27},... | collective-permute-start | bytes 1622024 | tf_op jit(solution)/shard_map/ppermute | solution.py:776
  62.8 0.6 reshape.91.mask
  63.4 16.8 %attention_forward.1 = (bf16[1600,1536]{1,0:T(8,128)(2,1)}, bf16[1600,512]{1,0:T(8,128)(2,1)}, f32[8,8,200]{2,1,0:T(8,128)}, f32[1600,512]{1,0:T(8,128)}, bf16[1600,512]{1,0:T(8,128)(2,1)}) custom-call(bf16[1600,512]{1,0:T(8,128)(2,1)} %x.3, s32[8,1,200]{2,1,0:T(1,128)} %reshape.91.mask, bf16[512,2176]{1,0:T(8,128)(2,1)} %pad_maximum_fusion.small.wqkv.wout.refs_3_.refs_2_, ...), custom_call_target="tpu_custom_call" | custom-call | flops 170000000 | bytes 170000 | tf_op jit(solution)/shard_map/attention_forward/pallas_call | solution.py:315
  80.2 10.4 %dispatch.3 = (bf16[8,208,512]{2,1,0:T(8,128)(2,1)}, bf16[8,400,512]{2,1,0:T(8,128)(2,1)}) custom-call(s32[2,1600]{1,0:T(2,128)} %get-tuple-element.67.slot_rows, s32[2,1600]{1,0:T(2,128)} %bitcast.54, bf16[1600,512]{1,0:T(8,128)(2,1)} %get-tuple-element.72.rows, bf16[8,208,512]{2,1,0:T(8,128)(2,1)} %get-tuple-element.73.outs_0_), custom_call_target="tpu_custom_call" | custom-call | flops 100000000 | bytes 100000 | tf_op jit(solution)/shard_map/dispatch/pallas_call | solution.py:247
  90.6 1.6 collective-permute-done.5
  92.3 27.9 %all_to_all.40 = bf16[8,208,512]{2,1,0:T(8,128)(2,1)} all-to-all(bf16[8,208,512]{2,1,0:T(8,128)(2,1)} %get-tuple-element.77), channel_id=1, replica_groups={{0,4,8,12,2,6,10,14},{1,5,9,13,3,7,11,15},{18,22,26,30,16,20,24,28},{19..., dimensions={0} | all-to-all | bytes 3407872 | tf_op jit(solution)/shard_map/all_to_all | solution.py:789
  120.2 4.7 %all-to-all-start.2 = ((bf16[8,400,512]{2,1,0:T(8,128)(2,1)}), bf16[8,400,512]{2,1,0:T(8,128)(2,1)}, u32[]{:S(2)}, u32[]{:S(2)}) async-start(bf16[8,400,512]{2,1,0:T(8,128)(2,1)} %get-tuple-element.86), calls=%async_computation.2 | async-start | bytes 6553600 | tf_op jit(solution)/shard_map/all_to_all | solution.py:789
  124.9 1.3 broadcast_select_fusion.16
  126.2 0.5 collective-permute-start.8
  126.7 1.1 broadcast_select_fusion.14
  128.0 0.4 collective-permute-start.10
  128.4 0.5 compare_convert_fusion.refs_2_.refs_1_
  129.0 2.8 pad_maximum_fusion.2.refs_4_.refs_3_
  131.8 0.8 copy-done.7
  132.8 1.5 pad_maximum_fusion.1.refs_5_.refs_6_.refs_4_
  134.3 0.7 maximum_select_fusion
  134.9 0.7 copy-done
  135.6 44.4 %experts.2 = (bf16[8,416,512]{2,1,0:T(8,128)(2,1)}, bf16[2,1040,512]{2,1,0:T(8,128)(2,1)}, bf16[2,1040,512]{2,1,0:T(8,128)(2,1)}, f32[512,128]{1,0:T(8,128)}) custom-call(bf16[1664,512]{1,0:T(8,128)(2,1)} %bitcast.43, bf16[8,224,512]{2,1,0:T(8,128)(2,1)} %copy-done.3, f32[1,128]{1,0:T(1,128)} %compare_convert_fusion.refs_2_.refs_1_, ...), custom_call_target="tpu_custom_call" | custom-call | flops 500000000 | bytes 500000 | tf_op jit(solution)/shard_map/experts/pallas_call | solution.py:525
  180.0 4.8 %all-to-all-start.3 = ((bf16[8,416,512]{2,1,0:T(8,128)(2,1)}), bf16[8,416,512]{2,1,0:T(8,128)(2,1)S(1)}, u32[]{:S(2)}, u32[]{:S(2)}) async-start(bf16[8,416,512]{2,1,0:T(8,128)(2,1)} %get-tuple-element.92), calls=%async_computation.3 | async-start | bytes 6815744 | tf_op jit(solution)/shard_map/all_to_all | solution.py:789
  184.8 42.4 %experts.3 = (bf16[8,192,512]{2,1,0:T(8,128)(2,1)}, bf16[8,192,512]{2,1,0:T(8,128)(2,1)}, bf16[2,1040,512]{2,1,0:T(8,128)(2,1)}, bf16[2,1040,512]{2,1,0:T(8,128)(2,1)}, f32[512,128]{1,0:T(8,128)}) custom-call(bf16[8,400,512]{2,1,0:T(8,128)(2,1)} %all-to-all-done.2.refs_0_, f32[1,128]{1,0:T(1,128)} %compare_convert_fusion.refs_2_.refs_1_, ...), custom_call_target="tpu_custom_call" | custom-call | flops 500000000 | bytes 500000 | tf_op jit(solution)/shard_map/experts/pallas_call | solution.py:525
  227.2 5.4 %all-to-all-done.3 = bf16[8,416,512]{2,1,0:T(8,128)(2,1)S(1)} async-done(((bf16[8,416,512]{2,1,0:T(8,128)(2,1)}), bf16[8,416,512]{2,1,0:T(8,128)(2,1)S(1)}, u32[]{:S(2)}, u32[]{:S(2)}) %all-to-all-start.3) | async-done | bytes 3407904 | tf_op jit(solution)/shard_map/all_to_all | solution.py:789
  232.6 4.5 %all-to-all-start.4 = ((bf16[8,192,512]{2,1,0:T(8,128)(2,1)}), bf16[8,192,512]{2,1,0:T(8,128)(2,1)}, u32[]{:S(2)}, u32[]{:S(2)}) async-start(bf16[8,192,512]{2,1,0:T(8,128)(2,1)} %get-tuple-element.97), calls=%async_computation.4 | async-start | bytes 3145728 | tf_op jit(solution)/shard_map/all_to_all | solution.py:789
  237.2 4.4 %broadcast_select_fusion = (bf16[1040,512]{1,0:T(8,128)(2,1)}, bf16[1040,512]{1,0:T(8,128)(2,1)}, bf16[1040,512]{1,0:T(8,128)(2,1)}) fusion(pred[]{:T(512)S(6)} %lt.23, bf16[2,1040,512]{2,1,0:T(8,128)(2,1)} %collective-permute-done.11, bf16[2,1040,512]{2,1,0:T(8,128)(2,1)} %get-tuple-element.99), kind=kLoop, calls=%fused_computation.12 | loop fusion | flops 4792320 | bytes 7454721 | tf_op jit(solution)/shard_map/jit(_where)/select_n | solution.py:833
  241.5 18.0 %all-to-all-done.4.ret_b = bf16[8,192,512]{2,1,0:T(8,128)(2,1)} async-done(((bf16[8,192,512]{2,1,0:T(8,128)(2,1)}), bf16[8,192,512]{2,1,0:T(8,128)(2,1)}, u32[]{:S(2)}, u32[]{:S(2)}) %all-to-all-start.4) | async-done | bytes 1572896 | tf_op jit(solution)/shard_map/all_to_all | solution.py:789
  259.6 4.3 %all-to-all-start.5 = ((bf16[8,192,512]{2,1,0:T(8,128)(2,1)}), bf16[8,192,512]{2,1,0:T(8,128)(2,1)}, u32[]{:S(2)}, u32[]{:S(2)}) async-start(bf16[8,192,512]{2,1,0:T(8,128)(2,1)} %get-tuple-element.104), calls=%async_computation.5 | async-start | bytes 3145728 | tf_op jit(solution)/shard_map/all_to_all | solution.py:789
  263.9 1.9 collective-permute-start.12
  265.8 1.8 collective-permute-start.13
  267.6 51.5 %attention_backward.1 = (f32[1600,512]{1,0:T(8,128)}, bf16[512,2176]{1,0:T(8,128)(2,1)}) custom-call(bf16[1600,512]{1,0:T(8,128)(2,1)} %x.3, s32[8,1,200]{2,1,0:T(1,128)} %reshape.91.mask, bf16[512,2176]{1,0:T(8,128)(2,1)} %pad_maximum_fusion.small.wqkv.wout.refs_3_.refs_2_, bf16[512,2176]{1,0:T(8,128)(2,1)} %pad_maximum_fusion.small.wqkv.wout.refs_3_.refs_2_, ...), custom_call_target="tpu_custom_call" | custom-call | flops 500000000 | bytes 500000 | tf_op jit(solution)/shard_map/attention_backward/pallas_call | solution.py:634
  319.0 19.0 %collective-permute-done.12 = bf16[1040,512]{1,0:T(8,128)(2,1)S(1)} collective-permute-done((bf16[1040,512]{1,0:T(8,128)(2,1)}, bf16[1040,512]{1,0:T(8,128)(2,1)S(1)}, u32[]{:S(2)}, u32[]{:S(2)}) %collective-permute-start.12) | collective-permute-done | bytes 1064992 | tf_op jit(solution)/shard_map/ppermute | solution.py:776
  338.0 2.1 broadcast_select_fusion.5
  340.2 0.5 collective-permute-start.14
  340.7 1.4 collective-permute-done.15
  342.1 0.8 collective-permute-done.14
  342.9 0.4 select_convert_fusion
  343.4 20.1 %collective-permute-start.16 = (bf16[128,2176]{1,0:T(8,128)(2,1)S(1)}, bf16[128,2176]{1,0:T(8,128)(2,1)S(1)}, u32[]{:S(2)}, u32[]{:S(2)}) collective-permute-start(bf16[128,2176]{1,0:T(8,128)(2,1)S(1)} %select_convert_fusion), channel_id=1, source_target_pairs={{0,2},{1,3},{2,0},{3,1},{4,6},{5,7},{6,4},{7,5},{8,10},{9,11},{10,... | collective-permute-start | bytes 1671176 | tf_op jit(solution)/shard_map/ppermute | solution.py:776
  363.4 12.9 %collective-permute-done.16 = bf16[128,2176]{1,0:T(8,128)(2,1)S(1)} collective-permute-done((bf16[128,2176]{1,0:T(8,128)(2,1)S(1)}, bf16[128,2176]{1,0:T(8,128)(2,1)S(1)}, u32[]{:S(2)}, u32[]{:S(2)}) %collective-permute-start.16) | collective-permute-done | bytes 557088 | tf_op jit(solution)/shard_map/ppermute | solution.py:776
  376.4 1.3 add_convert_fusion.2
  377.7 4.6 %all-to-all-start.6 = ((bf16[8,16,2176]{2,1,0:T(8,128)(2,1)}), bf16[8,16,2176]{2,1,0:T(8,128)(2,1)S(1)}, u32[]{:S(2)}, u32[]{:S(2)}) async-start(bf16[8,16,2176]{2,1,0:T(8,128)(2,1)} %bitcast.25), calls=%async_computation.6 | async-start | bytes 1114112 | tf_op jit(solution)/shard_map/all_to_all | solution.py:863
  382.3 15.0 %all-to-all-done.6 = bf16[8,16,2176]{2,1,0:T(8,128)(2,1)S(1)} async-done(((bf16[8,16,2176]{2,1,0:T(8,128)(2,1)}), bf16[8,16,2176]{2,1,0:T(8,128)(2,1)S(1)}, u32[]{:S(2)}, u32[]{:S(2)}) %all-to-all-start.6) | async-done | bytes 557088 | tf_op jit(solution)/shard_map/all_to_all | solution.py:863
  397.3 0.8 broadcast_in_dim.34
  398.2 4.2 all-to-all-start.7
  402.4 1.7 convert_add_fusion
  404.0 9.7 %combine.1 = bf16[1600,512]{1,0:T(8,128)(2,1)} custom-call(s32[1600,2]{1,0:T(8,128)} %get-tuple-element.63.slot, f32[1600,512]{1,0:T(8,128)} %get-tuple-element.71.residual, bf16[8,2,208,512]{3,2,1,0:T(8,128)(2,1)} %bitcast.42, bf16[8,192,512]{2,1,0:T(8,128)(2,1)} %all-to-all-done.5.ret_b), custom_call_target="tpu_custom_call" | custom-call | flops 100000000 | bytes 100000 | tf_op jit(solution)/shard_map/combine/pallas_call | solution.py:683
  413.7 0.6 fusion.4
  414.3 0.5 constant_dynamic-slice_fusion
  414.8 1.5 slice_bitcast_fusion
  416.3 1.0 all-to-all-done.7
  417.3 1.1 bitcast_convert_fusion
  418.4 0.8 slice_reduce_fusion
  419.2 0.7 slice.122
  419.9 1.0 slice.121
  420.9 0.7 copy.36
  (46 shorter events, 1.0 us)
Async XLA Ops:
  4.7 32.3 %copy-start.6 = (bf16[128,2176]{1,0:T(8,128)(2,1)S(1)}, bf16[128,2176]{1,0:T(8,128)(2,1)}, u32[]{:S(2)}) copy-start(bf16[128,2176]{1,0:T(8,128)(2,1)} %get-tuple-element.64) | copy-start | bytes 1671172
  4.7 15.8 %collective-permute-start = (bf16[128,2176]{1,0:T(8,128)(2,1)}, bf16[128,2176]{1,0:T(8,128)(2,1)S(1)}, u32[]{:S(2)}, u32[]{:S(2)}) collective-permute-start(bf16[128,2176]{1,0:T(8,128)(2,1)} %get-tuple-element.64), channel_id=1, source_target_pairs={{0,2},{1,3},{2,0},{3,1},{4,6},{5,7},{6,4},{7,5},{8,10},{9,11},{10,... | collective-permute-start | bytes 1671176 | tf_op jit(solution)/shard_map/ppermute | solution.py:776
  7.7 29.4 %collective-permute-start.1 = (bf16[128,2176]{1,0:T(8,128)(2,1)}, bf16[128,2176]{1,0:T(8,128)(2,1)S(1)}, u32[]{:S(2)}, u32[]{:S(2)}) collective-permute-start(bf16[128,2176]{1,0:T(8,128)(2,1)} %get-tuple-element.64), channel_id=1, source_target_pairs={{0,1},{1,0},{2,3},{3,2},{4,5},{5,4},{6,7},{7,6},{8,9},{9,8},{10,11... | collective-permute-start | bytes 1671176 | tf_op jit(solution)/shard_map/ppermute | solution.py:776
  20.6 16.5 %collective-permute-start.2 = (bf16[128,2176]{1,0:T(8,128)(2,1)S(1)}, bf16[128,2176]{1,0:T(8,128)(2,1)S(1)}, u32[]{:S(2)}, u32[]{:S(2)}) collective-permute-start(bf16[128,2176]{1,0:T(8,128)(2,1)S(1)} %collective-permute-done), channel_id=1, source_target_pairs={{0,1},{1,0},{2,3},{3,2},{4,5},{5,4},{6,7},{7,6},{8,9},{9,8},{10,11... | collective-permute-start | bytes 1671176 | tf_op jit(solution)/shard_map/ppermute | solution.py:776
  20.6 18.3 %collective-permute-start.4 = (bf16[512,512]{1,0:T(8,128)(2,1)}, bf16[512,512]{1,0:T(8,128)(2,1)S(1)}, u32[]{:S(2)}, u32[]{:S(2)}) collective-permute-start(bf16[512,512]{1,0:T(8,128)(2,1)} %get-tuple-element.69), channel_id=1, source_target_pairs={{2,18},{3,19},{6,22},{7,23},{10,26},{11,27},{14,30},{15,31},{18,2}... | collective-permute-start | bytes 1572872 | tf_op jit(solution)/shard_map/ppermute | solution.py:776
  21.3 18.2 %collective-permute-start.3 = (bf16[512,512]{1,0:T(8,128)(2,1)}, bf16[512,512]{1,0:T(8,128)(2,1)}, u32[]{:S(2)}, u32[]{:S(2)}) collective-permute-start(bf16[512,512]{1,0:T(8,128)(2,1)} %get-tuple-element.69), channel_id=1, source_target_pairs={{0,18},{1,19},{2,0},{3,1},{4,22},{5,23},{6,4},{7,5},{8,26},{9,27},... | collective-permute-start | bytes 1572872 | tf_op jit(solution)/shard_map/ppermute | solution.py:776
  38.8 17.6 %copy-start.9 = (bf16[528,512]{1,0:T(8,128)(2,1)S(1)}, bf16[528,512]{1,0:T(8,128)(2,1)}, u32[]{:S(2)}) copy-start(bf16[528,512]{1,0:T(8,128)(2,1)} %get-tuple-element.76) | copy-start | bytes 1622020
  38.8 23.9 %copy-start.11 = (s32[8,200]{1,0:T(8,128)S(1)}, s32[8,200]{1,0:T(8,128)}, u32[]{:S(2)}) copy-start(s32[8,200]{1,0:T(8,128)} %param.18) | copy-start | bytes 19204
  38.8 17.6 %copy-start.10 = (bf16[512,512]{1,0:T(8,128)(2,1)}, bf16[512,512]{1,0:T(8,128)(2,1)S(1)}, u32[]{:S(2)}) copy-start(bf16[512,512]{1,0:T(8,128)(2,1)S(1)} %collective-permute-done.4) | copy-start | bytes 1572868
  39.4 52.9 %all-to-all-start = ((bf16[8,224,512]{2,1,0:T(8,128)(2,1)}), bf16[8,224,512]{2,1,0:T(8,128)(2,1)S(1)}, u32[]{:S(2)}, u32[]{:S(2)}) async-start(bf16[8,224,512]{2,1,0:T(8,128)(2,1)} %get-tuple-element.75), calls=%async_computation | async-start | bytes 3670016 | tf_op jit(solution)/shard_map/all_to_all | solution.py:789
  56.4 34.2 %collective-permute-start.6 = (bf16[528,512]{1,0:T(8,128)(2,1)S(1)}, bf16[528,512]{1,0:T(8,128)(2,1)S(1)}, u32[]{:S(2)}, u32[]{:S(2)}) collective-permute-start(bf16[528,512]{1,0:T(8,128)(2,1)S(1)} %copy-done.9), channel_id=1, source_target_pairs={{2,18},{3,19},{6,22},{7,23},{10,26},{11,27},{14,30},{15,31},{18,2}... | collective-permute-start | bytes 1622024 | tf_op jit(solution)/shard_map/ppermute | solution.py:776
  57.1 35.1 %collective-permute-start.5 = (bf16[528,512]{1,0:T(8,128)(2,1)S(1)}, bf16[528,512]{1,0:T(8,128)(2,1)}, u32[]{:S(2)}, u32[]{:S(2)}) collective-permute-start(bf16[528,512]{1,0:T(8,128)(2,1)S(1)} %copy-done.9), channel_id=1, source_target_pairs={{0,18},{1,19},{2,0},{3,1},{4,22},{5,23},{6,4},{7,5},{8,26},{9,27},... | collective-permute-start | bytes 1622024 | tf_op jit(solution)/shard_map/ppermute | solution.py:776
  92.3 27.9 %copy-start.3 = (bf16[8,224,512]{2,1,0:T(8,128)(2,1)}, bf16[8,224,512]{2,1,0:T(8,128)(2,1)S(1)}, u32[]{:S(2)}) copy-start(bf16[8,224,512]{2,1,0:T(8,128)(2,1)S(1)} %all-to-all-done.refs_1_) | copy-start | bytes 5505028
  120.2 59.8 %all-to-all-start.2 = ((bf16[8,400,512]{2,1,0:T(8,128)(2,1)}), bf16[8,400,512]{2,1,0:T(8,128)(2,1)}, u32[]{:S(2)}, u32[]{:S(2)}) async-start(bf16[8,400,512]{2,1,0:T(8,128)(2,1)} %get-tuple-element.86), calls=%async_computation.2 | async-start | bytes 6553600 | tf_op jit(solution)/shard_map/all_to_all | solution.py:789
  126.2 2.8 collective-permute-start.7
  126.2 2.8 collective-permute-start.8
  127.9 3.9 collective-permute-start.9
  128.0 3.8 collective-permute-start.10
  131.8 0.8 copy-start.7
  131.8 1.0 copy-start.8
  134.2 1.4 copy-start
  180.0 52.7 %all-to-all-start.3 = ((bf16[8,416,512]{2,1,0:T(8,128)(2,1)}), bf16[8,416,512]{2,1,0:T(8,128)(2,1)S(1)}, u32[]{:S(2)}, u32[]{:S(2)}) async-start(bf16[8,416,512]{2,1,0:T(8,128)(2,1)} %get-tuple-element.92), calls=%async_computation.3 | async-start | bytes 6815744 | tf_op jit(solution)/shard_map/all_to_all | solution.py:789
  227.2 10.0 %collective-permute-start.11 = (bf16[2,1040,512]{2,1,0:T(8,128)(2,1)}, bf16[2,1040,512]{2,1,0:T(8,128)(2,1)}, u32[]{:S(2)}, u32[]{:S(2)}) collective-permute-start(bf16[2,1040,512]{2,1,0:T(8,128)(2,1)} %get-tuple-element.100), channel_id=1, source_target_pairs={{0,1},{1,0},{2,3},{3,2},{4,5},{5,4},{6,7},{7,6},{8,9},{9,8},{10,11... | collective-permute-start | bytes 6389768 | tf_op jit(solution)/shard_map/ppermute | solution.py:776
  232.6 8.9 %copy-start.1 = (bf16[8,416,512]{2,1,0:T(8,128)(2,1)}, bf16[8,416,512]{2,1,0:T(8,128)(2,1)S(1)}, u32[]{:S(2)}) copy-start(bf16[8,416,512]{2,1,0:T(8,128)(2,1)S(1)} %all-to-all-done.3) | copy-start | bytes 10223620
  232.6 26.9 %all-to-all-start.4 = ((bf16[8,192,512]{2,1,0:T(8,128)(2,1)}), bf16[8,192,512]{2,1,0:T(8,128)(2,1)}, u32[]{:S(2)}, u32[]{:S(2)}) async-start(bf16[8,192,512]{2,1,0:T(8,128)(2,1)} %get-tuple-element.97), calls=%async_computation.4 | async-start | bytes 3145728 | tf_op jit(solution)/shard_map/all_to_all | solution.py:789
  259.6 78.5 %all-to-all-start.5 = ((bf16[8,192,512]{2,1,0:T(8,128)(2,1)}), bf16[8,192,512]{2,1,0:T(8,128)(2,1)}, u32[]{:S(2)}, u32[]{:S(2)}) async-start(bf16[8,192,512]{2,1,0:T(8,128)(2,1)} %get-tuple-element.104), calls=%async_computation.5 | async-start | bytes 3145728 | tf_op jit(solution)/shard_map/all_to_all | solution.py:789
  263.9 74.2 %collective-permute-start.12 = (bf16[1040,512]{1,0:T(8,128)(2,1)}, bf16[1040,512]{1,0:T(8,128)(2,1)S(1)}, u32[]{:S(2)}, u32[]{:S(2)}) collective-permute-start(bf16[1040,512]{1,0:T(8,128)(2,1)} %get-tuple-element.105), channel_id=1, source_target_pairs={{18,0},{19,1},{0,2},{1,3},{22,4},{23,5},{4,6},{5,7},{26,8},{27,9},... | collective-permute-start | bytes 3194888 | tf_op jit(solution)/shard_map/ppermute | solution.py:776
  265.8 72.2 %collective-permute-start.13 = (bf16[1040,512]{1,0:T(8,128)(2,1)}, bf16[1040,512]{1,0:T(8,128)(2,1)}, u32[]{:S(2)}, u32[]{:S(2)}) collective-permute-start(bf16[1040,512]{1,0:T(8,128)(2,1)} %get-tuple-element.106), channel_id=1, source_target_pairs={{2,18},{3,19},{6,22},{7,23},{10,26},{11,27},{14,30},{15,31},{18,2}... | collective-permute-start | bytes 3194888 | tf_op jit(solution)/shard_map/ppermute | solution.py:776
  319.0 23.9 %copy-start.2 = (bf16[512,2176]{1,0:T(8,128)(2,1)S(1)}, bf16[512,2176]{1,0:T(8,128)(2,1)}, u32[]{:S(2)}) copy-start(bf16[512,2176]{1,0:T(8,128)(2,1)} %get-tuple-element.109) | copy-start | bytes 6684676
  338.0 5.3 %copy-start.5 = (bf16[1040,512]{1,0:T(8,128)(2,1)}, bf16[1040,512]{1,0:T(8,128)(2,1)S(1)}, u32[]{:S(2)}) copy-start(bf16[1040,512]{1,0:T(8,128)(2,1)S(1)} %collective-permute-done.12) | copy-start | bytes 3194884
  340.1 2.0 collective-permute-start.15
  340.2 2.7 collective-permute-start.14
  343.4 33.0 %collective-permute-start.16 = (bf16[128,2176]{1,0:T(8,128)(2,1)S(1)}, bf16[128,2176]{1,0:T(8,128)(2,1)S(1)}, u32[]{:S(2)}, u32[]{:S(2)}) collective-permute-start(bf16[128,2176]{1,0:T(8,128)(2,1)S(1)} %select_convert_fusion), channel_id=1, source_target_pairs={{0,2},{1,3},{2,0},{3,1},{4,6},{5,7},{6,4},{7,5},{8,10},{9,11},{10,... | collective-permute-start | bytes 1671176 | tf_op jit(solution)/shard_map/ppermute | solution.py:776
  377.7 24.7 %copy-start.4 = (bf16[1040,512]{1,0:T(8,128)(2,1)S(1)}, bf16[1040,512]{1,0:T(8,128)(2,1)}, u32[]{:S(2)}) copy-start(bf16[1040,512]{1,0:T(8,128)(2,1)} %get-tuple-element.110) | copy-start | bytes 3194884
  377.7 19.6 %all-to-all-start.6 = ((bf16[8,16,2176]{2,1,0:T(8,128)(2,1)}), bf16[8,16,2176]{2,1,0:T(8,128)(2,1)S(1)}, u32[]{:S(2)}, u32[]{:S(2)}) async-start(bf16[8,16,2176]{2,1,0:T(8,128)(2,1)} %bitcast.25), calls=%async_computation.6 | async-start | bytes 1114112 | tf_op jit(solution)/shard_map/all_to_all | solution.py:863
  398.2 19.1 %all-to-all-start.7 = ((bf16[8,16,2176]{2,1,0:T(8,128)(2,1)}), bf16[8,16,2176]{2,1,0:T(8,128)(2,1)}, u32[]{:S(2)}, u32[]{:S(2)}) async-start(bf16[8,16,2176]{2,1,0:T(8,128)(2,1)} %broadcast_in_dim.34), calls=%async_computation.7 | async-start | bytes 1114112 | tf_op jit(solution)/shard_map/all_to_all | solution.py:863

commit v3 on v2

--- a/solution.py
+++ b/solution.py
@@ -102,36 +102,46 @@
 EXTRA = 16
 
 
-def pack_kernel(wqkv, wout, router, ga, sa, gm, sm, w_in, w_out, b_in, b_out, dense, first, second, tail):
+def pack_kernel(wqkv, wout, router, ga, sa, gm, sm, w_in, w_out, b_in, b_out, dense, *refs):
+    *pieces, tail = refs
     width = wout.shape[1]
-    experts = router.shape[1]
+    experts = router.shape[0]
     share = wout.shape[0]
     hidden = w_in.shape[0]
     dense[:, : 3 * width] = wqkv[...]
     dense[:, 3 * width : 4 * width] = wout[...]
     tail[...] = jnp.zeros_like(tail)
+    tail[0:experts, 0:share] = router[...].astype(F32)
     for k, row in enumerate((ga, sa, gm, sm)):
         tail[experts + k : experts + k + 1, 0:share] = row[...].astype(F32)
     columns = jnp.transpose(tail[0:LANES, 0:LANES])[:share, :]
     dense[:, 4 * width :] = columns.astype(BF16)
-    dense[:, 4 * width : 4 * width + experts] = router[...]
-    first[...] = w_in[...]
-    second[0:hidden, :] = w_out[...]
+    sources = ((w_in, 0), (w_out, hidden))
+    start = 0
+    for piece in pieces:
+        stop = start + piece.shape[0]
+        for source, base in sources:
+            low, high = max(start, base), min(stop, base + hidden)
+            if low < high:
+                piece[low - start : high - start, :] = source[low - base : high - base, :]
+        start = stop
     tail[0:EXTRA, :] = jnp.zeros((EXTRA, width), F32)
     tail[0:1, 0:hidden] = b_in[...].astype(F32)
     tail[1:2, 0:share] = b_out[...].astype(F32)
-    second[hidden:, :] = tail[0:EXTRA, :].astype(BF16)
+    pieces[-1][pieces[-1].shape[0] - EXTRA :, :] = tail[0:EXTRA, :].astype(BF16)
 
 
 def pack(wqkv, wout, router, gains, w_in, w_out, b_in, b_out):
     share, width = wout.shape
     hidden = w_in.shape[0]
+    double = 2 * hidden + EXTRA
+    cuts = [0] + [double * part // 100 // EXTRA * EXTRA for part in (50,)] + [double]
+    sizes = [high - low for low, high in zip(cuts, cuts[1:])]
     return pl.pallas_call(
         pack_kernel,
         out_shape=[
             jax.ShapeDtypeStruct((share, 4 * width + LANES), BF16),
-            jax.ShapeDtypeStruct((hidden, width), BF16),
-            jax.ShapeDtypeStruct((hidden + EXTRA, width), BF16),
+            *[jax.ShapeDtypeStruct((n, width), BF16) for n in sizes],
         ],
         scratch_shapes=[pltpu.VMEM((LANES, width), F32)],
         compiler_params=params(),
@@ -213,15 +223,13 @@
     )(priority, route_rows, capacity[None, :])
 
 
-def dispatch_kernel(parts, with_other, slot_rows, route_rows, rows, *outs):
+def dispatch_kernel(pieces, with_other, has_carry, slot_rows, route_rows, rows, *outs):
     e = pl.program_id(0)
-    if not with_other:
+    if has_carry:
         carry, *outs = outs
-        outs[-1][0, parts[-1] :, :] = carry[0]
-    start = 0
-    for size, out in zip(parts, outs):
+        outs[-1][0, pieces[-1][1] :, :] = carry[0]
+    for (start, size), out in zip(pieces, outs):
         place = lax.broadcasted_iota(jnp.int32, (size, 1), 0) + (start + e * size)
-        start += pl.num_programs(0) * size
         hit_a = slot_rows[0:1, :] == place
         hit_b = slot_rows[1:2, :] == place
         pick = jnp.where(hit_a | hit_b, 1.0, 0.0).astype(BF16)
@@ -234,18 +242,16 @@
             out[0, size : size + EXTRA, 0:size] = turned[0:EXTRA, :].astype(BF16)
 
 
-def dispatch(slot_rows, route_rows, rows, experts, parts, carry=None):
+def dispatch(slot_rows, route_rows, rows, experts, pieces, with_other, carry=None):
     total, width = rows.shape
-    with_other = carry is None
-    if with_other:
-        tall = [size + EXTRA for size in parts]
-        extra, extra_spec = (), ()
-    else:
-        tall = [parts[0], parts[1] + carry.shape[1]]
+    tall = [size + (EXTRA if with_other else 0) for _, size in pieces]
+    extra, extra_spec = (), ()
+    if carry is not None:
+        tall[-1] += carry.shape[1]
         extra = (carry,)
         extra_spec = (pl.BlockSpec((1,) + carry.shape[1:], lambda e: (e, 0, 0)),)
     return pl.pallas_call(
-        partial(dispatch_kernel, parts, with_other),
+        partial(dispatch_kernel, pieces, with_other, carry is not None),
         grid=(experts,),
         in_specs=[whole((2, total)), whole((2, total)), whole((total, width)), *extra_spec],
         out_specs=[pl.BlockSpec((1, t, width), lambda e: (e, 0, 0)) for t in tall],
@@ -254,6 +260,10 @@
         name="dispatch",
         cost_estimate=cost(10),
     )(slot_rows, route_rows, rows, *extra)
+
+
+def stack_rows(length, width):
+    return LANES * HEADS // width * ((length + 15) // 16 * 16)
 
 
 def attention_kernel(
@@ -399,7 +409,7 @@
             return acc + jnp.sum(scaled.astype(F32), axis=0, keepdims=True)
 
         db[...] = jnp.zeros_like(db)
-        db[1:2, :] = lax.fori_loop(0, steps, step, jnp.zeros((1, width), F32))
+        db[1:2, :] = lax.fori_loop(0, steps, step, jnp.zeros((1, width), F32), unroll=4)
 
     chunk = w_in.shape[1]
     hidden_share = (dw_mine.shape[1] - EXTRA) // 2
@@ -489,23 +499,23 @@
             hid[at, 0:LANES] = spread
             return carry
 
-        lax.fori_loop(0, steps, step, 0)
+        lax.fori_loop(0, steps, step, 0, unroll=4)
         drouter[...] = mm_tn(rows[...], hid[:, 0:LANES]) + (0.0 if old is None else old[2][...])
 
 
 def run_experts(given, block, own, dense, weights, b_out, old):
     experts, _, width = given[0].shape
     total = experts * block
-    first, second = weights
-    quarters, share, _ = first.shape
+    quarters, double, _ = weights.shape
+    share = (double - EXTRA) // 2
     chunk = min(share, 512)
     per = share // chunk
     half = quarters // 2
     at = lambda f: (f // per, f % per, 0)
-    bias_at = lambda f: (f // per, share // EXTRA, 0)
+    out_at = lambda f: (f // per, per + f % per, 0)
+    bias_at = lambda f: (f // per, 2 * share // EXTRA, 0)
     mine_at = lambda f: (jnp.minimum(f // per, half - 1), 0, 0)
     mate_at = lambda f: (jnp.maximum(f // per - half, 0), 0, 0)
-    double = 2 * share + EXTRA
     steps = quarters * per
     dw_shape = jax.ShapeDtypeStruct((half, double, width), BF16)
     sums = [
@@ -530,7 +540,7 @@
             whole((1, LANES)),
             small_spec(width),
             pl.BlockSpec((1, chunk, width), at),
-            pl.BlockSpec((1, chunk, width), at),
+            pl.BlockSpec((1, chunk, width), out_at),
             pl.BlockSpec((1, EXTRA, width), bias_at),
             whole((1, width)),
         ]
@@ -552,13 +562,13 @@
         compiler_params=params(1),
         name="experts",
         cost_estimate=cost(50),
-    )(*given, own, dense, first, second, second, b_out, *old)
+    )(*given, own, dense, weights, weights, weights, b_out, *old)
 
 
 def backward_kernel(
     experts, x, mask, small, wqkv, wout, triple, context, logs, residual, up, slot, ret_a, ret_b, drouter,
     input_grad, packed,
-    tg, gains, dqkv, dwout, dgains,
+    tg, gains, dqkv, dwout, dgains, stack_k, stack_v, dq_t,
 ):
     step = pl.program_id(0)
     length, width = x.shape
@@ -569,6 +579,8 @@
         dwout[...] = jnp.zeros_like(dwout)
         dgains[...] = jnp.zeros_like(dgains)
         gains[0:4, :] = gain_rows(small, experts)
+        stack_k[...] = jnp.zeros_like(stack_k)
+        stack_v[...] = jnp.zeros_like(stack_v)
 
     second_grad = gather_slots(slot, (ret_a, ret_b))
     unit_b, scale_b = norm_stats(residual[...])
@@ -583,33 +595,45 @@
     head_width = width // HEADS
     scale = head_width ** (-0.5)
     per = LANES // head_width
+    tall = stack_k.shape[0] // per
     hide_row = jnp.where(mask[0] > 0, 0.0, NEGATIVE)
     hide = jnp.transpose(jnp.broadcast_to(hide_row, (LANES, length)))[:, 0:1]
+    hide = jnp.concatenate([hide, jnp.full((tall - length, 1), NEGATIVE, F32)], axis=0)
     for group in range(HEADS // per):
         begin = group * LANES
-        queries = triple[:, begin : begin + LANES]
+        queries = triple[:, begin : begin + LANES] * jnp.asarray(scale, BF16)
         keys = triple[:, width + begin : width + begin + LANES]
         values = triple[:, 2 * width + begin : 2 * width + begin + LANES]
         pulled = context_grad[:, begin : begin + LANES]
-        dq = jnp.zeros((length, LANES), F32)
-        dk = jnp.zeros((length, LANES), F32)
-        dv = jnp.zeros((length, LANES), F32)
         for inner in range(per):
+            inside = (lane >= inner * head_width) & (lane < (inner + 1) * head_width)
+            only = jnp.where(inside, 1.0, 0.0).astype(BF16)
+            stack_k[inner * tall : inner * tall + length, :] = keys * only
+            stack_v[inner * tall : inner * tall + length, :] = values * only
+        scores = mm_nt(stack_k[...], queries)
+        prob_grad = mm_nt(stack_v[...], pulled)
+        probs, score_grad = [], []
+        for inner in range(per):
+            rows = slice(inner * tall, (inner + 1) * tall)
             head = group * per + inner
-            inside = (lane >= inner * head_width) & (lane < (inner + 1) * head_width)
-            chosen = queries * jnp.where(inside, scale, 0.0).astype(BF16)
-            log_row = logs[0, head : head + 1, :]
-            probs = jnp.exp(mm_nt(keys, chosen) + hide - log_row)
-            picked = pulled * jnp.where(inside, 1.0, 0.0).astype(BF16)
-            prob_grad = mm_nt(values, picked)
-            inner_sum = jnp.sum(probs * prob_grad, axis=0, keepdims=True)
-            score_grad = (probs * (prob_grad - inner_sum)).astype(BF16)
-            dq = jnp.where(inside, mm_tn(score_grad, keys), dq)
-            dk = jnp.where(inside, mm(score_grad, queries), dk)
-            dv = jnp.where(inside, mm(probs.astype(BF16), pulled), dv)
-        tg[:, begin : begin + LANES] = (dq * scale).astype(BF16)
-        tg[:, width + begin : width + begin + LANES] = (dk * scale).astype(BF16)
+            prob = jnp.exp(scores[rows, :] + (hide - logs[0, head : head + 1, :]))
+            pull = prob_grad[rows, :]
+            inner_sum = jnp.sum(prob * pull, axis=0, keepdims=True)
+            probs.append(prob.astype(BF16))
+            score_grad.append((prob * (pull - inner_sum)).astype(BF16))
+        probs = jnp.concatenate(probs, axis=0)
+        score_grad = jnp.concatenate(score_grad, axis=0)
+        dk_all = mm(score_grad, queries)
+        dv_all = mm(probs, pulled)
+        dq_t[begin : begin + LANES, :] = mm(jnp.transpose(stack_k[...]), score_grad) * scale
+        dk, dv = dk_all[0:length, :], dv_all[0:length, :]
+        for inner in range(1, per):
+            rows = slice(inner * tall, inner * tall + length)
+            dk = jnp.where(lane >= inner * head_width, dk_all[rows, :], dk)
+            dv = jnp.where(lane >= inner * head_width, dv_all[rows, :], dv)
+        tg[:, width + begin : width + begin + LANES] = dk.astype(BF16)
         tg[:, 2 * width + begin : 2 * width + begin + LANES] = dv.astype(BF16)
+    tg[:, 0:width] = jnp.transpose(dq_t[...]).astype(BF16)
     unit, scale_a = norm_stats(x[...].astype(F32))
     low = (unit * gains[0:1, :] + gains[1:2, :]).astype(BF16)
     dqkv[...] += mm_tn(low, tg[...])
@@ -663,6 +687,9 @@
             pltpu.VMEM((width, 3 * width), F32),
             pltpu.VMEM((width, width), F32),
             pltpu.VMEM((LANES, width), F32),
+            pltpu.VMEM((stack_rows(length, width), LANES), BF16),
+            pltpu.VMEM((stack_rows(length, width), LANES), BF16),
+            pltpu.VMEM((width, length), F32),
         ],
         compiler_params=params(1),
         name="attention_backward",
@@ -754,11 +781,11 @@
         flat = self.flat
         self.cross = [(flat(*p), flat(p[0], p[1], 1 - p[2], p[3])) for p in places]
         self.core = [(flat(*p), flat(p[0], p[1], p[2], 1 - p[3])) for p in places]
-        swap = lambda p: (p[0] ^ 2, p[1], 1, p[3]) if p[2] == 0 else (p[0], p[1], 0, p[3])
-        self.first = [(flat(*p), flat(*swap(p))) for p in places]
-        self.second = [
-            (flat(*p), flat(p[0] ^ 2, p[1], 1, p[3])) for p in places if p[2] == 1
-        ]
+        near = lambda p: p[2] == p[0] % 2
+        away = lambda p: (p[0] ^ 2, p[1], 1 - p[0] % 2, p[3])
+        home = lambda p: (p[0], p[1], p[0] % 2, p[3])
+        self.first = [(flat(*p), flat(*(away(p) if near(p) else home(p)))) for p in places]
+        self.second = [(flat(*p), flat(*away(p))) for p in places if not near(p)]
         self.groups = [
             [self.host(half, e, c) for e in range(seq)] for half in range(2) for c in range(2)
         ]
@@ -769,8 +796,8 @@
     def host(self, half, expert, c):
         z, y = expert // 2, expert % 2
         if z // 2 == half:
-            return self.flat(z, y, 0, c)
-        return self.flat(z ^ 2, y, 1, c)
+            return self.flat(z, y, z % 2, c)
+        return self.flat(z ^ 2, y, 1 - z % 2, c)
 
     def send(self, a, pairs):
         return lax.ppermute(a, self.AXES, pairs)
@@ -778,12 +805,18 @@
     def x_zero(self):
         return lax.axis_index("wt") < 2
 
+    def odd_level(self):
+        return lax.axis_index("seq") // 2 % 2 == 1
+
+    def near(self):
+        return self.x_zero() != self.odd_level()
+
     def core_zero(self):
         return lax.axis_index("wt") % 2 == 0
 
     def own_id(self):
         rank = lax.axis_index("seq")
-        return jnp.where(self.x_zero(), rank, rank ^ 4)
+        return jnp.where(self.near(), rank, rank ^ 4)
 
     def exchange(self, a):
         return lax.all_to_all(
@@ -815,22 +848,32 @@
 
     def fetch(self, packed, begun):
         got, got_b = begun
-        flip = self.x_zero()
+        flip = self.near()
         low = jnp.where(flip, packed, got)
         high = jnp.where(flip, got, got_b)
         return jnp.stack([low, high, self.send(low, self.core), self.send(high, self.core)])
 
     def spread_out_bias(self, quarters):
-        a, b, c, d = (quarters[i] for i in range(4))
-        return jnp.where(
-            self.core_zero(), jnp.stack([a, c, b, d]), jnp.stack([c, a, d, b])
-        )
+        mine, odd = self.core_zero(), self.odd_level()
+        order = []
+        for x in range(2):
+            for c in range(2):
+                same = mine == (c == 0)
+                level = odd == (x == 1)
+                order.append(
+                    jnp.where(
+                        same,
+                        jnp.where(level, quarters[0], quarters[1]),
+                        jnp.where(level, quarters[2], quarters[3]),
+                    )
+                )
+        return jnp.stack(order)
 
     def begin_reduce(self, mine, mate):
         got = self.send(mate, self.core)
         low = (mine[0].astype(F32) + got[0].astype(F32)).astype(BF16)
         high = (mine[1].astype(F32) + got[1].astype(F32)).astype(BF16)
-        return low, high, jnp.where(self.x_zero(), high, low)
+        return low, high, jnp.where(self.near(), high, low)
 
     def reduce_expert(self, parts):
         low, high, give = parts
@@ -838,7 +881,7 @@
 
     def finish_expert(self, parts, received):
         far, far_b = received
-        return jnp.where(self.x_zero(), parts[0], far_b).astype(F32) + far.astype(F32)
+        return jnp.where(self.near(), parts[0], far_b).astype(F32) + far.astype(F32)
 
     def first_back(self):
         return [(b, a) for a, b in self.first]
@@ -900,7 +943,7 @@
     front = (cap // 2 + EXTRA - 1) // EXTRA * EXTRA
     parts = (front, cap - front)
     packed, *shards = pack(
-        query_key_value, attention_out, router_weight,
+        query_key_value, attention_out, router_weight.T,
         (attention_gain, attention_shift, mixture_gain, mixture_shift),
         expert_in[0], expert_out[0], expert_in_bias, expert_out_bias,
     )
@@ -910,20 +953,25 @@
     route_rows = routes.T
     slot, slot_rows = make_slots(route_rows, priority, capacity, parts)
     slot_rows, far = tie((slot_rows, far))
-    ups_a, ups_b = dispatch(slot_rows, route_rows, cotangent, experts, parts)
+    pieces = ((0, front), (experts * front, cap - front))
+    send = partial(dispatch, slot_rows, route_rows)
+    ups_a, ups_b = send(cotangent, experts, pieces, True)
     dense = plan.gather_dense(packed, far)
     dense, ups_a, fetched[0] = tie((dense, ups_a, fetched[0]))
     ups_a = plan.exchange(ups_a)
 
     triple, context, logs, residual, normed = attention_forward(inputs, key_mask, dense, experts)
-    rows_a, mixed_b = dispatch(slot_rows, route_rows, normed, experts, parts, ups_b)
+    (rows_a,) = send(normed, experts, pieces[:1], False)
+    (mixed_b,) = send(normed, experts, pieces[1:], False, ups_b)
     rows_a, ups_a, fetched[1] = tie((rows_a, ups_a, fetched[1]))
-    weights = [plan.fetch(*pair) for pair in zip(shards, fetched)]
+    rows_a = plan.exchange(rows_a)
+    weights = jnp.concatenate(
+        [plan.fetch(*pair) for pair in zip(shards, fetched)], axis=1
+    )
     b_out = plan.spread_out_bias(
-        weights[1][:, hidden_share + 1, :share].astype(F32)
+        weights[:, 2 * hidden_share + 1, :share].astype(F32)
     ).reshape(1, width)
-    rows_a = plan.exchange(rows_a)
-    rows_a, mixed_b = tie((rows_a, mixed_b))
+    rows_a, mixed_b, weights, b_out = tie((rows_a, mixed_b, weights, b_out))
     mixed_b = plan.exchange(mixed_b)
     ret_a, *sums = run_experts((rows_a, ups_a), parts[0], own, dense, weights, b_out, ())
     ret_a, mixed_b = tie((ret_a, mixed_b))
@@ -942,8 +990,9 @@
         inputs, key_mask, dense, triple, context, logs, residual, cotangent, slot,
         (ret_a, back_b), sums[2], experts,
     )
-    grads, sent_b, received = tie((grads, sent_b, received))
+    grads, received = tie((grads, received))
     mine = plan.begin_dense_sum(grads)
+    mine, sent_b = tie((mine, sent_b))
     shard = plan.finish_expert(halves, received)
     done = plan.reduce_dense(mine)
     block_output = combine(slot, residual, (ret_a, sent_b), 400)

time: 423 us -> 368 us (0.87)
  blocking collectives: 27.9 us -> 0 us
  waiting for transfers between devices: 80.9 us -> 63.7 us
  Pallas kernels: 196 us -> 186 us
    all_to_all x1 -> x0, blocking collectives: 27.9 us -> none  [exchange(): lax.all_to_all(a, self.AXES, split_axis=0, concat_axis=0, axis_index_grou...]
    ppermute x17, waiting for transfers between devices: 41.5 us -> 25 us  [send(): return lax.ppermute(a, self.AXES, pairs)]
    ppermute x17, starting transfers between devices: 40.8 us -> 25.6 us  [send(): return lax.ppermute(a, self.AXES, pairs)]
    all_to_all x5 -> x6, starting transfers between devices: 35.3 us -> 45.8 us  [exchange(): lax.all_to_all(a, self.AXES, split_axis=0, concat_axis=0, axis_index_grou...]
    pallas_call x1, Pallas kernels: 51.5 us -> 41.4 us  [attention_backward(): pl.pallas_call(partial(backward_kernel, experts), grid=(images,), in_spec...]
    pallas_call x2, Pallas kernels: 86.7 us -> 81.2 us  [run_experts(): pl.pallas_call(partial(experts_kernel, block, bool(old)), grid=(steps,),...]
    pallas_call x2 -> x3, Pallas kernels: 20.9 us -> 26.1 us  [dispatch(): pl.pallas_call(partial(dispatch_kernel, pieces, with_other, carry is not...]
    all_to_all x2, starting transfers between devices: 8.76 us -> 13.5 us  [reduce_dense(): lax.all_to_all(v, 'seq', split_axis=0, concat_axis=0, tiled=True)]
  transfers between devices with their start and end apart: 24 -> 25, of which waited for: 11 -> 13; matrix products, arithmetic and copies ran while one was open for 4% -> 6% of each run, Pallas kernels for 46% -> 50%
where the time goes in v3:
time: 368 us; the launch traced here: 366 us
  Pallas kernels  186 us (51%)
  starting transfers between devices  84.9 us (23%)
  waiting for transfers between devices  63.7 us (17%)
  other arithmetic  20.7 us (6%)
  local copies, waits for them, and re-layouts  10.5 us (3%)
    pallas_call x2, Pallas kernels, run_experts(): pl.pallas_call(partial(experts_kernel, block, bool(old)), grid=(steps,),...  81.2 us
    all_to_all x6, starting transfers between devices, exchange(): lax.all_to_all(a, self.AXES, split_axis=0, concat_axis=0, axis_index_grou...  45.8 us
    pallas_call x1, Pallas kernels, attention_backward(): pl.pallas_call(partial(backward_kernel, experts), grid=(images,), in_spec...  41.4 us
    pallas_call x3, Pallas kernels, dispatch(): pl.pallas_call(partial(dispatch_kernel, pieces, with_other, carry is not...  26.1 us
    ppermute x17, starting transfers between devices, send(): return lax.ppermute(a, self.AXES, pairs)  25.6 us
    ppermute x17, waiting for transfers between devices, send(): return lax.ppermute(a, self.AXES, pairs)  25 us
    all_to_all x6, waiting for transfers between devices, exchange(): lax.all_to_all(a, self.AXES, split_axis=0, concat_axis=0, axis_index_grou...  22.9 us
    pallas_call x1, Pallas kernels, attention_forward(): pl.pallas_call(partial(attention_kernel, experts), grid=(images,), in_spe...  16.8 us
  transfers between devices with their start and end apart: 25, of which 13 were waited for; matrix products, arithmetic and copies ran while one was open for 6% of the time, Pallas kernels for 50%

profile of v3, /device:TPU:0, one launch (start us, length us, event | category | flops | bytes accessed | tf_op | source)
XLA Modules:
  0.0 366.3 jit_solution(9427419182462697562)
XLA Ops:
  0.6 2.7 pack.1
  3.3 2.9 collective-permute-start
  6.3 7.9 %slots.1 = (s32[1600,2]{1,0:T(8,128)}, s32[2,1600]{1,0:T(2,128)}) custom-call(s32[1,1600]{1,0:T(1,128)} %prow.1, s32[2,1600]{1,0:T(2,128)} %bitcast.53, s32[1,8]{1,0:T(1,128)} %bitcast.64), custom_call_target="tpu_custom_call" | custom-call | flops 80000000 | bytes 80000 | tf_op jit(solution)/shard_map/slots/pallas_call | solution.py:208
  14.1 5.0 %collective-permute-done = bf16[128,2176]{1,0:T(8,128)(2,1)S(1)} collective-permute-done((bf16[128,2176]{1,0:T(8,128)(2,1)}, bf16[128,2176]{1,0:T(8,128)(2,1)S(1)}, u32[]{:S(2)}, u32[]{:S(2)}) %collective-permute-start) | collective-permute-done | bytes 557088 | tf_op jit(solution)/shard_map/ppermute | solution.py:803
  19.2 0.7 collective-permute-start.4
  19.9 5.3 %collective-permute-start.3 = (bf16[512,512]{1,0:T(8,128)(2,1)}, bf16[512,512]{1,0:T(8,128)(2,1)S(1)}, u32[]{:S(2)}, u32[]{:S(2)}) collective-permute-start(bf16[512,512]{1,0:T(8,128)(2,1)} %get-tuple-element.70), channel_id=1, source_target_pairs={{0,18},{1,19},{2,0},{3,1},{4,22},{5,23},{6,4},{7,5},{8,10},{9,11},... | collective-permute-start | bytes 1572872 | tf_op jit(solution)/shard_map/ppermute | solution.py:803
  25.2 10.5 %dispatch.3 = (bf16[8,224,512]{2,1,0:T(8,128)(2,1)}, bf16[8,208,512]{2,1,0:T(8,128)(2,1)}) custom-call(s32[2,1600]{1,0:T(2,128)} %get-tuple-element.68.slot_rows, s32[2,1600]{1,0:T(2,128)} %bitcast.54, bf16[1600,512]{1,0:T(8,128)(2,1)} %up.1), custom_call_target="tpu_custom_call" | custom-call | flops 100000000 | bytes 100000 | tf_op jit(solution)/shard_map/dispatch/pallas_call | solution.py:253
  36.0 1.5 pad_maximum_fusion.small.wqkv.wout.refs_3_.refs_2_
  37.5 0.4 collective-permute-done.3
  37.9 14.7 %all-to-all-start = ((bf16[8,224,512]{2,1,0:T(8,128)(2,1)}), bf16[8,224,512]{2,1,0:T(8,128)(2,1)S(1)}, u32[]{:S(2)}, u32[]{:S(2)}) async-start(bf16[8,224,512]{2,1,0:T(8,128)(2,1)} %get-tuple-element.74), calls=%async_computation | async-start | bytes 3670016 | tf_op jit(solution)/shard_map/all_to_all | solution.py:822
  52.7 0.7 collective-permute-start.6
  53.4 5.6 %collective-permute-start.5 = (bf16[528,512]{1,0:T(8,128)(2,1)S(1)}, bf16[528,512]{1,0:T(8,128)(2,1)S(1)}, u32[]{:S(2)}, u32[]{:S(2)}) collective-permute-start(bf16[528,512]{1,0:T(8,128)(2,1)S(1)} %copy-done.9), channel_id=1, source_target_pairs={{0,18},{1,19},{2,0},{3,1},{4,22},{5,23},{6,4},{7,5},{8,10},{9,11},... | collective-permute-start | bytes 1622024 | tf_op jit(solution)/shard_map/ppermute | solution.py:803
  59.0 0.6 reshape.90.mask
  59.6 16.8 %attention_forward.1 = (bf16[1600,1536]{1,0:T(8,128)(2,1)}, bf16[1600,512]{1,0:T(8,128)(2,1)}, f32[8,8,200]{2,1,0:T(8,128)}, f32[1600,512]{1,0:T(8,128)}, bf16[1600,512]{1,0:T(8,128)(2,1)}) custom-call(bf16[1600,512]{1,0:T(8,128)(2,1)} %x.3, s32[8,1,200]{2,1,0:T(1,128)} %reshape.90.mask, bf16[512,2176]{1,0:T(8,128)(2,1)} %pad_maximum_fusion.small.wqkv.wout.refs_3_.refs_2_, ...), custom_call_target="tpu_custom_call" | custom-call | flops 170000000 | bytes 170000 | tf_op jit(solution)/shard_map/attention_forward/pallas_call | solution.py:325
  76.4 7.1 %dispatch.4 = bf16[8,208,512]{2,1,0:T(8,128)(2,1)} custom-call(s32[2,1600]{1,0:T(2,128)} %get-tuple-element.68.slot_rows, s32[2,1600]{1,0:T(2,128)} %bitcast.55, bf16[1600,512]{1,0:T(8,128)(2,1)} %get-tuple-element.73.rows), custom_call_target="tpu_custom_call" | custom-call | flops 100000000 | bytes 100000 | tf_op jit(solution)/shard_map/dispatch/pallas_call | solution.py:253
  83.6 4.4 %collective-permute-done.5 = bf16[528,512]{1,0:T(8,128)(2,1)S(1)} collective-permute-done((bf16[528,512]{1,0:T(8,128)(2,1)S(1)}, bf16[528,512]{1,0:T(8,128)(2,1)S(1)}, u32[]{:S(2)}, u32[]{:S(2)}) %collective-permute-start.5) | collective-permute-done | bytes 540704 | tf_op jit(solution)/shard_map/ppermute | solution.py:803
  87.9 0.4 all-to-all-done.refs_1_
  88.7 6.2 %all-to-all-start.1 = ((bf16[8,208,512]{2,1,0:T(8,128)(2,1)}), bf16[8,208,512]{2,1,0:T(8,128)(2,1)S(1)}, u32[]{:S(2)}, u32[]{:S(2)}) async-start(bf16[8,208,512]{2,1,0:T(8,128)(2,1)} %dispatch.4), calls=%async_computation.1 | async-start | bytes 3407872 | tf_op jit(solution)/shard_map/all_to_all | solution.py:822
  94.9 2.3 broadcast_select_fusion.14
  97.2 0.5 collective-permute-start.10
  97.7 1.3 broadcast_select_fusion.16
  99.1 0.5 collective-permute-start.8
  99.6 8.5 %dispatch.5 = bf16[8,400,512]{2,1,0:T(8,128)(2,1)} custom-call(s32[2,1600]{1,0:T(2,128)} %get-tuple-element.68.slot_rows, s32[2,1600]{1,0:T(2,128)} %bitcast.56, bf16[1600,512]{1,0:T(8,128)(2,1)} %get-tuple-element.73.rows, bf16[8,208,512]{2,1,0:T(8,128)(2,1)} %get-tuple-element.77.outs_0_), custom_call_target="tpu_custom_call" | custom-call | flops 100000000 | bytes 100000 | tf_op jit(solution)/shard_map/dispatch/pallas_call | solution.py:253
  108.1 0.7 fusion.2
  108.8 0.6 pad_maximum_fusion.4
  109.4 3.4 maximum_maximum_fusion.refs_4_.refs_5_.refs_6_.refs_3_
  112.8 3.6 all-to-all-done.1
  116.4 1.2 copy-done.4
  117.6 5.7 %all-to-all-start.2 = ((bf16[8,400,512]{2,1,0:T(8,128)(2,1)}), bf16[8,400,512]{2,1,0:T(8,128)(2,1)S(1)}, u32[]{:S(2)}, u32[]{:S(2)}) async-start(bf16[8,400,512]{2,1,0:T(8,128)(2,1)} %dispatch.5), calls=%async_computation.2 | async-start | bytes 6553600 | tf_op jit(solution)/shard_map/all_to_all | solution.py:822
  123.3 0.5 compare_convert_fusion.refs_2_.refs_1_
  123.8 41.5 %experts.2 = (bf16[8,416,512]{2,1,0:T(8,128)(2,1)}, bf16[2,1040,512]{2,1,0:T(8,128)(2,1)}, bf16[2,1040,512]{2,1,0:T(8,128)(2,1)}, f32[512,128]{1,0:T(8,128)}) custom-call(bf16[1664,512]{1,0:T(8,128)(2,1)} %bitcast.44, bf16[8,224,512]{2,1,0:T(8,128)(2,1)} %copy-done.3, f32[1,128]{1,0:T(1,128)} %compare_convert_fusion.refs_2_.refs_1_, ...), custom_call_target="tpu_custom_call" | custom-call | flops 500000000 | bytes 500000 | tf_op jit(solution)/shard_map/experts/pallas_call | solution.py:535
  165.5 1.7 copy-done.2
  167.2 5.7 %all-to-all-start.3 = ((bf16[8,416,512]{2,1,0:T(8,128)(2,1)}), bf16[8,416,512]{2,1,0:T(8,128)(2,1)S(1)}, u32[]{:S(2)}, u32[]{:S(2)}) async-start(bf16[8,416,512]{2,1,0:T(8,128)(2,1)} %get-tuple-element.93), calls=%async_computation.3 | async-start | bytes 6815744 | tf_op jit(solution)/shard_map/all_to_all | solution.py:822
  172.8 39.8 %experts.3 = (bf16[8,192,512]{2,1,0:T(8,128)(2,1)}, bf16[8,192,512]{2,1,0:T(8,128)(2,1)}, bf16[2,1040,512]{2,1,0:T(8,128)(2,1)}, bf16[2,1040,512]{2,1,0:T(8,128)(2,1)}, f32[512,128]{1,0:T(8,128)}) custom-call(bf16[8,400,512]{2,1,0:T(8,128)(2,1)} %copy-done.2, f32[1,128]{1,0:T(1,128)} %compare_convert_fusion.refs_2_.refs_1_, ...), custom_call_target="tpu_custom_call" | custom-call | flops 500000000 | bytes 500000 | tf_op jit(solution)/shard_map/experts/pallas_call | solution.py:535
  212.7 3.4 all-to-all-done.3
  216.1 6.0 %all-to-all-start.4 = ((bf16[8,192,512]{2,1,0:T(8,128)(2,1)}), bf16[8,192,512]{2,1,0:T(8,128)(2,1)}, u32[]{:S(2)}, u32[]{:S(2)}) async-start(bf16[8,192,512]{2,1,0:T(8,128)(2,1)} %get-tuple-element.98), calls=%async_computation.4 | async-start | bytes 3145728 | tf_op jit(solution)/shard_map/all_to_all | solution.py:822
  222.1 4.4 %broadcast_select_fusion = (bf16[1040,512]{1,0:T(8,128)(2,1)}, bf16[1040,512]{1,0:T(8,128)(2,1)}, bf16[1040,512]{1,0:T(8,128)(2,1)}) fusion(pred[]{:T(512)S(6)} %ne.53, bf16[2,1040,512]{2,1,0:T(8,128)(2,1)} %collective-permute-done.11, bf16[2,1040,512]{2,1,0:T(8,128)(2,1)} %get-tuple-element.100), kind=kLoop, calls=%fused_computation.11 | loop fusion | flops 4792320 | bytes 7454721 | tf_op jit(solution)/shard_map/jit(_where)/select_n | solution.py:876
  226.5 15.3 %all-to-all-done.4.ret_b = bf16[8,192,512]{2,1,0:T(8,128)(2,1)} async-done(((bf16[8,192,512]{2,1,0:T(8,128)(2,1)}), bf16[8,192,512]{2,1,0:T(8,128)(2,1)}, u32[]{:S(2)}, u32[]{:S(2)}) %all-to-all-start.4) | async-done | bytes 1572896 | tf_op jit(solution)/shard_map/all_to_all | solution.py:822
  241.8 0.5 collective-permute-start.12
  242.2 1.6 collective-permute-start.13
  243.8 7.6 %all-to-all-start.5 = ((bf16[8,192,512]{2,1,0:T(8,128)(2,1)}), bf16[8,192,512]{2,1,0:T(8,128)(2,1)S(1)}, u32[]{:S(2)}, u32[]{:S(2)}) async-start(bf16[8,192,512]{2,1,0:T(8,128)(2,1)} %get-tuple-element.108), calls=%async_computation.5 | async-start | bytes 3145728 | tf_op jit(solution)/shard_map/all_to_all | solution.py:822
  251.4 41.4 %attention_backward.1 = (f32[1600,512]{1,0:T(8,128)}, bf16[512,2176]{1,0:T(8,128)(2,1)}) custom-call(bf16[1600,512]{1,0:T(8,128)(2,1)} %x.3, s32[8,1,200]{2,1,0:T(1,128)} %reshape.90.mask, bf16[512,2176]{1,0:T(8,128)(2,1)} %pad_maximum_fusion.small.wqkv.wout.refs_3_.refs_2_, bf16[512,2176]{1,0:T(8,128)(2,1)} %pad_maximum_fusion.small.wqkv.wout.refs_3_.refs_2_, ...), custom_call_target="tpu_custom_call" | custom-call | flops 500000000 | bytes 500000 | tf_op jit(solution)/shard_map/attention_backward/pallas_call | solution.py:658
  292.8 2.1 broadcast_select_fusion.5
  295.0 0.5 collective-permute-start.14
  295.5 1.4 collective-permute-done.15
  297.0 0.8 collective-permute-done.14
  297.8 0.4 select_convert_fusion
  298.2 6.5 %collective-permute-start.16 = (bf16[128,2176]{1,0:T(8,128)(2,1)S(1)}, bf16[128,2176]{1,0:T(8,128)(2,1)S(1)}, u32[]{:S(2)}, u32[]{:S(2)}) collective-permute-start(bf16[128,2176]{1,0:T(8,128)(2,1)S(1)} %select_convert_fusion), channel_id=1, source_target_pairs={{0,2},{1,3},{2,0},{3,1},{4,6},{5,7},{6,4},{7,5},{8,10},{9,11},{10,... | collective-permute-start | bytes 1671176 | tf_op jit(solution)/shard_map/ppermute | solution.py:803
  304.7 12.9 %collective-permute-done.16 = bf16[128,2176]{1,0:T(8,128)(2,1)S(1)} collective-permute-done((bf16[128,2176]{1,0:T(8,128)(2,1)S(1)}, bf16[128,2176]{1,0:T(8,128)(2,1)S(1)}, u32[]{:S(2)}, u32[]{:S(2)}) %collective-permute-start.16) | collective-permute-done | bytes 557088 | tf_op jit(solution)/shard_map/ppermute | solution.py:803
  317.6 1.3 add_convert_fusion.2
  318.9 9.9 %all-to-all-start.6 = ((bf16[8,16,2176]{2,1,0:T(8,128)(2,1)}), bf16[8,16,2176]{2,1,0:T(8,128)(2,1)S(1)}, u32[]{:S(2)}, u32[]{:S(2)}) async-start(bf16[8,16,2176]{2,1,0:T(8,128)(2,1)} %bitcast.26), calls=%async_computation.6 | async-start | bytes 1114112 | tf_op jit(solution)/shard_map/all_to_all | solution.py:906
  328.8 14.7 %all-to-all-done.6 = bf16[8,16,2176]{2,1,0:T(8,128)(2,1)S(1)} async-done(((bf16[8,16,2176]{2,1,0:T(8,128)(2,1)}), bf16[8,16,2176]{2,1,0:T(8,128)(2,1)S(1)}, u32[]{:S(2)}, u32[]{:S(2)}) %all-to-all-start.6) | async-done | bytes 557088 | tf_op jit(solution)/shard_map/all_to_all | solution.py:906
  343.6 0.8 broadcast_in_dim.34
  344.4 3.6 all-to-all-start.7
  348.1 1.7 convert_add_fusion
  349.8 0.6 fusion.9
  350.3 0.5 constant_dynamic-slice_fusion
  350.9 1.5 slice_bitcast_fusion
  352.3 9.6 %combine.1 = bf16[1600,512]{1,0:T(8,128)(2,1)} custom-call(s32[1600,2]{1,0:T(8,128)} %get-tuple-element.64.slot, f32[1600,512]{1,0:T(8,128)} %get-tuple-element.72.residual, bf16[8,2,208,512]{3,2,1,0:T(8,128)(2,1)} %bitcast.43, bf16[8,192,512]{2,1,0:T(8,128)(2,1)} %copy-done.5), custom_call_target="tpu_custom_call" | custom-call | flops 100000000 | bytes 100000 | tf_op jit(solution)/shard_map/combine/pallas_call | solution.py:710
  362.0 1.1 all-to-all-done.7
  363.2 0.8 slice_reduce_fusion
  364.0 0.7 slice.121
  364.7 1.0 slice.120
  365.7 0.7 copy.33
  (53 shorter events, 1.4 us)
Async XLA Ops:
  3.3 32.3 %copy-start.8 = (bf16[128,2176]{1,0:T(8,128)(2,1)S(1)}, bf16[128,2176]{1,0:T(8,128)(2,1)}, u32[]{:S(2)}) copy-start(bf16[128,2176]{1,0:T(8,128)(2,1)} %get-tuple-element.65) | copy-start | bytes 1671172
  3.3 15.8 %collective-permute-start = (bf16[128,2176]{1,0:T(8,128)(2,1)}, bf16[128,2176]{1,0:T(8,128)(2,1)S(1)}, u32[]{:S(2)}, u32[]{:S(2)}) collective-permute-start(bf16[128,2176]{1,0:T(8,128)(2,1)} %get-tuple-element.65), channel_id=1, source_target_pairs={{0,2},{1,3},{2,0},{3,1},{4,6},{5,7},{6,4},{7,5},{8,10},{9,11},{10,... | collective-permute-start | bytes 1671176 | tf_op jit(solution)/shard_map/ppermute | solution.py:803
  6.3 29.4 %collective-permute-start.1 = (bf16[128,2176]{1,0:T(8,128)(2,1)}, bf16[128,2176]{1,0:T(8,128)(2,1)S(1)}, u32[]{:S(2)}, u32[]{:S(2)}) collective-permute-start(bf16[128,2176]{1,0:T(8,128)(2,1)} %get-tuple-element.65), channel_id=1, source_target_pairs={{0,1},{1,0},{2,3},{3,2},{4,5},{5,4},{6,7},{7,6},{8,9},{9,8},{10,11... | collective-permute-start | bytes 1671176 | tf_op jit(solution)/shard_map/ppermute | solution.py:803
  19.2 16.5 %collective-permute-start.2 = (bf16[128,2176]{1,0:T(8,128)(2,1)S(1)}, bf16[128,2176]{1,0:T(8,128)(2,1)S(1)}, u32[]{:S(2)}, u32[]{:S(2)}) collective-permute-start(bf16[128,2176]{1,0:T(8,128)(2,1)S(1)} %collective-permute-done), channel_id=1, source_target_pairs={{0,1},{1,0},{2,3},{3,2},{4,5},{5,4},{6,7},{7,6},{8,9},{9,8},{10,11... | collective-permute-start | bytes 1671176 | tf_op jit(solution)/shard_map/ppermute | solution.py:803
  19.2 18.3 %collective-permute-start.4 = (bf16[512,512]{1,0:T(8,128)(2,1)}, bf16[512,512]{1,0:T(8,128)(2,1)S(1)}, u32[]{:S(2)}, u32[]{:S(2)}) collective-permute-start(bf16[512,512]{1,0:T(8,128)(2,1)} %get-tuple-element.70), channel_id=1, source_target_pairs={{2,18},{3,19},{6,22},{7,23},{8,24},{9,25},{12,28},{13,29},{18,2},{... | collective-permute-start | bytes 1572872 | tf_op jit(solution)/shard_map/ppermute | solution.py:803
  19.9 18.1 %collective-permute-start.3 = (bf16[512,512]{1,0:T(8,128)(2,1)}, bf16[512,512]{1,0:T(8,128)(2,1)S(1)}, u32[]{:S(2)}, u32[]{:S(2)}) collective-permute-start(bf16[512,512]{1,0:T(8,128)(2,1)} %get-tuple-element.70), channel_id=1, source_target_pairs={{0,18},{1,19},{2,0},{3,1},{4,22},{5,23},{6,4},{7,5},{8,10},{9,11},... | collective-permute-start | bytes 1572872 | tf_op jit(solution)/shard_map/ppermute | solution.py:803
  37.5 15.2 %copy-start.9 = (bf16[528,512]{1,0:T(8,128)(2,1)S(1)}, bf16[528,512]{1,0:T(8,128)(2,1)}, u32[]{:S(2)}) copy-start(bf16[528,512]{1,0:T(8,128)(2,1)} %get-tuple-element.75) | copy-start | bytes 1622020
  37.5 21.5 %copy-start.14 = (s32[8,200]{1,0:T(8,128)S(1)}, s32[8,200]{1,0:T(8,128)}, u32[]{:S(2)}) copy-start(s32[8,200]{1,0:T(8,128)} %param.18) | copy-start | bytes 19204
  37.5 15.1 %copy-start.12 = (bf16[512,512]{1,0:T(8,128)(2,1)}, bf16[512,512]{1,0:T(8,128)(2,1)S(1)}, u32[]{:S(2)}) copy-start(bf16[512,512]{1,0:T(8,128)(2,1)S(1)} %collective-permute-done.4) | copy-start | bytes 1572868
  37.9 14.7 %copy-start.13 = (bf16[512,512]{1,0:T(8,128)(2,1)}, bf16[512,512]{1,0:T(8,128)(2,1)S(1)}, u32[]{:S(2)}) copy-start(bf16[512,512]{1,0:T(8,128)(2,1)S(1)} %collective-permute-done.3) | copy-start | bytes 1572868
  37.9 50.5 %all-to-all-start = ((bf16[8,224,512]{2,1,0:T(8,128)(2,1)}), bf16[8,224,512]{2,1,0:T(8,128)(2,1)S(1)}, u32[]{:S(2)}, u32[]{:S(2)}) async-start(bf16[8,224,512]{2,1,0:T(8,128)(2,1)} %get-tuple-element.74), calls=%async_computation | async-start | bytes 3670016 | tf_op jit(solution)/shard_map/all_to_all | solution.py:822
  52.7 30.9 %collective-permute-start.6 = (bf16[528,512]{1,0:T(8,128)(2,1)S(1)}, bf16[528,512]{1,0:T(8,128)(2,1)S(1)}, u32[]{:S(2)}, u32[]{:S(2)}) collective-permute-start(bf16[528,512]{1,0:T(8,128)(2,1)S(1)} %copy-done.9), channel_id=1, source_target_pairs={{2,18},{3,19},{6,22},{7,23},{8,24},{9,25},{12,28},{13,29},{18,2},{... | collective-permute-start | bytes 1622024 | tf_op jit(solution)/shard_map/ppermute | solution.py:803
  53.4 34.6 %collective-permute-start.5 = (bf16[528,512]{1,0:T(8,128)(2,1)S(1)}, bf16[528,512]{1,0:T(8,128)(2,1)S(1)}, u32[]{:S(2)}, u32[]{:S(2)}) collective-permute-start(bf16[528,512]{1,0:T(8,128)(2,1)S(1)} %copy-done.9), channel_id=1, source_target_pairs={{0,18},{1,19},{2,0},{3,1},{4,22},{5,23},{6,4},{7,5},{8,10},{9,11},... | collective-permute-start | bytes 1622024 | tf_op jit(solution)/shard_map/ppermute | solution.py:803
  83.6 4.8 %copy-start.10 = (bf16[528,512]{1,0:T(8,128)(2,1)}, bf16[528,512]{1,0:T(8,128)(2,1)S(1)}, u32[]{:S(2)}) copy-start(bf16[528,512]{1,0:T(8,128)(2,1)S(1)} %collective-permute-done.6) | copy-start | bytes 1622020
  87.9 0.8 copy-start.11
  88.4 8.8 %copy-start.3 = (bf16[8,224,512]{2,1,0:T(8,128)(2,1)}, bf16[8,224,512]{2,1,0:T(8,128)(2,1)S(1)}, u32[]{:S(2)}) copy-start(bf16[8,224,512]{2,1,0:T(8,128)(2,1)S(1)} %all-to-all-done.refs_1_) | copy-start | bytes 5505028
  88.7 27.6 %all-to-all-start.1 = ((bf16[8,208,512]{2,1,0:T(8,128)(2,1)}), bf16[8,208,512]{2,1,0:T(8,128)(2,1)S(1)}, u32[]{:S(2)}, u32[]{:S(2)}) async-start(bf16[8,208,512]{2,1,0:T(8,128)(2,1)} %dispatch.4), calls=%async_computation.1 | async-start | bytes 3407872 | tf_op jit(solution)/shard_map/all_to_all | solution.py:822
  97.2 10.8 %collective-permute-start.9 = (bf16[528,512]{1,0:T(8,128)(2,1)}, bf16[528,512]{1,0:T(8,128)(2,1)S(1)}, u32[]{:S(2)}, u32[]{:S(2)}) collective-permute-start(bf16[528,512]{1,0:T(8,128)(2,1)} %get-tuple-element.171), channel_id=1, source_target_pairs={{0,1},{1,0},{2,3},{3,2},{4,5},{5,4},{6,7},{7,6},{8,9},{9,8},{10,11... | collective-permute-start | bytes 1622024 | tf_op jit(solution)/shard_map/ppermute | solution.py:803
  97.2 10.8 %collective-permute-start.10 = (bf16[528,512]{1,0:T(8,128)(2,1)}, bf16[528,512]{1,0:T(8,128)(2,1)S(1)}, u32[]{:S(2)}, u32[]{:S(2)}) collective-permute-start(bf16[528,512]{1,0:T(8,128)(2,1)} %get-tuple-element.172), channel_id=1, source_target_pairs={{0,1},{1,0},{2,3},{3,2},{4,5},{5,4},{6,7},{7,6},{8,9},{9,8},{10,11... | collective-permute-start | bytes 1622024 | tf_op jit(solution)/shard_map/ppermute | solution.py:803
  99.0 10.4 %collective-permute-start.7 = (bf16[512,512]{1,0:T(8,128)(2,1)S(1)}, bf16[512,512]{1,0:T(8,128)(2,1)}, u32[]{:S(2)}, u32[]{:S(2)}) collective-permute-start(bf16[512,512]{1,0:T(8,128)(2,1)S(1)} %get-tuple-element.173), channel_id=1, source_target_pairs={{0,1},{1,0},{2,3},{3,2},{4,5},{5,4},{6,7},{7,6},{8,9},{9,8},{10,11... | collective-permute-start | bytes 1572872 | tf_op jit(solution)/shard_map/ppermute | solution.py:803
  99.1 10.3 %collective-permute-start.8 = (bf16[512,512]{1,0:T(8,128)(2,1)S(1)}, bf16[512,512]{1,0:T(8,128)(2,1)}, u32[]{:S(2)}, u32[]{:S(2)}) collective-permute-start(bf16[512,512]{1,0:T(8,128)(2,1)S(1)} %get-tuple-element.174), channel_id=1, source_target_pairs={{0,1},{1,0},{2,3},{3,2},{4,5},{5,4},{6,7},{7,6},{8,9},{9,8},{10,11... | collective-permute-start | bytes 1572872 | tf_op jit(solution)/shard_map/ppermute | solution.py:803
  116.4 1.2 copy-start.4
  117.6 47.9 %all-to-all-start.2 = ((bf16[8,400,512]{2,1,0:T(8,128)(2,1)}), bf16[8,400,512]{2,1,0:T(8,128)(2,1)S(1)}, u32[]{:S(2)}, u32[]{:S(2)}) async-start(bf16[8,400,512]{2,1,0:T(8,128)(2,1)} %dispatch.5), calls=%async_computation.2 | async-start | bytes 6553600 | tf_op jit(solution)/shard_map/all_to_all | solution.py:822
  165.5 1.7 copy-start.2
  167.2 48.9 %all-to-all-start.3 = ((bf16[8,416,512]{2,1,0:T(8,128)(2,1)}), bf16[8,416,512]{2,1,0:T(8,128)(2,1)S(1)}, u32[]{:S(2)}, u32[]{:S(2)}) async-start(bf16[8,416,512]{2,1,0:T(8,128)(2,1)} %get-tuple-element.93), calls=%async_computation.3 | async-start | bytes 6815744 | tf_op jit(solution)/shard_map/all_to_all | solution.py:822
  212.6 9.5 %collective-permute-start.11 = (bf16[2,1040,512]{2,1,0:T(8,128)(2,1)}, bf16[2,1040,512]{2,1,0:T(8,128)(2,1)}, u32[]{:S(2)}, u32[]{:S(2)}) collective-permute-start(bf16[2,1040,512]{2,1,0:T(8,128)(2,1)} %get-tuple-element.101), channel_id=1, source_target_pairs={{0,1},{1,0},{2,3},{3,2},{4,5},{5,4},{6,7},{7,6},{8,9},{9,8},{10,11... | collective-permute-start | bytes 6389768 | tf_op jit(solution)/shard_map/ppermute | solution.py:803
  216.1 10.4 %copy-start = (bf16[8,416,512]{2,1,0:T(8,128)(2,1)}, bf16[8,416,512]{2,1,0:T(8,128)(2,1)S(1)}, u32[]{:S(2)}) copy-start(bf16[8,416,512]{2,1,0:T(8,128)(2,1)S(1)} %all-to-all-done.3) | copy-start | bytes 10223620
  216.1 25.6 %all-to-all-start.4 = ((bf16[8,192,512]{2,1,0:T(8,128)(2,1)}), bf16[8,192,512]{2,1,0:T(8,128)(2,1)}, u32[]{:S(2)}, u32[]{:S(2)}) async-start(bf16[8,192,512]{2,1,0:T(8,128)(2,1)} %get-tuple-element.98), calls=%async_computation.4 | async-start | bytes 3145728 | tf_op jit(solution)/shard_map/all_to_all | solution.py:822
  241.8 51.0 %collective-permute-start.12 = (bf16[1040,512]{1,0:T(8,128)(2,1)}, bf16[1040,512]{1,0:T(8,128)(2,1)S(1)}, u32[]{:S(2)}, u32[]{:S(2)}) collective-permute-start(bf16[1040,512]{1,0:T(8,128)(2,1)} %get-tuple-element.105), channel_id=1, source_target_pairs={{18,0},{19,1},{0,2},{1,3},{22,4},{23,5},{4,6},{5,7},{10,8},{11,9},... | collective-permute-start | bytes 3194888 | tf_op jit(solution)/shard_map/ppermute | solution.py:803
  242.2 50.6 %collective-permute-start.13 = (bf16[1040,512]{1,0:T(8,128)(2,1)}, bf16[1040,512]{1,0:T(8,128)(2,1)}, u32[]{:S(2)}, u32[]{:S(2)}) collective-permute-start(bf16[1040,512]{1,0:T(8,128)(2,1)} %get-tuple-element.106), channel_id=1, source_target_pairs={{2,18},{3,19},{6,22},{7,23},{8,24},{9,25},{12,28},{13,29},{18,2},{... | collective-permute-start | bytes 3194888 | tf_op jit(solution)/shard_map/ppermute | solution.py:803
  243.8 75.1 %all-to-all-start.5 = ((bf16[8,192,512]{2,1,0:T(8,128)(2,1)}), bf16[8,192,512]{2,1,0:T(8,128)(2,1)S(1)}, u32[]{:S(2)}, u32[]{:S(2)}) async-start(bf16[8,192,512]{2,1,0:T(8,128)(2,1)} %get-tuple-element.108), calls=%async_computation.5 | async-start | bytes 3145728 | tf_op jit(solution)/shard_map/all_to_all | solution.py:822
  292.8 5.0 %copy-start.1 = (bf16[512,2176]{1,0:T(8,128)(2,1)S(1)}, bf16[512,2176]{1,0:T(8,128)(2,1)}, u32[]{:S(2)}) copy-start(bf16[512,2176]{1,0:T(8,128)(2,1)} %get-tuple-element.107) | copy-start | bytes 6684676
  292.8 5.4 %copy-start.7 = (bf16[1040,512]{1,0:T(8,128)(2,1)}, bf16[1040,512]{1,0:T(8,128)(2,1)S(1)}, u32[]{:S(2)}) copy-start(bf16[1040,512]{1,0:T(8,128)(2,1)S(1)} %collective-permute-done.12) | copy-start | bytes 3194884
  294.9 2.0 collective-permute-start.15
  295.0 2.7 collective-permute-start.14
  298.2 19.5 %collective-permute-start.16 = (bf16[128,2176]{1,0:T(8,128)(2,1)S(1)}, bf16[128,2176]{1,0:T(8,128)(2,1)S(1)}, u32[]{:S(2)}, u32[]{:S(2)}) collective-permute-start(bf16[128,2176]{1,0:T(8,128)(2,1)S(1)} %select_convert_fusion), channel_id=1, source_target_pairs={{0,2},{1,3},{2,0},{3,1},{4,6},{5,7},{6,4},{7,5},{8,10},{9,11},{10,... | collective-permute-start | bytes 1671176 | tf_op jit(solution)/shard_map/ppermute | solution.py:803
  318.9 29.1 %copy-start.6 = (bf16[1040,512]{1,0:T(8,128)(2,1)S(1)}, bf16[1040,512]{1,0:T(8,128)(2,1)}, u32[]{:S(2)}) copy-start(bf16[1040,512]{1,0:T(8,128)(2,1)} %get-tuple-element.112) | copy-start | bytes 3194884
  318.9 30.8 %copy-start.5 = (bf16[8,192,512]{2,1,0:T(8,128)(2,1)}, bf16[8,192,512]{2,1,0:T(8,128)(2,1)S(1)}, u32[]{:S(2)}) copy-start(bf16[8,192,512]{2,1,0:T(8,128)(2,1)S(1)} %all-to-all-done.5.ret_b) | copy-start | bytes 4718596
  318.9 24.6 %all-to-all-start.6 = ((bf16[8,16,2176]{2,1,0:T(8,128)(2,1)}), bf16[8,16,2176]{2,1,0:T(8,128)(2,1)S(1)}, u32[]{:S(2)}, u32[]{:S(2)}) async-start(bf16[8,16,2176]{2,1,0:T(8,128)(2,1)} %bitcast.26), calls=%async_computation.6 | async-start | bytes 1114112 | tf_op jit(solution)/shard_map/all_to_all | solution.py:906
  344.4 18.6 %all-to-all-start.7 = ((bf16[8,16,2176]{2,1,0:T(8,128)(2,1)}), bf16[8,16,2176]{2,1,0:T(8,128)(2,1)S(1)}, u32[]{:S(2)}, u32[]{:S(2)}) async-start(bf16[8,16,2176]{2,1,0:T(8,128)(2,1)} %broadcast_in_dim.34), calls=%async_computation.7 | async-start | bytes 1114112 | tf_op jit(solution)/shard_map/all_to_all | solution.py:906

commit v4 on v3

--- a/solution.py
+++ b/solution.py
@@ -135,7 +135,7 @@
     share, width = wout.shape
     hidden = w_in.shape[0]
     double = 2 * hidden + EXTRA
-    cuts = [0] + [double * part // 100 // EXTRA * EXTRA for part in (50,)] + [double]
+    cuts = [0] + [double * part // 100 // EXTRA * EXTRA for part in (55,)] + [double]
     sizes = [high - low for low, high in zip(cuts, cuts[1:])]
     return pl.pallas_call(
         pack_kernel,
@@ -223,43 +223,49 @@
     )(priority, route_rows, capacity[None, :])
 
 
-def dispatch_kernel(pieces, with_other, has_carry, slot_rows, route_rows, rows, *outs):
-    e = pl.program_id(0)
-    if has_carry:
-        carry, *outs = outs
-        outs[-1][0, pieces[-1][1] :, :] = carry[0]
-    for (start, size), out in zip(pieces, outs):
-        place = lax.broadcasted_iota(jnp.int32, (size, 1), 0) + (start + e * size)
-        hit_a = slot_rows[0:1, :] == place
-        hit_b = slot_rows[1:2, :] == place
-        pick = jnp.where(hit_a | hit_b, 1.0, 0.0).astype(BF16)
-        out[0, 0:size, :] = mm(pick, rows[...]).astype(BF16)
-        if with_other:
-            named = route_rows[...].astype(F32) + 1.0
-            found = jnp.where(hit_a, named[1:2, :], jnp.where(hit_b, named[0:1, :], 0.0))
-            column = jnp.sum(found, axis=1, keepdims=True) - 1.0
-            turned = jnp.transpose(jnp.broadcast_to(column, (size, LANES)))
-            out[0, size : size + EXTRA, 0:size] = turned[0:EXTRA, :].astype(BF16)
-
-
-def dispatch(slot_rows, route_rows, rows, experts, pieces, with_other, carry=None):
-    total, width = rows.shape
-    tall = [size + (EXTRA if with_other else 0) for _, size in pieces]
-    extra, extra_spec = (), ()
-    if carry is not None:
-        tall[-1] += carry.shape[1]
-        extra = (carry,)
-        extra_spec = (pl.BlockSpec((1,) + carry.shape[1:], lambda e: (e, 0, 0)),)
+def dispatch_kernel(start, size, with_other, slot_rows, route_rows, *refs):
+    *sources, out = refs
+    group = out.shape[0]
+    tall = group * size
+    width = out.shape[2]
+    place = lax.broadcasted_iota(jnp.int32, (tall, 1), 0) + (start + pl.program_id(0) * tall)
+    hit_a = slot_rows[0:1, :] == place
+    hit_b = slot_rows[1:2, :] == place
+    pick = jnp.where(hit_a | hit_b, 1.0, 0.0).astype(BF16)
+    for k, source in enumerate(sources):
+        found = mm(pick, source[...]).astype(BF16)
+        out[:, k * size : (k + 1) * size, :] = found.reshape(group, size, width)
+    if with_other:
+        named = route_rows[...].astype(F32) + 1.0
+        found = jnp.where(hit_a, named[1:2, :], jnp.where(hit_b, named[0:1, :], 0.0))
+        column = jnp.sum(found, axis=1, keepdims=True) - 1.0
+        last = len(sources) * size
+        for g in range(group):
+            turned = jnp.transpose(
+                jnp.broadcast_to(column[g * size : (g + 1) * size, :], (size, LANES))
+            )
+            out[g, last : last + EXTRA, 0:size] = turned[0:EXTRA, :].astype(BF16)
+
+
+def dispatch(slot_rows, route_rows, sources, experts, piece, with_other):
+    total, width = sources[0].shape
+    start, size = piece
+    tall = size * len(sources) + (EXTRA if with_other else 0)
+    group = 1 if with_other else 2
     return pl.pallas_call(
-        partial(dispatch_kernel, pieces, with_other, carry is not None),
-        grid=(experts,),
-        in_specs=[whole((2, total)), whole((2, total)), whole((total, width)), *extra_spec],
-        out_specs=[pl.BlockSpec((1, t, width), lambda e: (e, 0, 0)) for t in tall],
-        out_shape=[jax.ShapeDtypeStruct((experts, t, width), BF16) for t in tall],
+        partial(dispatch_kernel, start, size, with_other),
+        grid=(experts // group,),
+        in_specs=[
+            whole((2, total)),
+            whole((2, total)),
+            *[whole((total, width)) for _ in sources],
+        ],
+        out_specs=pl.BlockSpec((group, tall, width), lambda e: (e, 0, 0)),
+        out_shape=jax.ShapeDtypeStruct((experts, tall, width), BF16),
         compiler_params=params(1),
         name="dispatch",
         cost_estimate=cost(10),
-    )(slot_rows, route_rows, rows, *extra)
+    )(slot_rows, route_rows, *sources)
 
 
 def stack_rows(length, width):
@@ -566,8 +572,8 @@
 
 
 def backward_kernel(
-    experts, x, mask, small, wqkv, wout, triple, context, logs, residual, up, slot, ret_a, ret_b, drouter,
-    input_grad, packed,
+    experts, x, mask, small, wqkv, wout, triple, context, logs, residual, up, slot, ret_a, ret_b, drouter, parity,
+    input_grad, keep, give_a, give_b,
     tg, gains, dqkv, dwout, dgains, stack_k, stack_v, dq_t,
 ):
     step = pl.program_id(0)
@@ -644,13 +650,30 @@
 
     @pl.when(step == pl.num_programs(0) - 1)
     def _():
-        packed[:, : 3 * width] = dqkv[...].astype(BF16)
-        packed[:, 3 * width : 4 * width] = dwout[...].astype(BF16)
-        packed[:, 4 * width :] = (drouter[...] + jnp.transpose(dgains[...])).astype(BF16)
+        tail = drouter[...] + jnp.transpose(dgains[...])
+        share = width // 4
+        odd = parity[0, 0]
+        for part in range(4):
+            rows = slice(part * share, (part + 1) * share)
+            spot = slice(part // 2 * share, (part // 2 + 1) * share)
+
+            def put(target, spot):
+                target[spot, : 3 * width] = dqkv[rows, :].astype(BF16)
+                target[spot, 3 * width : 4 * width] = dwout[rows, :].astype(BF16)
+                target[spot, 4 * width :] = tail[rows, :].astype(BF16)
+
+            @pl.when(odd == part % 2)
+            def _():
+                put(keep, spot)
+
+            @pl.when(odd != part % 2)
+            def _():
+                put(give_b if part // 2 else give_a, slice(0, share))
 
 
 def attention_backward(
-    x, mask, dense, triple, context, logs, residual, up, slot, ret, drouter, experts
+    x, mask, dense, triple, context, logs, residual, up, slot, ret, drouter, parity,
+    experts,
 ):
     total, width = x.shape
     images, length = mask.shape
@@ -672,14 +695,19 @@
             pl.BlockSpec((length, 2), rows),
             *returned_specs(ret, 0),
             whole((width, LANES)),
+            pl.BlockSpec(memory_space=pltpu.SMEM),
         ],
         out_specs=[
             pl.BlockSpec((length, width), rows),
-            whole((width, 4 * width + LANES)),
+            whole((width // 2, 4 * width + LANES)),
+            whole((width // 4, 4 * width + LANES)),
+            whole((width // 4, 4 * width + LANES)),
         ],
         out_shape=[
             jax.ShapeDtypeStruct((total, width), F32),
-            jax.ShapeDtypeStruct((width, 4 * width + LANES), BF16),
+            jax.ShapeDtypeStruct((width // 2, 4 * width + LANES), BF16),
+            jax.ShapeDtypeStruct((width // 4, 4 * width + LANES), BF16),
+            jax.ShapeDtypeStruct((width // 4, 4 * width + LANES), BF16),
         ],
         scratch_shapes=[
             pltpu.VMEM((length, 3 * width), BF16),
@@ -696,7 +724,7 @@
         cost_estimate=cost(50),
     )(
         x, mask.reshape(images, 1, length), dense, dense, dense, triple, context, logs, residual,
-        up, slot, *ret, drouter,
+        up, slot, *ret, drouter, parity,
     )
 
 
@@ -723,6 +751,29 @@
     )(slot, residual, *ret)
 
 
+def unpack_kernel(experts, total, wqkv, wout, router, *gains):
+    width = wout.shape[1]
+    wqkv[...] = total[:, : 3 * width].astype(F32)
+    wout[...] = total[:, 3 * width : 4 * width].astype(F32)
+    turned = jnp.transpose(total[:, 4 * width :].astype(F32))
+    router[...] = turned[0:experts, :]
+    for k, gain in enumerate(gains):
+        gain[...] = turned[experts + k : experts + k + 1, :]
+
+
+def unpack(total, experts):
+    share = total.shape[0]
+    width = (total.shape[1] - LANES) // 4
+    shapes = [(share, 3 * width), (share, width), (experts, share)] + [(1, share)] * 4
+    return pl.pallas_call(
+        partial(unpack_kernel, experts),
+        out_shape=[jax.ShapeDtypeStruct(shape, F32) for shape in shapes],
+        compiler_params=params(),
+        name="unpack",
+        cost_estimate=cost(2),
+    )(total)
+
+
 class PlainPlan:
     def __init__(self, seq, wt):
         self.seq, self.wt = seq, wt
@@ -758,11 +809,16 @@
     def finish_expert(self, parts, received):
         return received.astype(F32)
 
-    def begin_dense_sum(self, grads):
+    def parity(self):
+        return jnp.zeros((1, 1), jnp.int32)
+
+    def begin_dense_sum(self, keep, give_a, give_b):
+        half = keep.shape[0] // 2
+        grads = jnp.concatenate([keep[:half], give_a, keep[half:], give_b])
         return lax.psum_scatter(grads, "wt", scatter_dimension=0, tiled=True)
 
     def reduce_dense(self, part):
-        return lax.psum(part, "seq").astype(F32)
+        return lax.psum(part, "seq")
 
 
 class CubePlan:
@@ -886,15 +942,15 @@
     def first_back(self):
         return [(b, a) for a, b in self.first]
 
-    def begin_dense_sum(self, grads):
-        share = grads.shape[0] // 4
-        width = grads.shape[1]
-        parts = [grads[i * share : (i + 1) * share] for i in range(4)]
-        first = self.core_zero()
-        keep = [jnp.where(first, parts[0], parts[1]), jnp.where(first, parts[2], parts[3])]
-        give = [jnp.where(first, parts[1], parts[0]), jnp.where(first, parts[3], parts[2])]
-        got = [self.send(v.astype(BF16), self.core).astype(F32) for v in give]
-        low, high = keep[0].astype(F32) + got[0], keep[1].astype(F32) + got[1]
+    def parity(self):
+        return (lax.axis_index("wt") % 2).reshape(1, 1)
+
+    def begin_dense_sum(self, keep, *give):
+        share = keep.shape[0] // 2
+        low, high = (
+            keep[k * share : (k + 1) * share].astype(F32) + self.send(v, self.core).astype(F32)
+            for k, v in enumerate(give)
+        )
         flip = self.x_zero()
         out = self.send(jnp.where(flip, high, low).astype(BF16), self.cross)
         mine = jnp.where(flip, low, high) + out.astype(F32)
@@ -906,7 +962,7 @@
         swap = lambda v: lax.all_to_all(v, "seq", split_axis=0, concat_axis=0, tiled=True)
         total = jnp.sum(swap(pieces).astype(F32), axis=0, keepdims=True).astype(BF16)
         spread = swap(jnp.broadcast_to(total, pieces.shape))
-        return spread.reshape(share, width).astype(F32)
+        return spread.reshape(share, width)
 
 
 def plan_of(seq, wt):
@@ -952,17 +1008,17 @@
     own = (jnp.arange(LANES) == plan.own_id()).astype(F32)[None, :]
     route_rows = routes.T
     slot, slot_rows = make_slots(route_rows, priority, capacity, parts)
-    slot_rows, far = tie((slot_rows, far))
+    slot_rows, far, fetched[0] = tie((slot_rows, far, fetched[0]))
     pieces = ((0, front), (experts * front, cap - front))
     send = partial(dispatch, slot_rows, route_rows)
-    ups_a, ups_b = send(cotangent, experts, pieces, True)
+    ups_a = send((cotangent,), experts, pieces[0], True)
     dense = plan.gather_dense(packed, far)
-    dense, ups_a, fetched[0] = tie((dense, ups_a, fetched[0]))
+    dense, ups_a = tie((dense, ups_a))
     ups_a = plan.exchange(ups_a)
 
     triple, context, logs, residual, normed = attention_forward(inputs, key_mask, dense, experts)
-    (rows_a,) = send(normed, experts, pieces[:1], False)
-    (mixed_b,) = send(normed, experts, pieces[1:], False, ups_b)
+    rows_a = send((normed,), experts, pieces[0], False)
+    mixed_b = send((normed, cotangent), experts, pieces[1], True)
     rows_a, ups_a, fetched[1] = tie((rows_a, ups_a, fetched[1]))
     rows_a = plan.exchange(rows_a)
     weights = jnp.concatenate(
@@ -986,28 +1042,29 @@
     sent_b = plan.exchange(sent_b)
     received = plan.reduce_expert(halves)
     ret_a = ret_a.reshape(experts, 2, front, width)
-    input_grad, grads = attention_backward(
+    input_grad, *grads = attention_backward(
         inputs, key_mask, dense, triple, context, logs, residual, cotangent, slot,
-        (ret_a, back_b), sums[2], experts,
+        (ret_a, back_b), sums[2], plan.parity(), experts,
     )
     grads, received = tie((grads, received))
-    mine = plan.begin_dense_sum(grads)
+    mine = plan.begin_dense_sum(*grads)
     mine, sent_b = tie((mine, sent_b))
     shard = plan.finish_expert(halves, received)
     done = plan.reduce_dense(mine)
-    block_output = combine(slot, residual, (ret_a, sent_b), 400)
-    base = 4 * width
+    block_output = combine(slot, residual, (ret_a, sent_b), 200)
+    dqkv, dwout, drouter, *dgains = unpack(done, experts)
+    dgains = [g.reshape(share) for g in dgains]
     rank = lax.axis_index("wt")
     return (
         block_output,
         input_grad,
-        done[:, base + experts],
-        done[:, base + experts + 1],
-        done[:, : 3 * width],
-        done[:, 3 * width : base],
-        done[:, base + experts + 2],
-        done[:, base + experts + 3],
-        done[:, base : base + experts],
+        dgains[0],
+        dgains[1],
+        dqkv,
+        dwout,
+        dgains[2],
+        dgains[3],
+        drouter.T,
         shard[None, :hidden_share],
         shard[2 * hidden_share, :hidden_share][None],
         shard[None, hidden_share : 2 * hidden_share],

time: 368 us -> 365 us (level)
  starting transfers between devices: 84.9 us -> 72 us
  waiting for transfers between devices: 63.7 us -> 75.3 us
    ppermute x17, waiting for transfers between devices: 25 us -> 37.6 us  [send(): return lax.ppermute(a, self.AXES, pairs)]
    all_to_all x6, starting transfers between devices: 45.8 us -> 33.7 us  [exchange(): lax.all_to_all(a, self.AXES, split_axis=0, concat_axis=0, axis_index_grou...]
    pallas_call x3 -> x4, Pallas kernels: 26.1 us -> 26 us  [the longest x3 24 us: dispatch(): pl.pallas_call(partial(dispatch_kernel, start, size, with_other), grid=(e...]
  transfers between devices with their start and end apart: 25 -> 25, of which waited for: 13 -> 10; matrix products, arithmetic and copies ran while one was open for 6% -> 6% of each run, Pallas kernels for 50% -> 50%
where the time goes in v4:
time: 365 us; the launch traced here: 363 us
  Pallas kernels  187 us (51%)
  waiting for transfers between devices  75.3 us (21%)
  starting transfers between devices  72 us (20%)
  other arithmetic  19.4 us (5%)
  local copies, waits for them, and re-layouts  8.57 us (2%)
    pallas_call x2, Pallas kernels, run_experts(): pl.pallas_call(partial(experts_kernel, block, bool(old)), grid=(steps,),...  81.3 us
    pallas_call x1, Pallas kernels, attention_backward(): pl.pallas_call(partial(backward_kernel, experts), grid=(images,), in_spec...  41.4 us
    ppermute x17, waiting for transfers between devices, send(): return lax.ppermute(a, self.AXES, pairs)  37.6 us
    all_to_all x6, starting transfers between devices, exchange(): lax.all_to_all(a, self.AXES, split_axis=0, concat_axis=0, axis_index_grou...  33.7 us
    ppermute x17, starting transfers between devices, send(): return lax.ppermute(a, self.AXES, pairs)  24.9 us
    pallas_call x3, Pallas kernels, dispatch(): pl.pallas_call(partial(dispatch_kernel, start, size, with_other), grid=(e...  24 us
    all_to_all x6, waiting for transfers between devices, exchange(): lax.all_to_all(a, self.AXES, split_axis=0, concat_axis=0, axis_index_grou...  22.8 us
    pallas_call x1, Pallas kernels, attention_forward(): pl.pallas_call(partial(attention_kernel, experts), grid=(images,), in_spe...  16.9 us
  transfers between devices with their start and end apart: 25, of which 10 were waited for; matrix products, arithmetic and copies ran while one was open for 6% of the time, Pallas kernels for 50%

profile of v4, /device:TPU:0, one launch (start us, length us, event | category | flops | bytes accessed | tf_op | source)
XLA Modules:
  0.0 363.3 jit_solution(9484540057690231684)
XLA Ops:
  0.7 2.7 pack.1
  3.3 1.6 collective-permute-start.2
  4.9 5.8 %collective-permute-start.1 = (bf16[560,512]{1,0:T(8,128)(2,1)}, bf16[560,512]{1,0:T(8,128)(2,1)}, u32[]{:S(2)}, u32[]{:S(2)}) collective-permute-start(bf16[560,512]{1,0:T(8,128)(2,1)} %get-tuple-element.76), channel_id=1, source_target_pairs={{0,18},{1,19},{2,0},{3,1},{4,22},{5,23},{6,4},{7,5},{8,10},{9,11},... | collective-permute-start | bytes 1720328 | tf_op jit(solution)/shard_map/ppermute | solution.py:859
  10.7 0.3 collective-permute-start
  11.0 7.9 %slots.1 = (s32[1600,2]{1,0:T(8,128)}, s32[2,1600]{1,0:T(2,128)}) custom-call(s32[1,1600]{1,0:T(1,128)} %prow.1, s32[2,1600]{1,0:T(2,128)} %bitcast.58, s32[1,8]{1,0:T(1,128)} %bitcast.70), custom_call_target="tpu_custom_call" | custom-call | flops 80000000 | bytes 80000 | tf_op jit(solution)/shard_map/slots/pallas_call | solution.py:208
  18.9 16.9 %collective-permute-done = bf16[128,2176]{1,0:T(8,128)(2,1)S(1)} collective-permute-done((bf16[128,2176]{1,0:T(8,128)(2,1)}, bf16[128,2176]{1,0:T(8,128)(2,1)S(1)}, u32[]{:S(2)}, u32[]{:S(2)}) %collective-permute-start) | collective-permute-done | bytes 557088 | tf_op jit(solution)/shard_map/ppermute | solution.py:859
  35.8 7.3 %dispatch.3 = bf16[8,224,512]{2,1,0:T(8,128)(2,1)} custom-call(s32[2,1600]{1,0:T(2,128)} %get-tuple-element.78.slot_rows, s32[2,1600]{1,0:T(2,128)} %bitcast.59, bf16[1600,512]{1,0:T(8,128)(2,1)} %up.1), custom_call_target="tpu_custom_call" | custom-call | flops 100000000 | bytes 100000 | tf_op jit(solution)/shard_map/dispatch/pallas_call | solution.py:255
  43.2 0.3 broadcast_select_fusion.10
  43.5 1.5 pad_maximum_fusion.small.wqkv.wout.refs_3_.refs_2_
  45.0 4.3 %all-to-all-start = ((bf16[8,224,512]{2,1,0:T(8,128)(2,1)}), bf16[8,224,512]{2,1,0:T(8,128)(2,1)S(1)}, u32[]{:S(2)}, u32[]{:S(2)}) async-start(bf16[8,224,512]{2,1,0:T(8,128)(2,1)} %dispatch.3), calls=%async_computation | async-start | bytes 3670016 | tf_op jit(solution)/shard_map/all_to_all | solution.py:878
  49.3 0.7 collective-permute-start.6
  50.0 5.6 %collective-permute-start.5 = (bf16[480,512]{1,0:T(8,128)(2,1)S(1)}, bf16[480,512]{1,0:T(8,128)(2,1)S(1)}, u32[]{:S(2)}, u32[]{:S(2)}) collective-permute-start(bf16[480,512]{1,0:T(8,128)(2,1)S(1)} %copy-done.10), channel_id=1, source_target_pairs={{0,18},{1,19},{2,0},{3,1},{4,22},{5,23},{6,4},{7,5},{8,10},{9,11},... | collective-permute-start | bytes 1474568 | tf_op jit(solution)/shard_map/ppermute | solution.py:859
  55.6 0.6 reshape.105.mask
  56.2 16.9 %attention_forward.1 = (bf16[1600,1536]{1,0:T(8,128)(2,1)}, bf16[1600,512]{1,0:T(8,128)(2,1)}, f32[8,8,200]{2,1,0:T(8,128)}, f32[1600,512]{1,0:T(8,128)}, bf16[1600,512]{1,0:T(8,128)(2,1)}) custom-call(bf16[1600,512]{1,0:T(8,128)(2,1)} %x.3, s32[8,1,200]{2,1,0:T(1,128)} %reshape.105.mask, bf16[512,2176]{1,0:T(8,128)(2,1)} %pad_maximum_fusion.small.wqkv.wout.refs_3_.refs_2_, ...), custom_call_target="tpu_custom_call" | custom-call | flops 170000000 | bytes 170000 | tf_op jit(solution)/shard_map/attention_forward/pallas_call | solution.py:331
  73.1 6.0 %dispatch.4 = bf16[8,208,512]{2,1,0:T(8,128)(2,1)} custom-call(s32[2,1600]{1,0:T(2,128)} %get-tuple-element.78.slot_rows, s32[2,1600]{1,0:T(2,128)} %bitcast.60, bf16[1600,512]{1,0:T(8,128)(2,1)} %get-tuple-element.81.refs_0_), custom_call_target="tpu_custom_call" | custom-call | flops 100000000 | bytes 100000 | tf_op jit(solution)/shard_map/dispatch/pallas_call | solution.py:255
  79.1 5.3 %collective-permute-done.5 = bf16[480,512]{1,0:T(8,128)(2,1)S(1)} collective-permute-done((bf16[480,512]{1,0:T(8,128)(2,1)S(1)}, bf16[480,512]{1,0:T(8,128)(2,1)S(1)}, u32[]{:S(2)}, u32[]{:S(2)}) %collective-permute-start.5) | collective-permute-done | bytes 491552 | tf_op jit(solution)/shard_map/ppermute | solution.py:859
  84.4 0.7 copy-done.12
  85.2 6.0 %all-to-all-start.1 = ((bf16[8,208,512]{2,1,0:T(8,128)(2,1)}), bf16[8,208,512]{2,1,0:T(8,128)(2,1)S(1)}, u32[]{:S(2)}, u32[]{:S(2)}) async-start(bf16[8,208,512]{2,1,0:T(8,128)(2,1)} %dispatch.4), calls=%async_computation.1 | async-start | bytes 3407872 | tf_op jit(solution)/shard_map/all_to_all | solution.py:878
  91.1 2.2 broadcast_select_fusion.12
  93.4 0.5 collective-permute-start.10
  93.9 1.3 broadcast_select_fusion.2
  95.2 0.1 collective-permute-start.7
  95.3 0.5 collective-permute-start.8
  95.8 10.6 %dispatch.5 = bf16[8,400,512]{2,1,0:T(8,128)(2,1)} custom-call(s32[2,1600]{1,0:T(2,128)} %get-tuple-element.78.slot_rows, s32[2,1600]{1,0:T(2,128)} %bitcast.61, bf16[1600,512]{1,0:T(8,128)(2,1)} %get-tuple-element.81.refs_0_, bf16[1600,512]{1,0:T(8,128)(2,1)} %up.1), custom_call_target="tpu_custom_call" | custom-call | flops 100000000 | bytes 100000 | tf_op jit(solution)/shard_map/dispatch/pallas_call | solution.py:255
  106.4 0.7 fusion.2
  107.1 0.6 pad_maximum_fusion.4
  107.7 3.5 maximum_maximum_fusion.refs_4_.refs_5_.refs_6_.refs_3_
  111.2 2.8 all-to-all-done.1
  114.0 1.2 copy-done.3
  115.2 4.7 %all-to-all-start.2 = ((bf16[8,400,512]{2,1,0:T(8,128)(2,1)}), bf16[8,400,512]{2,1,0:T(8,128)(2,1)S(1)}, u32[]{:S(2)}, u32[]{:S(2)}) async-start(bf16[8,400,512]{2,1,0:T(8,128)(2,1)} %dispatch.5), calls=%async_computation.2 | async-start | bytes 6553600 | tf_op jit(solution)/shard_map/all_to_all | solution.py:878
  119.9 0.5 compare_convert_fusion.refs_2_.refs_1_
  120.4 41.5 %experts.2 = (bf16[8,416,512]{2,1,0:T(8,128)(2,1)}, bf16[2,1040,512]{2,1,0:T(8,128)(2,1)}, bf16[2,1040,512]{2,1,0:T(8,128)(2,1)}, f32[512,128]{1,0:T(8,128)}) custom-call(bf16[1664,512]{1,0:T(8,128)(2,1)} %bitcast.48, bf16[8,224,512]{2,1,0:T(8,128)(2,1)} %copy-done.2, f32[1,128]{1,0:T(1,128)} %compare_convert_fusion.refs_2_.refs_1_, ...), custom_call_target="tpu_custom_call" | custom-call | flops 500000000 | bytes 500000 | tf_op jit(solution)/shard_map/experts/pallas_call | solution.py:541
  161.9 0.8 all-to-all-done.2.refs_0_
  162.8 1.7 copy-done.1
  164.5 5.3 %all-to-all-start.3 = ((bf16[8,416,512]{2,1,0:T(8,128)(2,1)}), bf16[8,416,512]{2,1,0:T(8,128)(2,1)S(1)}, u32[]{:S(2)}, u32[]{:S(2)}) async-start(bf16[8,416,512]{2,1,0:T(8,128)(2,1)} %get-tuple-element.100), calls=%async_computation.3 | async-start | bytes 6815744 | tf_op jit(solution)/shard_map/all_to_all | solution.py:878
  169.8 39.8 %experts.3 = (bf16[8,192,512]{2,1,0:T(8,128)(2,1)}, bf16[8,192,512]{2,1,0:T(8,128)(2,1)}, bf16[2,1040,512]{2,1,0:T(8,128)(2,1)}, bf16[2,1040,512]{2,1,0:T(8,128)(2,1)}, f32[512,128]{1,0:T(8,128)}) custom-call(bf16[8,400,512]{2,1,0:T(8,128)(2,1)} %copy-done.1, f32[1,128]{1,0:T(1,128)} %compare_convert_fusion.refs_2_.refs_1_, ...), custom_call_target="tpu_custom_call" | custom-call | flops 500000000 | bytes 500000 | tf_op jit(solution)/shard_map/experts/pallas_call | solution.py:541
  209.6 0.1 collective-permute-start.11
  209.6 3.8 %all-to-all-done.3 = bf16[8,416,512]{2,1,0:T(8,128)(2,1)S(1)} async-done(((bf16[8,416,512]{2,1,0:T(8,128)(2,1)}), bf16[8,416,512]{2,1,0:T(8,128)(2,1)S(1)}, u32[]{:S(2)}, u32[]{:S(2)}) %all-to-all-start.3) | async-done | bytes 3407904 | tf_op jit(solution)/shard_map/all_to_all | solution.py:878
  213.4 5.8 %all-to-all-start.4 = ((bf16[8,192,512]{2,1,0:T(8,128)(2,1)}), bf16[8,192,512]{2,1,0:T(8,128)(2,1)}, u32[]{:S(2)}, u32[]{:S(2)}) async-start(bf16[8,192,512]{2,1,0:T(8,128)(2,1)} %get-tuple-element.105), calls=%async_computation.4 | async-start | bytes 3145728 | tf_op jit(solution)/shard_map/all_to_all | solution.py:878
  219.2 4.4 %broadcast_select_fusion = (bf16[1040,512]{1,0:T(8,128)(2,1)}, bf16[1040,512]{1,0:T(8,128)(2,1)}, bf16[1040,512]{1,0:T(8,128)(2,1)}) fusion(pred[]{:T(512)S(6)} %ne.53, bf16[2,1040,512]{2,1,0:T(8,128)(2,1)} %collective-permute-done.11, bf16[2,1040,512]{2,1,0:T(8,128)(2,1)} %get-tuple-element.107), kind=kLoop, calls=%fused_computation.11 | loop fusion | flops 4792320 | bytes 7454721 | tf_op jit(solution)/shard_map/jit(_where)/select_n | solution.py:932
  223.6 15.4 %all-to-all-done.4.ret_b = bf16[8,192,512]{2,1,0:T(8,128)(2,1)} async-done(((bf16[8,192,512]{2,1,0:T(8,128)(2,1)}), bf16[8,192,512]{2,1,0:T(8,128)(2,1)}, u32[]{:S(2)}, u32[]{:S(2)}) %all-to-all-start.4) | async-done | bytes 1572896 | tf_op jit(solution)/shard_map/all_to_all | solution.py:878
  239.0 0.4 collective-permute-start.12
  239.4 1.6 collective-permute-start.13
  241.1 7.6 %all-to-all-start.5 = ((bf16[8,192,512]{2,1,0:T(8,128)(2,1)}), bf16[8,192,512]{2,1,0:T(8,128)(2,1)S(1)}, u32[]{:S(2)}, u32[]{:S(2)}) async-start(bf16[8,192,512]{2,1,0:T(8,128)(2,1)} %get-tuple-element.119), calls=%async_computation.5 | async-start | bytes 3145728 | tf_op jit(solution)/shard_map/all_to_all | solution.py:878
  248.7 41.4 %attention_backward.1 = (f32[1600,512]{1,0:T(8,128)}, bf16[256,2176]{1,0:T(8,128)(2,1)}, bf16[128,2176]{1,0:T(8,128)(2,1)}, bf16[128,2176]{1,0:T(8,128)(2,1)}) custom-call(bf16[1600,512]{1,0:T(8,128)(2,1)} %x.3, s32[8,1,200]{2,1,0:T(1,128)} %reshape.105.mask, bf16[512,2176]{1,0:T(8,128)(2,1)} %pad_maximum_fusion.small.wqkv.wout.refs_3_.refs_2_, ...), custom_call_target="tpu_custom_call" | custom-call | flops 500000000 | bytes 500000 | tf_op jit(solution)/shard_map/attention_backward/pallas_call | solution.py:681
  290.2 0.5 collective-permute-start.15
  290.7 1.7 collective-permute-done.14
  292.3 0.8 collective-permute-done.15
  293.1 1.5 select_convert_fusion
  294.6 7.1 %collective-permute-start.16 = (bf16[128,2176]{1,0:T(8,128)(2,1)S(1)}, bf16[128,2176]{1,0:T(8,128)(2,1)S(1)}, u32[]{:S(2)}, u32[]{:S(2)}) collective-permute-start(bf16[128,2176]{1,0:T(8,128)(2,1)S(1)} %select_convert_fusion), channel_id=1, source_target_pairs={{0,2},{1,3},{2,0},{3,1},{4,6},{5,7},{6,4},{7,5},{8,10},{9,11},{10,... | collective-permute-start | bytes 1671176 | tf_op jit(solution)/shard_map/ppermute | solution.py:859
  301.7 12.9 %collective-permute-done.16 = bf16[128,2176]{1,0:T(8,128)(2,1)S(1)} collective-permute-done((bf16[128,2176]{1,0:T(8,128)(2,1)S(1)}, bf16[128,2176]{1,0:T(8,128)(2,1)S(1)}, u32[]{:S(2)}, u32[]{:S(2)}) %collective-permute-start.16) | collective-permute-done | bytes 557088 | tf_op jit(solution)/shard_map/ppermute | solution.py:859
  314.7 1.2 add_convert_fusion.2
  315.8 9.8 %all-to-all-start.6 = ((bf16[8,16,2176]{2,1,0:T(8,128)(2,1)}), bf16[8,16,2176]{2,1,0:T(8,128)(2,1)S(1)}, u32[]{:S(2)}, u32[]{:S(2)}) async-start(bf16[8,16,2176]{2,1,0:T(8,128)(2,1)} %bitcast.27), calls=%async_computation.6 | async-start | bytes 1114112 | tf_op jit(solution)/shard_map/all_to_all | solution.py:962
  325.7 14.9 %all-to-all-done.6 = bf16[8,16,2176]{2,1,0:T(8,128)(2,1)S(1)} async-done(((bf16[8,16,2176]{2,1,0:T(8,128)(2,1)}), bf16[8,16,2176]{2,1,0:T(8,128)(2,1)S(1)}, u32[]{:S(2)}, u32[]{:S(2)}) %all-to-all-start.6) | async-done | bytes 557088 | tf_op jit(solution)/shard_map/all_to_all | solution.py:962
  340.6 0.1 reduce_sum.12
  340.6 0.8 broadcast_in_dim.34
  341.5 3.6 all-to-all-start.7
  345.1 1.7 convert_add_fusion
  346.8 0.6 fusion.9
  347.4 0.5 constant_dynamic-slice_fusion
  347.9 1.5 slice_bitcast_fusion
  349.4 11.0 %combine.1 = bf16[1600,512]{1,0:T(8,128)(2,1)} custom-call(s32[1600,2]{1,0:T(8,128)} %get-tuple-element.73.slot, f32[1600,512]{1,0:T(8,128)} %get-tuple-element.80.residual, bf16[8,2,208,512]{3,2,1,0:T(8,128)(2,1)} %bitcast.47, bf16[8,192,512]{2,1,0:T(8,128)(2,1)} %copy-done.4), custom_call_target="tpu_custom_call" | custom-call | flops 100000000 | bytes 100000 | tf_op jit(solution)/shard_map/combine/pallas_call | solution.py:738
  360.4 0.8 copy-done.7
  361.2 2.0 unpack.1
  (45 shorter events, 0.2 us)
Async XLA Ops:
  3.3 39.8 %copy-start.9 = (bf16[128,2176]{1,0:T(8,128)(2,1)S(1)}, bf16[128,2176]{1,0:T(8,128)(2,1)}, u32[]{:S(2)}) copy-start(bf16[128,2176]{1,0:T(8,128)(2,1)} %get-tuple-element.74) | copy-start | bytes 1671172
  3.3 32.5 %collective-permute-start.2 = (bf16[560,512]{1,0:T(8,128)(2,1)}, bf16[560,512]{1,0:T(8,128)(2,1)}, u32[]{:S(2)}, u32[]{:S(2)}) collective-permute-start(bf16[560,512]{1,0:T(8,128)(2,1)} %get-tuple-element.76), channel_id=1, source_target_pairs={{2,18},{3,19},{6,22},{7,23},{8,24},{9,25},{12,28},{13,29},{18,2},{... | collective-permute-start | bytes 1720328 | tf_op jit(solution)/shard_map/ppermute | solution.py:859
  4.9 30.9 %collective-permute-start.1 = (bf16[560,512]{1,0:T(8,128)(2,1)}, bf16[560,512]{1,0:T(8,128)(2,1)}, u32[]{:S(2)}, u32[]{:S(2)}) collective-permute-start(bf16[560,512]{1,0:T(8,128)(2,1)} %get-tuple-element.76), channel_id=1, source_target_pairs={{0,18},{1,19},{2,0},{3,1},{4,22},{5,23},{6,4},{7,5},{8,10},{9,11},... | collective-permute-start | bytes 1720328 | tf_op jit(solution)/shard_map/ppermute | solution.py:859
  10.7 25.1 %collective-permute-start = (bf16[128,2176]{1,0:T(8,128)(2,1)}, bf16[128,2176]{1,0:T(8,128)(2,1)S(1)}, u32[]{:S(2)}, u32[]{:S(2)}) collective-permute-start(bf16[128,2176]{1,0:T(8,128)(2,1)} %get-tuple-element.74), channel_id=1, source_target_pairs={{0,2},{1,3},{2,0},{3,1},{4,6},{5,7},{6,4},{7,5},{8,10},{9,11},{10,... | collective-permute-start | bytes 1671176 | tf_op jit(solution)/shard_map/ppermute | solution.py:859
  11.0 32.1 %collective-permute-start.3 = (bf16[128,2176]{1,0:T(8,128)(2,1)}, bf16[128,2176]{1,0:T(8,128)(2,1)S(1)}, u32[]{:S(2)}, u32[]{:S(2)}) collective-permute-start(bf16[128,2176]{1,0:T(8,128)(2,1)} %get-tuple-element.74), channel_id=1, source_target_pairs={{0,1},{1,0},{2,3},{3,2},{4,5},{5,4},{6,7},{7,6},{8,9},{9,8},{10,11... | collective-permute-start | bytes 1671176 | tf_op jit(solution)/shard_map/ppermute | solution.py:859
  35.8 7.4 %collective-permute-start.4 = (bf16[128,2176]{1,0:T(8,128)(2,1)S(1)}, bf16[128,2176]{1,0:T(8,128)(2,1)S(1)}, u32[]{:S(2)}, u32[]{:S(2)}) collective-permute-start(bf16[128,2176]{1,0:T(8,128)(2,1)S(1)} %collective-permute-done), channel_id=1, source_target_pairs={{0,1},{1,0},{2,3},{3,2},{4,5},{5,4},{6,7},{7,6},{8,9},{9,8},{10,11... | collective-permute-start | bytes 1671176 | tf_op jit(solution)/shard_map/ppermute | solution.py:859
  45.0 4.3 %copy-start.10 = (bf16[480,512]{1,0:T(8,128)(2,1)S(1)}, bf16[480,512]{1,0:T(8,128)(2,1)}, u32[]{:S(2)}) copy-start(bf16[480,512]{1,0:T(8,128)(2,1)} %get-tuple-element.83) | copy-start | bytes 1474564
  45.0 10.6 %copy-start.13 = (s32[8,200]{1,0:T(8,128)S(1)}, s32[8,200]{1,0:T(8,128)}, u32[]{:S(2)}) copy-start(s32[8,200]{1,0:T(8,128)} %param.18) | copy-start | bytes 19204
  45.0 39.4 %all-to-all-start = ((bf16[8,224,512]{2,1,0:T(8,128)(2,1)}), bf16[8,224,512]{2,1,0:T(8,128)(2,1)S(1)}, u32[]{:S(2)}, u32[]{:S(2)}) async-start(bf16[8,224,512]{2,1,0:T(8,128)(2,1)} %dispatch.3), calls=%async_computation | async-start | bytes 3670016 | tf_op jit(solution)/shard_map/all_to_all | solution.py:878
  49.3 29.8 %collective-permute-start.6 = (bf16[480,512]{1,0:T(8,128)(2,1)S(1)}, bf16[480,512]{1,0:T(8,128)(2,1)S(1)}, u32[]{:S(2)}, u32[]{:S(2)}) collective-permute-start(bf16[480,512]{1,0:T(8,128)(2,1)S(1)} %copy-done.10), channel_id=1, source_target_pairs={{2,18},{3,19},{6,22},{7,23},{8,24},{9,25},{12,28},{13,29},{18,2},{... | collective-permute-start | bytes 1474568 | tf_op jit(solution)/shard_map/ppermute | solution.py:859
  50.0 34.4 %collective-permute-start.5 = (bf16[480,512]{1,0:T(8,128)(2,1)S(1)}, bf16[480,512]{1,0:T(8,128)(2,1)S(1)}, u32[]{:S(2)}, u32[]{:S(2)}) collective-permute-start(bf16[480,512]{1,0:T(8,128)(2,1)S(1)} %copy-done.10), channel_id=1, source_target_pairs={{0,18},{1,19},{2,0},{3,1},{4,22},{5,23},{6,4},{7,5},{8,10},{9,11},... | collective-permute-start | bytes 1474568 | tf_op jit(solution)/shard_map/ppermute | solution.py:859
  79.1 5.3 %copy-start.11 = (bf16[480,512]{1,0:T(8,128)(2,1)}, bf16[480,512]{1,0:T(8,128)(2,1)S(1)}, u32[]{:S(2)}) copy-start(bf16[480,512]{1,0:T(8,128)(2,1)S(1)} %collective-permute-done.6) | copy-start | bytes 1474564
  84.4 0.8 copy-start.12
  84.4 8.9 %copy-start.2 = (bf16[8,224,512]{2,1,0:T(8,128)(2,1)}, bf16[8,224,512]{2,1,0:T(8,128)(2,1)S(1)}, u32[]{:S(2)}) copy-start(bf16[8,224,512]{2,1,0:T(8,128)(2,1)S(1)} %all-to-all-done.refs_1_) | copy-start | bytes 5505028
  85.2 28.8 %all-to-all-start.1 = ((bf16[8,208,512]{2,1,0:T(8,128)(2,1)}), bf16[8,208,512]{2,1,0:T(8,128)(2,1)S(1)}, u32[]{:S(2)}, u32[]{:S(2)}) async-start(bf16[8,208,512]{2,1,0:T(8,128)(2,1)} %dispatch.4), calls=%async_computation.1 | async-start | bytes 3407872 | tf_op jit(solution)/shard_map/all_to_all | solution.py:878
  93.4 13.0 %collective-permute-start.9 = (bf16[480,512]{1,0:T(8,128)(2,1)}, bf16[480,512]{1,0:T(8,128)(2,1)S(1)}, u32[]{:S(2)}, u32[]{:S(2)}) collective-permute-start(bf16[480,512]{1,0:T(8,128)(2,1)} %get-tuple-element.146), channel_id=1, source_target_pairs={{0,1},{1,0},{2,3},{3,2},{4,5},{5,4},{6,7},{7,6},{8,9},{9,8},{10,11... | collective-permute-start | bytes 1474568 | tf_op jit(solution)/shard_map/ppermute | solution.py:859
  93.4 13.0 %collective-permute-start.10 = (bf16[480,512]{1,0:T(8,128)(2,1)}, bf16[480,512]{1,0:T(8,128)(2,1)S(1)}, u32[]{:S(2)}, u32[]{:S(2)}) collective-permute-start(bf16[480,512]{1,0:T(8,128)(2,1)} %get-tuple-element.147), channel_id=1, source_target_pairs={{0,1},{1,0},{2,3},{3,2},{4,5},{5,4},{6,7},{7,6},{8,9},{9,8},{10,11... | collective-permute-start | bytes 1474568 | tf_op jit(solution)/shard_map/ppermute | solution.py:859
  95.2 12.5 %collective-permute-start.7 = (bf16[560,512]{1,0:T(8,128)(2,1)S(1)}, bf16[560,512]{1,0:T(8,128)(2,1)}, u32[]{:S(2)}, u32[]{:S(2)}) collective-permute-start(bf16[560,512]{1,0:T(8,128)(2,1)S(1)} %get-tuple-element.144), channel_id=1, source_target_pairs={{0,1},{1,0},{2,3},{3,2},{4,5},{5,4},{6,7},{7,6},{8,9},{9,8},{10,11... | collective-permute-start | bytes 1720328 | tf_op jit(solution)/shard_map/ppermute | solution.py:859
  95.3 12.4 %collective-permute-start.8 = (bf16[560,512]{1,0:T(8,128)(2,1)S(1)}, bf16[560,512]{1,0:T(8,128)(2,1)}, u32[]{:S(2)}, u32[]{:S(2)}) collective-permute-start(bf16[560,512]{1,0:T(8,128)(2,1)S(1)} %get-tuple-element.145), channel_id=1, source_target_pairs={{0,1},{1,0},{2,3},{3,2},{4,5},{5,4},{6,7},{7,6},{8,9},{9,8},{10,11... | collective-permute-start | bytes 1720328 | tf_op jit(solution)/shard_map/ppermute | solution.py:859
  114.0 1.2 copy-start.3
  115.2 47.5 %all-to-all-start.2 = ((bf16[8,400,512]{2,1,0:T(8,128)(2,1)}), bf16[8,400,512]{2,1,0:T(8,128)(2,1)S(1)}, u32[]{:S(2)}, u32[]{:S(2)}) async-start(bf16[8,400,512]{2,1,0:T(8,128)(2,1)} %dispatch.5), calls=%async_computation.2 | async-start | bytes 6553600 | tf_op jit(solution)/shard_map/all_to_all | solution.py:878
  162.8 1.7 copy-start.1
  164.5 48.9 %all-to-all-start.3 = ((bf16[8,416,512]{2,1,0:T(8,128)(2,1)}), bf16[8,416,512]{2,1,0:T(8,128)(2,1)S(1)}, u32[]{:S(2)}, u32[]{:S(2)}) async-start(bf16[8,416,512]{2,1,0:T(8,128)(2,1)} %get-tuple-element.100), calls=%async_computation.3 | async-start | bytes 6815744 | tf_op jit(solution)/shard_map/all_to_all | solution.py:878
  209.6 9.6 %collective-permute-start.11 = (bf16[2,1040,512]{2,1,0:T(8,128)(2,1)}, bf16[2,1040,512]{2,1,0:T(8,128)(2,1)}, u32[]{:S(2)}, u32[]{:S(2)}) collective-permute-start(bf16[2,1040,512]{2,1,0:T(8,128)(2,1)} %get-tuple-element.108), channel_id=1, source_target_pairs={{0,1},{1,0},{2,3},{3,2},{4,5},{5,4},{6,7},{7,6},{8,9},{9,8},{10,11... | collective-permute-start | bytes 6389768 | tf_op jit(solution)/shard_map/ppermute | solution.py:859
  213.4 10.2 %copy-start = (bf16[8,416,512]{2,1,0:T(8,128)(2,1)}, bf16[8,416,512]{2,1,0:T(8,128)(2,1)S(1)}, u32[]{:S(2)}) copy-start(bf16[8,416,512]{2,1,0:T(8,128)(2,1)S(1)} %all-to-all-done.3) | copy-start | bytes 10223620
  213.4 25.6 %all-to-all-start.4 = ((bf16[8,192,512]{2,1,0:T(8,128)(2,1)}), bf16[8,192,512]{2,1,0:T(8,128)(2,1)}, u32[]{:S(2)}, u32[]{:S(2)}) async-start(bf16[8,192,512]{2,1,0:T(8,128)(2,1)} %get-tuple-element.105), calls=%async_computation.4 | async-start | bytes 3145728 | tf_op jit(solution)/shard_map/all_to_all | solution.py:878
  239.0 51.1 %collective-permute-start.12 = (bf16[1040,512]{1,0:T(8,128)(2,1)}, bf16[1040,512]{1,0:T(8,128)(2,1)S(1)}, u32[]{:S(2)}, u32[]{:S(2)}) collective-permute-start(bf16[1040,512]{1,0:T(8,128)(2,1)} %get-tuple-element.114), channel_id=1, source_target_pairs={{18,0},{19,1},{0,2},{1,3},{22,4},{23,5},{4,6},{5,7},{10,8},{11,9},... | collective-permute-start | bytes 3194888 | tf_op jit(solution)/shard_map/ppermute | solution.py:859
  239.4 50.7 %collective-permute-start.13 = (bf16[1040,512]{1,0:T(8,128)(2,1)}, bf16[1040,512]{1,0:T(8,128)(2,1)}, u32[]{:S(2)}, u32[]{:S(2)}) collective-permute-start(bf16[1040,512]{1,0:T(8,128)(2,1)} %get-tuple-element.115), channel_id=1, source_target_pairs={{2,18},{3,19},{6,22},{7,23},{8,24},{9,25},{12,28},{13,29},{18,2},{... | collective-permute-start | bytes 3194888 | tf_op jit(solution)/shard_map/ppermute | solution.py:859
  241.1 74.8 %all-to-all-start.5 = ((bf16[8,192,512]{2,1,0:T(8,128)(2,1)}), bf16[8,192,512]{2,1,0:T(8,128)(2,1)S(1)}, u32[]{:S(2)}, u32[]{:S(2)}) async-start(bf16[8,192,512]{2,1,0:T(8,128)(2,1)} %get-tuple-element.119), calls=%async_computation.5 | async-start | bytes 3145728 | tf_op jit(solution)/shard_map/all_to_all | solution.py:878
  290.0 24.6 %copy-start.5 = (bf16[256,2176]{1,0:T(8,128)(2,1)S(1)}, bf16[256,2176]{1,0:T(8,128)(2,1)}, u32[]{:S(2)}) copy-start(bf16[256,2176]{1,0:T(8,128)(2,1)} %get-tuple-element.116) | copy-start | bytes 3342340
  290.1 24.6 %copy-start.8 = (bf16[1040,512]{1,0:T(8,128)(2,1)}, bf16[1040,512]{1,0:T(8,128)(2,1)S(1)}, u32[]{:S(2)}) copy-start(bf16[1040,512]{1,0:T(8,128)(2,1)S(1)} %collective-permute-done.12) | copy-start | bytes 3194884
  290.1 2.2 collective-permute-start.14
  290.2 3.0 collective-permute-start.15
  294.6 20.0 %collective-permute-start.16 = (bf16[128,2176]{1,0:T(8,128)(2,1)S(1)}, bf16[128,2176]{1,0:T(8,128)(2,1)S(1)}, u32[]{:S(2)}, u32[]{:S(2)}) collective-permute-start(bf16[128,2176]{1,0:T(8,128)(2,1)S(1)} %select_convert_fusion), channel_id=1, source_target_pairs={{0,2},{1,3},{2,0},{3,1},{4,6},{5,7},{6,4},{7,5},{8,10},{9,11},{10,... | collective-permute-start | bytes 1671176 | tf_op jit(solution)/shard_map/ppermute | solution.py:859
  315.8 29.3 %copy-start.6 = (bf16[1040,512]{1,0:T(8,128)(2,1)S(1)}, bf16[1040,512]{1,0:T(8,128)(2,1)}, u32[]{:S(2)}) copy-start(bf16[1040,512]{1,0:T(8,128)(2,1)} %get-tuple-element.130) | copy-start | bytes 3194884
  315.8 30.9 %copy-start.4 = (bf16[8,192,512]{2,1,0:T(8,128)(2,1)}, bf16[8,192,512]{2,1,0:T(8,128)(2,1)S(1)}, u32[]{:S(2)}) copy-start(bf16[8,192,512]{2,1,0:T(8,128)(2,1)S(1)} %all-to-all-done.5.ret_b) | copy-start | bytes 4718596
  315.8 24.7 %all-to-all-start.6 = ((bf16[8,16,2176]{2,1,0:T(8,128)(2,1)}), bf16[8,16,2176]{2,1,0:T(8,128)(2,1)S(1)}, u32[]{:S(2)}, u32[]{:S(2)}) async-start(bf16[8,16,2176]{2,1,0:T(8,128)(2,1)} %bitcast.27), calls=%async_computation.6 | async-start | bytes 1114112 | tf_op jit(solution)/shard_map/all_to_all | solution.py:962
  341.5 18.9 %all-to-all-start.7 = ((bf16[8,16,2176]{2,1,0:T(8,128)(2,1)}), bf16[8,16,2176]{2,1,0:T(8,128)(2,1)S(1)}, u32[]{:S(2)}, u32[]{:S(2)}) async-start(bf16[8,16,2176]{2,1,0:T(8,128)(2,1)} %broadcast_in_dim.34), calls=%async_computation.7 | async-start | bytes 1114112 | tf_op jit(solution)/shard_map/all_to_all | solution.py:962
  360.4 0.8 copy-start.7

commit v5 on v4

--- a/solution.py
+++ b/solution.py
@@ -135,7 +135,7 @@
     share, width = wout.shape
     hidden = w_in.shape[0]
     double = 2 * hidden + EXTRA
-    cuts = [0] + [double * part // 100 // EXTRA * EXTRA for part in (55,)] + [double]
+    cuts = [0] + [double * part // 100 // EXTRA * EXTRA for part in (47,)] + [double]
     sizes = [high - low for low, high in zip(cuts, cuts[1:])]
     return pl.pallas_call(
         pack_kernel,
@@ -505,7 +505,7 @@
             hid[at, 0:LANES] = spread
             return carry
 
-        lax.fori_loop(0, steps, step, 0, unroll=4)
+        lax.fori_loop(0, steps, step, 0, unroll=8)
         drouter[...] = mm_tn(rows[...], hid[:, 0:LANES]) + (0.0 if old is None else old[2][...])
 
 

time: 365 us -> 365 us (level)
    ppermute x17, waiting for transfers between devices: 37.6 us -> 32.8 us  [send(): return lax.ppermute(a, self.AXES, pairs)]
  transfers between devices with their start and end apart: 25 -> 25, of which waited for: 10 -> 11; matrix products, arithmetic and copies ran while one was open for 6% -> 6% of each run, Pallas kernels for 50% -> 50%
where the time goes in v5:
time: 365 us; the launch traced here: 363 us
  Pallas kernels  186 us (51%)
  starting transfers between devices  75.5 us (21%)
  waiting for transfers between devices  71.7 us (20%)
  other arithmetic  19.4 us (5%)
  local copies, waits for them, and re-layouts  10.1 us (3%)
    pallas_call x2, Pallas kernels, run_experts(): pl.pallas_call(partial(experts_kernel, block, bool(old)), grid=(steps,),...  80 us
    pallas_call x1, Pallas kernels, attention_backward(): pl.pallas_call(partial(backward_kernel, experts), grid=(images,), in_spec...  41.4 us
    all_to_all x6, starting transfers between devices, exchange(): lax.all_to_all(a, self.AXES, split_axis=0, concat_axis=0, axis_index_grou...  37.1 us
    ppermute x17, waiting for transfers between devices, send(): return lax.ppermute(a, self.AXES, pairs)  32.8 us
    ppermute x17, starting transfers between devices, send(): return lax.ppermute(a, self.AXES, pairs)  25.2 us
    pallas_call x3, Pallas kernels, dispatch(): pl.pallas_call(partial(dispatch_kernel, start, size, with_other), grid=(e...  23.9 us
    all_to_all x6, waiting for transfers between devices, exchange(): lax.all_to_all(a, self.AXES, split_axis=0, concat_axis=0, axis_index_grou...  23.7 us
    pallas_call x1, Pallas kernels, attention_forward(): pl.pallas_call(partial(attention_kernel, experts), grid=(images,), in_spe...  16.9 us
  transfers between devices with their start and end apart: 25, of which 11 were waited for; matrix products, arithmetic and copies ran while one was open for 6% of the time, Pallas kernels for 50%

profile of v5, /device:TPU:0, one launch (start us, length us, event | category | flops | bytes accessed | tf_op | source)
XLA Modules:
  0.0 363.3 jit_solution(12752727774007029187)
XLA Ops:
  0.7 2.7 pack.1
  3.3 2.9 collective-permute-start
  6.3 0.7 collective-permute-start.2
  7.0 3.8 %collective-permute-start.1 = (bf16[480,512]{1,0:T(8,128)(2,1)}, bf16[480,512]{1,0:T(8,128)(2,1)S(1)}, u32[]{:S(2)}, u32[]{:S(2)}) collective-permute-start(bf16[480,512]{1,0:T(8,128)(2,1)} %get-tuple-element.76), channel_id=1, source_target_pairs={{0,18},{1,19},{2,0},{3,1},{4,22},{5,23},{6,4},{7,5},{8,10},{9,11},... | collective-permute-start | bytes 1474568 | tf_op jit(solution)/shard_map/ppermute | solution.py:859
  10.8 7.9 %slots.1 = (s32[1600,2]{1,0:T(8,128)}, s32[2,1600]{1,0:T(2,128)}) custom-call(s32[1,1600]{1,0:T(1,128)} %prow.1, s32[2,1600]{1,0:T(2,128)} %bitcast.58, s32[1,8]{1,0:T(1,128)} %bitcast.70), custom_call_target="tpu_custom_call" | custom-call | flops 80000000 | bytes 80000 | tf_op jit(solution)/shard_map/slots/pallas_call | solution.py:208
  18.7 11.0 %collective-permute-done.1 = bf16[480,512]{1,0:T(8,128)(2,1)S(1)} collective-permute-done((bf16[480,512]{1,0:T(8,128)(2,1)}, bf16[480,512]{1,0:T(8,128)(2,1)S(1)}, u32[]{:S(2)}, u32[]{:S(2)}) %collective-permute-start.1) | collective-permute-done | bytes 491552 | tf_op jit(solution)/shard_map/ppermute | solution.py:859
  29.7 0.8 copy-done.14
  30.5 7.3 %dispatch.3 = bf16[8,224,512]{2,1,0:T(8,128)(2,1)} custom-call(s32[2,1600]{1,0:T(2,128)} %get-tuple-element.78.slot_rows, s32[2,1600]{1,0:T(2,128)} %bitcast.59, bf16[1600,512]{1,0:T(8,128)(2,1)} %up.1), custom_call_target="tpu_custom_call" | custom-call | flops 100000000 | bytes 100000 | tf_op jit(solution)/shard_map/dispatch/pallas_call | solution.py:255
  37.8 0.3 broadcast_select_fusion.10
  38.1 1.5 pad_maximum_fusion.small.wqkv.wout.refs_3_.refs_2_
  39.6 7.6 %all-to-all-start = ((bf16[8,224,512]{2,1,0:T(8,128)(2,1)}), bf16[8,224,512]{2,1,0:T(8,128)(2,1)S(1)}, u32[]{:S(2)}, u32[]{:S(2)}) async-start(bf16[8,224,512]{2,1,0:T(8,128)(2,1)} %dispatch.3), calls=%async_computation | async-start | bytes 3670016 | tf_op jit(solution)/shard_map/all_to_all | solution.py:878
  47.3 0.7 collective-permute-start.6
  48.0 5.6 %collective-permute-start.5 = (bf16[560,512]{1,0:T(8,128)(2,1)S(1)}, bf16[560,512]{1,0:T(8,128)(2,1)S(1)}, u32[]{:S(2)}, u32[]{:S(2)}) collective-permute-start(bf16[560,512]{1,0:T(8,128)(2,1)S(1)} %copy-done.9), channel_id=1, source_target_pairs={{0,18},{1,19},{2,0},{3,1},{4,22},{5,23},{6,4},{7,5},{8,10},{9,11},... | collective-permute-start | bytes 1720328 | tf_op jit(solution)/shard_map/ppermute | solution.py:859
  53.6 1.3 reshape.105.mask
  54.9 16.9 %attention_forward.1 = (bf16[1600,1536]{1,0:T(8,128)(2,1)}, bf16[1600,512]{1,0:T(8,128)(2,1)}, f32[8,8,200]{2,1,0:T(8,128)}, f32[1600,512]{1,0:T(8,128)}, bf16[1600,512]{1,0:T(8,128)(2,1)}) custom-call(bf16[1600,512]{1,0:T(8,128)(2,1)} %x.3, s32[8,1,200]{2,1,0:T(1,128)} %reshape.105.mask, bf16[512,2176]{1,0:T(8,128)(2,1)} %pad_maximum_fusion.small.wqkv.wout.refs_3_.refs_2_, ...), custom_call_target="tpu_custom_call" | custom-call | flops 170000000 | bytes 170000 | tf_op jit(solution)/shard_map/attention_forward/pallas_call | solution.py:331
  71.8 6.0 %dispatch.4 = bf16[8,208,512]{2,1,0:T(8,128)(2,1)} custom-call(s32[2,1600]{1,0:T(2,128)} %get-tuple-element.78.slot_rows, s32[2,1600]{1,0:T(2,128)} %bitcast.60, bf16[1600,512]{1,0:T(8,128)(2,1)} %get-tuple-element.81.refs_0_), custom_call_target="tpu_custom_call" | custom-call | flops 100000000 | bytes 100000 | tf_op jit(solution)/shard_map/dispatch/pallas_call | solution.py:255
  77.8 6.4 %collective-permute-done.5 = bf16[560,512]{1,0:T(8,128)(2,1)S(1)} collective-permute-done((bf16[560,512]{1,0:T(8,128)(2,1)S(1)}, bf16[560,512]{1,0:T(8,128)(2,1)S(1)}, u32[]{:S(2)}, u32[]{:S(2)}) %collective-permute-start.5) | collective-permute-done | bytes 573472 | tf_op jit(solution)/shard_map/ppermute | solution.py:859
  84.2 0.8 copy-done.11
  85.0 5.7 %all-to-all-start.1 = ((bf16[8,208,512]{2,1,0:T(8,128)(2,1)}), bf16[8,208,512]{2,1,0:T(8,128)(2,1)S(1)}, u32[]{:S(2)}, u32[]{:S(2)}) async-start(bf16[8,208,512]{2,1,0:T(8,128)(2,1)} %dispatch.4), calls=%async_computation.1 | async-start | bytes 3407872 | tf_op jit(solution)/shard_map/all_to_all | solution.py:878
  90.7 2.3 broadcast_select_fusion.2
  93.1 0.5 collective-permute-start.10
  93.6 1.3 broadcast_select_fusion.12
  94.8 0.1 collective-permute-start.7
  94.9 0.5 collective-permute-start.8
  95.4 10.6 %dispatch.5 = bf16[8,400,512]{2,1,0:T(8,128)(2,1)} custom-call(s32[2,1600]{1,0:T(2,128)} %get-tuple-element.78.slot_rows, s32[2,1600]{1,0:T(2,128)} %bitcast.61, bf16[1600,512]{1,0:T(8,128)(2,1)} %get-tuple-element.81.refs_0_, bf16[1600,512]{1,0:T(8,128)(2,1)} %up.1), custom_call_target="tpu_custom_call" | custom-call | flops 100000000 | bytes 100000 | tf_op jit(solution)/shard_map/dispatch/pallas_call | solution.py:255
  106.0 0.7 fusion.2
  106.7 0.6 pad_maximum_fusion.4
  107.3 3.4 maximum_maximum_fusion.refs_4_.refs_5_.refs_6_.refs_3_
  110.7 2.5 all-to-all-done.1
  113.2 1.2 copy-done.3
  114.5 5.0 %all-to-all-start.2 = ((bf16[8,400,512]{2,1,0:T(8,128)(2,1)}), bf16[8,400,512]{2,1,0:T(8,128)(2,1)S(1)}, u32[]{:S(2)}, u32[]{:S(2)}) async-start(bf16[8,400,512]{2,1,0:T(8,128)(2,1)} %dispatch.5), calls=%async_computation.2 | async-start | bytes 6553600 | tf_op jit(solution)/shard_map/all_to_all | solution.py:878
  119.5 0.5 compare_convert_fusion.refs_2_.refs_1_
  120.0 40.8 %experts.2 = (bf16[8,416,512]{2,1,0:T(8,128)(2,1)}, bf16[2,1040,512]{2,1,0:T(8,128)(2,1)}, bf16[2,1040,512]{2,1,0:T(8,128)(2,1)}, f32[512,128]{1,0:T(8,128)}) custom-call(bf16[1664,512]{1,0:T(8,128)(2,1)} %bitcast.48, bf16[8,224,512]{2,1,0:T(8,128)(2,1)} %copy-done.2, f32[1,128]{1,0:T(1,128)} %compare_convert_fusion.refs_2_.refs_1_, ...), custom_call_target="tpu_custom_call" | custom-call | flops 500000000 | bytes 500000 | tf_op jit(solution)/shard_map/experts/pallas_call | solution.py:541
  160.8 1.5 all-to-all-done.2.refs_0_
  162.3 1.7 copy-done.1
  164.0 5.4 %all-to-all-start.3 = ((bf16[8,416,512]{2,1,0:T(8,128)(2,1)}), bf16[8,416,512]{2,1,0:T(8,128)(2,1)S(1)}, u32[]{:S(2)}, u32[]{:S(2)}) async-start(bf16[8,416,512]{2,1,0:T(8,128)(2,1)} %get-tuple-element.100), calls=%async_computation.3 | async-start | bytes 6815744 | tf_op jit(solution)/shard_map/all_to_all | solution.py:878
  169.3 39.2 %experts.3 = (bf16[8,192,512]{2,1,0:T(8,128)(2,1)}, bf16[8,192,512]{2,1,0:T(8,128)(2,1)}, bf16[2,1040,512]{2,1,0:T(8,128)(2,1)}, bf16[2,1040,512]{2,1,0:T(8,128)(2,1)}, f32[512,128]{1,0:T(8,128)}) custom-call(bf16[8,400,512]{2,1,0:T(8,128)(2,1)} %copy-done.1, f32[1,128]{1,0:T(1,128)} %compare_convert_fusion.refs_2_.refs_1_, ...), custom_call_target="tpu_custom_call" | custom-call | flops 500000000 | bytes 500000 | tf_op jit(solution)/shard_map/experts/pallas_call | solution.py:541
  208.6 4.3 %all-to-all-done.3 = bf16[8,416,512]{2,1,0:T(8,128)(2,1)S(1)} async-done(((bf16[8,416,512]{2,1,0:T(8,128)(2,1)}), bf16[8,416,512]{2,1,0:T(8,128)(2,1)S(1)}, u32[]{:S(2)}, u32[]{:S(2)}) %all-to-all-start.3) | async-done | bytes 3407904 | tf_op jit(solution)/shard_map/all_to_all | solution.py:878
  212.9 5.8 %all-to-all-start.4 = ((bf16[8,192,512]{2,1,0:T(8,128)(2,1)}), bf16[8,192,512]{2,1,0:T(8,128)(2,1)}, u32[]{:S(2)}, u32[]{:S(2)}) async-start(bf16[8,192,512]{2,1,0:T(8,128)(2,1)} %get-tuple-element.105), calls=%async_computation.4 | async-start | bytes 3145728 | tf_op jit(solution)/shard_map/all_to_all | solution.py:878
  218.7 4.4 %broadcast_select_fusion = (bf16[1040,512]{1,0:T(8,128)(2,1)}, bf16[1040,512]{1,0:T(8,128)(2,1)}, bf16[1040,512]{1,0:T(8,128)(2,1)}) fusion(pred[]{:T(512)S(6)} %ne.53, bf16[2,1040,512]{2,1,0:T(8,128)(2,1)} %collective-permute-done.11, bf16[2,1040,512]{2,1,0:T(8,128)(2,1)} %get-tuple-element.107), kind=kLoop, calls=%fused_computation.11 | loop fusion | flops 4792320 | bytes 7454721 | tf_op jit(solution)/shard_map/jit(_where)/select_n | solution.py:932
  223.1 15.4 %all-to-all-done.4.ret_b = bf16[8,192,512]{2,1,0:T(8,128)(2,1)} async-done(((bf16[8,192,512]{2,1,0:T(8,128)(2,1)}), bf16[8,192,512]{2,1,0:T(8,128)(2,1)}, u32[]{:S(2)}, u32[]{:S(2)}) %all-to-all-start.4) | async-done | bytes 1572896 | tf_op jit(solution)/shard_map/all_to_all | solution.py:878
  238.5 0.4 collective-permute-start.12
  238.9 1.6 collective-permute-start.13
  240.6 7.6 %all-to-all-start.5 = ((bf16[8,192,512]{2,1,0:T(8,128)(2,1)}), bf16[8,192,512]{2,1,0:T(8,128)(2,1)S(1)}, u32[]{:S(2)}, u32[]{:S(2)}) async-start(bf16[8,192,512]{2,1,0:T(8,128)(2,1)} %get-tuple-element.119), calls=%async_computation.5 | async-start | bytes 3145728 | tf_op jit(solution)/shard_map/all_to_all | solution.py:878
  248.2 41.4 %attention_backward.1 = (f32[1600,512]{1,0:T(8,128)}, bf16[256,2176]{1,0:T(8,128)(2,1)}, bf16[128,2176]{1,0:T(8,128)(2,1)}, bf16[128,2176]{1,0:T(8,128)(2,1)}) custom-call(bf16[1600,512]{1,0:T(8,128)(2,1)} %x.3, s32[8,1,200]{2,1,0:T(1,128)} %reshape.105.mask, bf16[512,2176]{1,0:T(8,128)(2,1)} %pad_maximum_fusion.small.wqkv.wout.refs_3_.refs_2_, ...), custom_call_target="tpu_custom_call" | custom-call | flops 500000000 | bytes 500000 | tf_op jit(solution)/shard_map/attention_backward/pallas_call | solution.py:681
  289.7 0.5 collective-permute-start.15
  290.2 1.7 collective-permute-done.14
  291.8 0.8 collective-permute-done.15
  292.6 1.5 select_convert_fusion
  294.1 7.6 %collective-permute-start.16 = (bf16[128,2176]{1,0:T(8,128)(2,1)S(1)}, bf16[128,2176]{1,0:T(8,128)(2,1)S(1)}, u32[]{:S(2)}, u32[]{:S(2)}) collective-permute-start(bf16[128,2176]{1,0:T(8,128)(2,1)S(1)} %select_convert_fusion), channel_id=1, source_target_pairs={{0,2},{1,3},{2,0},{3,1},{4,6},{5,7},{6,4},{7,5},{8,10},{9,11},{10,... | collective-permute-start | bytes 1671176 | tf_op jit(solution)/shard_map/ppermute | solution.py:859
  301.8 12.9 %collective-permute-done.16 = bf16[128,2176]{1,0:T(8,128)(2,1)S(1)} collective-permute-done((bf16[128,2176]{1,0:T(8,128)(2,1)S(1)}, bf16[128,2176]{1,0:T(8,128)(2,1)S(1)}, u32[]{:S(2)}, u32[]{:S(2)}) %collective-permute-start.16) | collective-permute-done | bytes 557088 | tf_op jit(solution)/shard_map/ppermute | solution.py:859
  314.7 1.2 add_convert_fusion.2
  315.9 9.6 %all-to-all-start.6 = ((bf16[8,16,2176]{2,1,0:T(8,128)(2,1)}), bf16[8,16,2176]{2,1,0:T(8,128)(2,1)S(1)}, u32[]{:S(2)}, u32[]{:S(2)}) async-start(bf16[8,16,2176]{2,1,0:T(8,128)(2,1)} %bitcast.27), calls=%async_computation.6 | async-start | bytes 1114112 | tf_op jit(solution)/shard_map/all_to_all | solution.py:962
  325.4 15.1 %all-to-all-done.6 = bf16[8,16,2176]{2,1,0:T(8,128)(2,1)S(1)} async-done(((bf16[8,16,2176]{2,1,0:T(8,128)(2,1)}), bf16[8,16,2176]{2,1,0:T(8,128)(2,1)S(1)}, u32[]{:S(2)}, u32[]{:S(2)}) %all-to-all-start.6) | async-done | bytes 557088 | tf_op jit(solution)/shard_map/all_to_all | solution.py:962
  340.5 0.1 reduce_sum.12
  340.6 0.8 broadcast_in_dim.34
  341.5 3.6 %all-to-all-start.7 = ((bf16[8,16,2176]{2,1,0:T(8,128)(2,1)}), bf16[8,16,2176]{2,1,0:T(8,128)(2,1)S(1)}, u32[]{:S(2)}, u32[]{:S(2)}) async-start(bf16[8,16,2176]{2,1,0:T(8,128)(2,1)} %broadcast_in_dim.34), calls=%async_computation.7 | async-start | bytes 1114112 | tf_op jit(solution)/shard_map/all_to_all | solution.py:962
  345.1 1.7 convert_add_fusion
  346.8 0.6 fusion.9
  347.3 0.5 constant_dynamic-slice_fusion
  347.9 1.5 slice_bitcast_fusion
  349.3 11.0 %combine.1 = bf16[1600,512]{1,0:T(8,128)(2,1)} custom-call(s32[1600,2]{1,0:T(8,128)} %get-tuple-element.73.slot, f32[1600,512]{1,0:T(8,128)} %get-tuple-element.80.residual, bf16[8,2,208,512]{3,2,1,0:T(8,128)(2,1)} %bitcast.47, bf16[8,192,512]{2,1,0:T(8,128)(2,1)} %copy-done.4), custom_call_target="tpu_custom_call" | custom-call | flops 100000000 | bytes 100000 | tf_op jit(solution)/shard_map/combine/pallas_call | solution.py:738
  360.5 0.8 copy-done.7
  361.3 2.0 unpack.1
  (47 shorter events, 0.3 us)
Async XLA Ops:
  3.3 34.5 %copy-start.12 = (bf16[128,2176]{1,0:T(8,128)(2,1)S(1)}, bf16[128,2176]{1,0:T(8,128)(2,1)}, u32[]{:S(2)}) copy-start(bf16[128,2176]{1,0:T(8,128)(2,1)} %get-tuple-element.74) | copy-start | bytes 1671172
  3.3 26.4 %collective-permute-start = (bf16[128,2176]{1,0:T(8,128)(2,1)}, bf16[128,2176]{1,0:T(8,128)(2,1)S(1)}, u32[]{:S(2)}, u32[]{:S(2)}) collective-permute-start(bf16[128,2176]{1,0:T(8,128)(2,1)} %get-tuple-element.74), channel_id=1, source_target_pairs={{0,2},{1,3},{2,0},{3,1},{4,6},{5,7},{6,4},{7,5},{8,10},{9,11},{10,... | collective-permute-start | bytes 1671176 | tf_op jit(solution)/shard_map/ppermute | solution.py:859
  6.3 12.4 %collective-permute-start.2 = (bf16[480,512]{1,0:T(8,128)(2,1)}, bf16[480,512]{1,0:T(8,128)(2,1)S(1)}, u32[]{:S(2)}, u32[]{:S(2)}) collective-permute-start(bf16[480,512]{1,0:T(8,128)(2,1)} %get-tuple-element.76), channel_id=1, source_target_pairs={{2,18},{3,19},{6,22},{7,23},{8,24},{9,25},{12,28},{13,29},{18,2},{... | collective-permute-start | bytes 1474568 | tf_op jit(solution)/shard_map/ppermute | solution.py:859
  7.0 22.7 %collective-permute-start.1 = (bf16[480,512]{1,0:T(8,128)(2,1)}, bf16[480,512]{1,0:T(8,128)(2,1)S(1)}, u32[]{:S(2)}, u32[]{:S(2)}) collective-permute-start(bf16[480,512]{1,0:T(8,128)(2,1)} %get-tuple-element.76), channel_id=1, source_target_pairs={{0,18},{1,19},{2,0},{3,1},{4,22},{5,23},{6,4},{7,5},{8,10},{9,11},... | collective-permute-start | bytes 1474568 | tf_op jit(solution)/shard_map/ppermute | solution.py:859
  10.8 27.0 %collective-permute-start.3 = (bf16[128,2176]{1,0:T(8,128)(2,1)}, bf16[128,2176]{1,0:T(8,128)(2,1)S(1)}, u32[]{:S(2)}, u32[]{:S(2)}) collective-permute-start(bf16[128,2176]{1,0:T(8,128)(2,1)} %get-tuple-element.74), channel_id=1, source_target_pairs={{0,1},{1,0},{2,3},{3,2},{4,5},{5,4},{6,7},{7,6},{8,9},{9,8},{10,11... | collective-permute-start | bytes 1671176 | tf_op jit(solution)/shard_map/ppermute | solution.py:859
  18.7 11.0 %copy-start.13 = (bf16[480,512]{1,0:T(8,128)(2,1)}, bf16[480,512]{1,0:T(8,128)(2,1)S(1)}, u32[]{:S(2)}) copy-start(bf16[480,512]{1,0:T(8,128)(2,1)S(1)} %collective-permute-done.2) | copy-start | bytes 1474564
  29.7 0.8 copy-start.14
  30.5 7.3 %collective-permute-start.4 = (bf16[128,2176]{1,0:T(8,128)(2,1)S(1)}, bf16[128,2176]{1,0:T(8,128)(2,1)S(1)}, u32[]{:S(2)}, u32[]{:S(2)}) collective-permute-start(bf16[128,2176]{1,0:T(8,128)(2,1)S(1)} %collective-permute-done), channel_id=1, source_target_pairs={{0,1},{1,0},{2,3},{3,2},{4,5},{5,4},{6,7},{7,6},{8,9},{9,8},{10,11... | collective-permute-start | bytes 1671176 | tf_op jit(solution)/shard_map/ppermute | solution.py:859
  39.6 7.6 %copy-start.9 = (bf16[560,512]{1,0:T(8,128)(2,1)S(1)}, bf16[560,512]{1,0:T(8,128)(2,1)}, u32[]{:S(2)}) copy-start(bf16[560,512]{1,0:T(8,128)(2,1)} %get-tuple-element.83) | copy-start | bytes 1720324
  39.6 44.6 %all-to-all-start = ((bf16[8,224,512]{2,1,0:T(8,128)(2,1)}), bf16[8,224,512]{2,1,0:T(8,128)(2,1)S(1)}, u32[]{:S(2)}, u32[]{:S(2)}) async-start(bf16[8,224,512]{2,1,0:T(8,128)(2,1)} %dispatch.3), calls=%async_computation | async-start | bytes 3670016 | tf_op jit(solution)/shard_map/all_to_all | solution.py:878
  47.3 30.5 %collective-permute-start.6 = (bf16[560,512]{1,0:T(8,128)(2,1)S(1)}, bf16[560,512]{1,0:T(8,128)(2,1)S(1)}, u32[]{:S(2)}, u32[]{:S(2)}) collective-permute-start(bf16[560,512]{1,0:T(8,128)(2,1)S(1)} %copy-done.9), channel_id=1, source_target_pairs={{2,18},{3,19},{6,22},{7,23},{8,24},{9,25},{12,28},{13,29},{18,2},{... | collective-permute-start | bytes 1720328 | tf_op jit(solution)/shard_map/ppermute | solution.py:859
  48.0 36.2 %collective-permute-start.5 = (bf16[560,512]{1,0:T(8,128)(2,1)S(1)}, bf16[560,512]{1,0:T(8,128)(2,1)S(1)}, u32[]{:S(2)}, u32[]{:S(2)}) collective-permute-start(bf16[560,512]{1,0:T(8,128)(2,1)S(1)} %copy-done.9), channel_id=1, source_target_pairs={{0,18},{1,19},{2,0},{3,1},{4,22},{5,23},{6,4},{7,5},{8,10},{9,11},... | collective-permute-start | bytes 1720328 | tf_op jit(solution)/shard_map/ppermute | solution.py:859
  77.8 6.4 %copy-start.10 = (bf16[560,512]{1,0:T(8,128)(2,1)}, bf16[560,512]{1,0:T(8,128)(2,1)S(1)}, u32[]{:S(2)}) copy-start(bf16[560,512]{1,0:T(8,128)(2,1)S(1)} %collective-permute-done.6) | copy-start | bytes 1720324
  84.2 0.8 copy-start.11
  84.2 8.8 %copy-start.2 = (bf16[8,224,512]{2,1,0:T(8,128)(2,1)}, bf16[8,224,512]{2,1,0:T(8,128)(2,1)S(1)}, u32[]{:S(2)}) copy-start(bf16[8,224,512]{2,1,0:T(8,128)(2,1)S(1)} %all-to-all-done.refs_1_) | copy-start | bytes 5505028
  85.0 28.2 %all-to-all-start.1 = ((bf16[8,208,512]{2,1,0:T(8,128)(2,1)}), bf16[8,208,512]{2,1,0:T(8,128)(2,1)S(1)}, u32[]{:S(2)}, u32[]{:S(2)}) async-start(bf16[8,208,512]{2,1,0:T(8,128)(2,1)} %dispatch.4), calls=%async_computation.1 | async-start | bytes 3407872 | tf_op jit(solution)/shard_map/all_to_all | solution.py:878
  93.1 12.9 %collective-permute-start.9 = (bf16[560,512]{1,0:T(8,128)(2,1)}, bf16[560,512]{1,0:T(8,128)(2,1)S(1)}, u32[]{:S(2)}, u32[]{:S(2)}) collective-permute-start(bf16[560,512]{1,0:T(8,128)(2,1)} %get-tuple-element.144), channel_id=1, source_target_pairs={{0,1},{1,0},{2,3},{3,2},{4,5},{5,4},{6,7},{7,6},{8,9},{9,8},{10,11... | collective-permute-start | bytes 1720328 | tf_op jit(solution)/shard_map/ppermute | solution.py:859
  93.1 12.9 %collective-permute-start.10 = (bf16[560,512]{1,0:T(8,128)(2,1)}, bf16[560,512]{1,0:T(8,128)(2,1)S(1)}, u32[]{:S(2)}, u32[]{:S(2)}) collective-permute-start(bf16[560,512]{1,0:T(8,128)(2,1)} %get-tuple-element.145), channel_id=1, source_target_pairs={{0,1},{1,0},{2,3},{3,2},{4,5},{5,4},{6,7},{7,6},{8,9},{9,8},{10,11... | collective-permute-start | bytes 1720328 | tf_op jit(solution)/shard_map/ppermute | solution.py:859
  94.8 12.5 %collective-permute-start.7 = (bf16[480,512]{1,0:T(8,128)(2,1)S(1)}, bf16[480,512]{1,0:T(8,128)(2,1)}, u32[]{:S(2)}, u32[]{:S(2)}) collective-permute-start(bf16[480,512]{1,0:T(8,128)(2,1)S(1)} %get-tuple-element.146), channel_id=1, source_target_pairs={{0,1},{1,0},{2,3},{3,2},{4,5},{5,4},{6,7},{7,6},{8,9},{9,8},{10,11... | collective-permute-start | bytes 1474568 | tf_op jit(solution)/shard_map/ppermute | solution.py:859
  94.9 12.4 %collective-permute-start.8 = (bf16[480,512]{1,0:T(8,128)(2,1)S(1)}, bf16[480,512]{1,0:T(8,128)(2,1)}, u32[]{:S(2)}, u32[]{:S(2)}) collective-permute-start(bf16[480,512]{1,0:T(8,128)(2,1)S(1)} %get-tuple-element.147), channel_id=1, source_target_pairs={{0,1},{1,0},{2,3},{3,2},{4,5},{5,4},{6,7},{7,6},{8,9},{9,8},{10,11... | collective-permute-start | bytes 1474568 | tf_op jit(solution)/shard_map/ppermute | solution.py:859
  113.2 1.2 copy-start.3
  114.5 47.8 %all-to-all-start.2 = ((bf16[8,400,512]{2,1,0:T(8,128)(2,1)}), bf16[8,400,512]{2,1,0:T(8,128)(2,1)S(1)}, u32[]{:S(2)}, u32[]{:S(2)}) async-start(bf16[8,400,512]{2,1,0:T(8,128)(2,1)} %dispatch.5), calls=%async_computation.2 | async-start | bytes 6553600 | tf_op jit(solution)/shard_map/all_to_all | solution.py:878
  162.3 1.7 copy-start.1
  164.0 48.9 %all-to-all-start.3 = ((bf16[8,416,512]{2,1,0:T(8,128)(2,1)}), bf16[8,416,512]{2,1,0:T(8,128)(2,1)S(1)}, u32[]{:S(2)}, u32[]{:S(2)}) async-start(bf16[8,416,512]{2,1,0:T(8,128)(2,1)} %get-tuple-element.100), calls=%async_computation.3 | async-start | bytes 6815744 | tf_op jit(solution)/shard_map/all_to_all | solution.py:878
  208.5 10.2 %collective-permute-start.11 = (bf16[2,1040,512]{2,1,0:T(8,128)(2,1)}, bf16[2,1040,512]{2,1,0:T(8,128)(2,1)}, u32[]{:S(2)}, u32[]{:S(2)}) collective-permute-start(bf16[2,1040,512]{2,1,0:T(8,128)(2,1)} %get-tuple-element.108), channel_id=1, source_target_pairs={{0,1},{1,0},{2,3},{3,2},{4,5},{5,4},{6,7},{7,6},{8,9},{9,8},{10,11... | collective-permute-start | bytes 6389768 | tf_op jit(solution)/shard_map/ppermute | solution.py:859
  212.9 10.2 %copy-start = (bf16[8,416,512]{2,1,0:T(8,128)(2,1)}, bf16[8,416,512]{2,1,0:T(8,128)(2,1)S(1)}, u32[]{:S(2)}) copy-start(bf16[8,416,512]{2,1,0:T(8,128)(2,1)S(1)} %all-to-all-done.3) | copy-start | bytes 10223620
  212.9 25.6 %all-to-all-start.4 = ((bf16[8,192,512]{2,1,0:T(8,128)(2,1)}), bf16[8,192,512]{2,1,0:T(8,128)(2,1)}, u32[]{:S(2)}, u32[]{:S(2)}) async-start(bf16[8,192,512]{2,1,0:T(8,128)(2,1)} %get-tuple-element.105), calls=%async_computation.4 | async-start | bytes 3145728 | tf_op jit(solution)/shard_map/all_to_all | solution.py:878
  238.5 51.1 %collective-permute-start.12 = (bf16[1040,512]{1,0:T(8,128)(2,1)}, bf16[1040,512]{1,0:T(8,128)(2,1)S(1)}, u32[]{:S(2)}, u32[]{:S(2)}) collective-permute-start(bf16[1040,512]{1,0:T(8,128)(2,1)} %get-tuple-element.114), channel_id=1, source_target_pairs={{18,0},{19,1},{0,2},{1,3},{22,4},{23,5},{4,6},{5,7},{10,8},{11,9},... | collective-permute-start | bytes 3194888 | tf_op jit(solution)/shard_map/ppermute | solution.py:859
  238.9 50.7 %collective-permute-start.13 = (bf16[1040,512]{1,0:T(8,128)(2,1)}, bf16[1040,512]{1,0:T(8,128)(2,1)}, u32[]{:S(2)}, u32[]{:S(2)}) collective-permute-start(bf16[1040,512]{1,0:T(8,128)(2,1)} %get-tuple-element.115), channel_id=1, source_target_pairs={{2,18},{3,19},{6,22},{7,23},{8,24},{9,25},{12,28},{13,29},{18,2},{... | collective-permute-start | bytes 3194888 | tf_op jit(solution)/shard_map/ppermute | solution.py:859
  240.6 75.3 %all-to-all-start.5 = ((bf16[8,192,512]{2,1,0:T(8,128)(2,1)}), bf16[8,192,512]{2,1,0:T(8,128)(2,1)S(1)}, u32[]{:S(2)}, u32[]{:S(2)}) async-start(bf16[8,192,512]{2,1,0:T(8,128)(2,1)} %get-tuple-element.119), calls=%async_computation.5 | async-start | bytes 3145728 | tf_op jit(solution)/shard_map/all_to_all | solution.py:878
  289.6 25.2 %copy-start.5 = (bf16[256,2176]{1,0:T(8,128)(2,1)S(1)}, bf16[256,2176]{1,0:T(8,128)(2,1)}, u32[]{:S(2)}) copy-start(bf16[256,2176]{1,0:T(8,128)(2,1)} %get-tuple-element.116) | copy-start | bytes 3342340
  289.6 25.1 %copy-start.8 = (bf16[1040,512]{1,0:T(8,128)(2,1)}, bf16[1040,512]{1,0:T(8,128)(2,1)S(1)}, u32[]{:S(2)}) copy-start(bf16[1040,512]{1,0:T(8,128)(2,1)S(1)} %collective-permute-done.12) | copy-start | bytes 3194884
  289.6 2.2 collective-permute-start.14
  289.7 3.0 collective-permute-start.15
  294.1 20.6 %collective-permute-start.16 = (bf16[128,2176]{1,0:T(8,128)(2,1)S(1)}, bf16[128,2176]{1,0:T(8,128)(2,1)S(1)}, u32[]{:S(2)}, u32[]{:S(2)}) collective-permute-start(bf16[128,2176]{1,0:T(8,128)(2,1)S(1)} %select_convert_fusion), channel_id=1, source_target_pairs={{0,2},{1,3},{2,0},{3,1},{4,6},{5,7},{6,4},{7,5},{8,10},{9,11},{10,... | collective-permute-start | bytes 1671176 | tf_op jit(solution)/shard_map/ppermute | solution.py:859
  315.9 29.2 %copy-start.6 = (bf16[1040,512]{1,0:T(8,128)(2,1)S(1)}, bf16[1040,512]{1,0:T(8,128)(2,1)}, u32[]{:S(2)}) copy-start(bf16[1040,512]{1,0:T(8,128)(2,1)} %get-tuple-element.130) | copy-start | bytes 3194884
  315.9 30.9 %copy-start.4 = (bf16[8,192,512]{2,1,0:T(8,128)(2,1)}, bf16[8,192,512]{2,1,0:T(8,128)(2,1)S(1)}, u32[]{:S(2)}) copy-start(bf16[8,192,512]{2,1,0:T(8,128)(2,1)S(1)} %all-to-all-done.5.ret_b) | copy-start | bytes 4718596
  315.9 24.6 %all-to-all-start.6 = ((bf16[8,16,2176]{2,1,0:T(8,128)(2,1)}), bf16[8,16,2176]{2,1,0:T(8,128)(2,1)S(1)}, u32[]{:S(2)}, u32[]{:S(2)}) async-start(bf16[8,16,2176]{2,1,0:T(8,128)(2,1)} %bitcast.27), calls=%async_computation.6 | async-start | bytes 1114112 | tf_op jit(solution)/shard_map/all_to_all | solution.py:962
  341.5 19.0 %all-to-all-start.7 = ((bf16[8,16,2176]{2,1,0:T(8,128)(2,1)}), bf16[8,16,2176]{2,1,0:T(8,128)(2,1)S(1)}, u32[]{:S(2)}, u32[]{:S(2)}) async-start(bf16[8,16,2176]{2,1,0:T(8,128)(2,1)} %broadcast_in_dim.34), calls=%async_computation.7 | async-start | bytes 1114112 | tf_op jit(solution)/shard_map/all_to_all | solution.py:962
  360.5 0.8 copy-start.7

commit v6 on v5

--- a/solution.py
+++ b/solution.py
@@ -505,7 +505,7 @@
             hid[at, 0:LANES] = spread
             return carry
 
-        lax.fori_loop(0, steps, step, 0, unroll=8)
+        lax.fori_loop(0, steps, step, 0, unroll=4)
         drouter[...] = mm_tn(rows[...], hid[:, 0:LANES]) + (0.0 if old is None else old[2][...])
 
 

time: 365 us -> 365 us (level)
  no operation moved by 1% of the time
where the time goes in v6:
time: 365 us; the launch traced here: 363 us
  Pallas kernels  187 us (51%)
  starting transfers between devices  75.5 us (21%)
  waiting for transfers between devices  70.4 us (19%)
  other arithmetic  19.4 us (5%)
  local copies, waits for them, and re-layouts  10.1 us (3%)
    pallas_call x2, Pallas kernels, run_experts(): pl.pallas_call(partial(experts_kernel, block, bool(old)), grid=(steps,),...  81.2 us
    pallas_call x1, Pallas kernels, attention_backward(): pl.pallas_call(partial(backward_kernel, experts), grid=(images,), in_spec...  41.4 us
    all_to_all x6, starting transfers between devices, exchange(): lax.all_to_all(a, self.AXES, split_axis=0, concat_axis=0, axis_index_grou...  37.1 us
    ppermute x17, waiting for transfers between devices, send(): return lax.ppermute(a, self.AXES, pairs)  32.8 us
    ppermute x17, starting transfers between devices, send(): return lax.ppermute(a, self.AXES, pairs)  25.2 us
    pallas_call x3, Pallas kernels, dispatch(): pl.pallas_call(partial(dispatch_kernel, start, size, with_other), grid=(e...  23.9 us
    all_to_all x6, waiting for transfers between devices, exchange(): lax.all_to_all(a, self.AXES, split_axis=0, concat_axis=0, axis_index_grou...  22.4 us
    pallas_call x1, Pallas kernels, attention_forward(): pl.pallas_call(partial(attention_kernel, experts), grid=(images,), in_spe...  16.9 us
  transfers between devices with their start and end apart: 25, of which 11 were waited for; matrix products, arithmetic and copies ran while one was open for 6% of the time, Pallas kernels for 50%

profile of v6, /device:TPU:0, one launch (start us, length us, event | category | flops | bytes accessed | tf_op | source)
XLA Modules:
  0.0 363.3 jit_solution(2706400463889290655)
XLA Ops:
  0.7 2.7 pack.1
  3.3 2.9 collective-permute-start
  6.3 0.7 collective-permute-start.2
  7.0 3.8 %collective-permute-start.1 = (bf16[480,512]{1,0:T(8,128)(2,1)}, bf16[480,512]{1,0:T(8,128)(2,1)S(1)}, u32[]{:S(2)}, u32[]{:S(2)}) collective-permute-start(bf16[480,512]{1,0:T(8,128)(2,1)} %get-tuple-element.76), channel_id=1, source_target_pairs={{0,18},{1,19},{2,0},{3,1},{4,22},{5,23},{6,4},{7,5},{8,10},{9,11},... | collective-permute-start | bytes 1474568 | tf_op jit(solution)/shard_map/ppermute | solution.py:859
  10.8 7.9 %slots.1 = (s32[1600,2]{1,0:T(8,128)}, s32[2,1600]{1,0:T(2,128)}) custom-call(s32[1,1600]{1,0:T(1,128)} %prow.1, s32[2,1600]{1,0:T(2,128)} %bitcast.58, s32[1,8]{1,0:T(1,128)} %bitcast.70), custom_call_target="tpu_custom_call" | custom-call | flops 80000000 | bytes 80000 | tf_op jit(solution)/shard_map/slots/pallas_call | solution.py:208
  18.7 11.0 %collective-permute-done.1 = bf16[480,512]{1,0:T(8,128)(2,1)S(1)} collective-permute-done((bf16[480,512]{1,0:T(8,128)(2,1)}, bf16[480,512]{1,0:T(8,128)(2,1)S(1)}, u32[]{:S(2)}, u32[]{:S(2)}) %collective-permute-start.1) | collective-permute-done | bytes 491552 | tf_op jit(solution)/shard_map/ppermute | solution.py:859
  29.7 0.8 copy-done.14
  30.5 7.3 %dispatch.3 = bf16[8,224,512]{2,1,0:T(8,128)(2,1)} custom-call(s32[2,1600]{1,0:T(2,128)} %get-tuple-element.78.slot_rows, s32[2,1600]{1,0:T(2,128)} %bitcast.59, bf16[1600,512]{1,0:T(8,128)(2,1)} %up.1), custom_call_target="tpu_custom_call" | custom-call | flops 100000000 | bytes 100000 | tf_op jit(solution)/shard_map/dispatch/pallas_call | solution.py:255
  37.8 0.3 broadcast_select_fusion.10
  38.1 1.5 pad_maximum_fusion.small.wqkv.wout.refs_3_.refs_2_
  39.6 7.6 %all-to-all-start = ((bf16[8,224,512]{2,1,0:T(8,128)(2,1)}), bf16[8,224,512]{2,1,0:T(8,128)(2,1)S(1)}, u32[]{:S(2)}, u32[]{:S(2)}) async-start(bf16[8,224,512]{2,1,0:T(8,128)(2,1)} %dispatch.3), calls=%async_computation | async-start | bytes 3670016 | tf_op jit(solution)/shard_map/all_to_all | solution.py:878
  47.3 0.7 collective-permute-start.6
  48.0 5.6 %collective-permute-start.5 = (bf16[560,512]{1,0:T(8,128)(2,1)S(1)}, bf16[560,512]{1,0:T(8,128)(2,1)S(1)}, u32[]{:S(2)}, u32[]{:S(2)}) collective-permute-start(bf16[560,512]{1,0:T(8,128)(2,1)S(1)} %copy-done.9), channel_id=1, source_target_pairs={{0,18},{1,19},{2,0},{3,1},{4,22},{5,23},{6,4},{7,5},{8,10},{9,11},... | collective-permute-start | bytes 1720328 | tf_op jit(solution)/shard_map/ppermute | solution.py:859
  53.6 1.3 reshape.105.mask
  54.9 16.9 %attention_forward.1 = (bf16[1600,1536]{1,0:T(8,128)(2,1)}, bf16[1600,512]{1,0:T(8,128)(2,1)}, f32[8,8,200]{2,1,0:T(8,128)}, f32[1600,512]{1,0:T(8,128)}, bf16[1600,512]{1,0:T(8,128)(2,1)}) custom-call(bf16[1600,512]{1,0:T(8,128)(2,1)} %x.3, s32[8,1,200]{2,1,0:T(1,128)} %reshape.105.mask, bf16[512,2176]{1,0:T(8,128)(2,1)} %pad_maximum_fusion.small.wqkv.wout.refs_3_.refs_2_, ...), custom_call_target="tpu_custom_call" | custom-call | flops 170000000 | bytes 170000 | tf_op jit(solution)/shard_map/attention_forward/pallas_call | solution.py:331
  71.8 6.0 %dispatch.4 = bf16[8,208,512]{2,1,0:T(8,128)(2,1)} custom-call(s32[2,1600]{1,0:T(2,128)} %get-tuple-element.78.slot_rows, s32[2,1600]{1,0:T(2,128)} %bitcast.60, bf16[1600,512]{1,0:T(8,128)(2,1)} %get-tuple-element.81.refs_0_), custom_call_target="tpu_custom_call" | custom-call | flops 100000000 | bytes 100000 | tf_op jit(solution)/shard_map/dispatch/pallas_call | solution.py:255
  77.8 6.4 %collective-permute-done.5 = bf16[560,512]{1,0:T(8,128)(2,1)S(1)} collective-permute-done((bf16[560,512]{1,0:T(8,128)(2,1)S(1)}, bf16[560,512]{1,0:T(8,128)(2,1)S(1)}, u32[]{:S(2)}, u32[]{:S(2)}) %collective-permute-start.5) | collective-permute-done | bytes 573472 | tf_op jit(solution)/shard_map/ppermute | solution.py:859
  84.2 0.8 copy-done.11
  85.0 5.7 %all-to-all-start.1 = ((bf16[8,208,512]{2,1,0:T(8,128)(2,1)}), bf16[8,208,512]{2,1,0:T(8,128)(2,1)S(1)}, u32[]{:S(2)}, u32[]{:S(2)}) async-start(bf16[8,208,512]{2,1,0:T(8,128)(2,1)} %dispatch.4), calls=%async_computation.1 | async-start | bytes 3407872 | tf_op jit(solution)/shard_map/all_to_all | solution.py:878
  90.7 2.3 broadcast_select_fusion.2
  93.1 0.5 collective-permute-start.10
  93.6 1.3 broadcast_select_fusion.12
  94.8 0.1 collective-permute-start.7
  94.9 0.5 collective-permute-start.8
  95.4 10.6 %dispatch.5 = bf16[8,400,512]{2,1,0:T(8,128)(2,1)} custom-call(s32[2,1600]{1,0:T(2,128)} %get-tuple-element.78.slot_rows, s32[2,1600]{1,0:T(2,128)} %bitcast.61, bf16[1600,512]{1,0:T(8,128)(2,1)} %get-tuple-element.81.refs_0_, bf16[1600,512]{1,0:T(8,128)(2,1)} %up.1), custom_call_target="tpu_custom_call" | custom-call | flops 100000000 | bytes 100000 | tf_op jit(solution)/shard_map/dispatch/pallas_call | solution.py:255
  106.0 0.7 fusion.2
  106.7 0.6 pad_maximum_fusion.4
  107.3 3.4 maximum_maximum_fusion.refs_4_.refs_5_.refs_6_.refs_3_
  110.7 2.5 all-to-all-done.1
  113.2 1.2 copy-done.3
  114.5 5.0 %all-to-all-start.2 = ((bf16[8,400,512]{2,1,0:T(8,128)(2,1)}), bf16[8,400,512]{2,1,0:T(8,128)(2,1)S(1)}, u32[]{:S(2)}, u32[]{:S(2)}) async-start(bf16[8,400,512]{2,1,0:T(8,128)(2,1)} %dispatch.5), calls=%async_computation.2 | async-start | bytes 6553600 | tf_op jit(solution)/shard_map/all_to_all | solution.py:878
  119.5 0.5 compare_convert_fusion.refs_2_.refs_1_
  120.0 41.5 %experts.2 = (bf16[8,416,512]{2,1,0:T(8,128)(2,1)}, bf16[2,1040,512]{2,1,0:T(8,128)(2,1)}, bf16[2,1040,512]{2,1,0:T(8,128)(2,1)}, f32[512,128]{1,0:T(8,128)}) custom-call(bf16[1664,512]{1,0:T(8,128)(2,1)} %bitcast.48, bf16[8,224,512]{2,1,0:T(8,128)(2,1)} %copy-done.2, f32[1,128]{1,0:T(1,128)} %compare_convert_fusion.refs_2_.refs_1_, ...), custom_call_target="tpu_custom_call" | custom-call | flops 500000000 | bytes 500000 | tf_op jit(solution)/shard_map/experts/pallas_call | solution.py:541
  161.5 0.8 all-to-all-done.2.refs_0_
  162.3 1.7 copy-done.1
  164.0 5.4 %all-to-all-start.3 = ((bf16[8,416,512]{2,1,0:T(8,128)(2,1)}), bf16[8,416,512]{2,1,0:T(8,128)(2,1)S(1)}, u32[]{:S(2)}, u32[]{:S(2)}) async-start(bf16[8,416,512]{2,1,0:T(8,128)(2,1)} %get-tuple-element.100), calls=%async_computation.3 | async-start | bytes 6815744 | tf_op jit(solution)/shard_map/all_to_all | solution.py:878
  169.3 39.8 %experts.3 = (bf16[8,192,512]{2,1,0:T(8,128)(2,1)}, bf16[8,192,512]{2,1,0:T(8,128)(2,1)}, bf16[2,1040,512]{2,1,0:T(8,128)(2,1)}, bf16[2,1040,512]{2,1,0:T(8,128)(2,1)}, f32[512,128]{1,0:T(8,128)}) custom-call(bf16[8,400,512]{2,1,0:T(8,128)(2,1)} %copy-done.1, f32[1,128]{1,0:T(1,128)} %compare_convert_fusion.refs_2_.refs_1_, ...), custom_call_target="tpu_custom_call" | custom-call | flops 500000000 | bytes 500000 | tf_op jit(solution)/shard_map/experts/pallas_call | solution.py:541
  209.2 3.7 %all-to-all-done.3 = bf16[8,416,512]{2,1,0:T(8,128)(2,1)S(1)} async-done(((bf16[8,416,512]{2,1,0:T(8,128)(2,1)}), bf16[8,416,512]{2,1,0:T(8,128)(2,1)S(1)}, u32[]{:S(2)}, u32[]{:S(2)}) %all-to-all-start.3) | async-done | bytes 3407904 | tf_op jit(solution)/shard_map/all_to_all | solution.py:878
  212.9 5.8 %all-to-all-start.4 = ((bf16[8,192,512]{2,1,0:T(8,128)(2,1)}), bf16[8,192,512]{2,1,0:T(8,128)(2,1)}, u32[]{:S(2)}, u32[]{:S(2)}) async-start(bf16[8,192,512]{2,1,0:T(8,128)(2,1)} %get-tuple-element.105), calls=%async_computation.4 | async-start | bytes 3145728 | tf_op jit(solution)/shard_map/all_to_all | solution.py:878
  218.7 4.4 %broadcast_select_fusion = (bf16[1040,512]{1,0:T(8,128)(2,1)}, bf16[1040,512]{1,0:T(8,128)(2,1)}, bf16[1040,512]{1,0:T(8,128)(2,1)}) fusion(pred[]{:T(512)S(6)} %ne.53, bf16[2,1040,512]{2,1,0:T(8,128)(2,1)} %collective-permute-done.11, bf16[2,1040,512]{2,1,0:T(8,128)(2,1)} %get-tuple-element.107), kind=kLoop, calls=%fused_computation.11 | loop fusion | flops 4792320 | bytes 7454721 | tf_op jit(solution)/shard_map/jit(_where)/select_n | solution.py:932
  223.1 15.4 %all-to-all-done.4.ret_b = bf16[8,192,512]{2,1,0:T(8,128)(2,1)} async-done(((bf16[8,192,512]{2,1,0:T(8,128)(2,1)}), bf16[8,192,512]{2,1,0:T(8,128)(2,1)}, u32[]{:S(2)}, u32[]{:S(2)}) %all-to-all-start.4) | async-done | bytes 1572896 | tf_op jit(solution)/shard_map/all_to_all | solution.py:878
  238.5 0.4 collective-permute-start.12
  238.9 1.6 collective-permute-start.13
  240.6 7.6 %all-to-all-start.5 = ((bf16[8,192,512]{2,1,0:T(8,128)(2,1)}), bf16[8,192,512]{2,1,0:T(8,128)(2,1)S(1)}, u32[]{:S(2)}, u32[]{:S(2)}) async-start(bf16[8,192,512]{2,1,0:T(8,128)(2,1)} %get-tuple-element.119), calls=%async_computation.5 | async-start | bytes 3145728 | tf_op jit(solution)/shard_map/all_to_all | solution.py:878
  248.2 41.4 %attention_backward.1 = (f32[1600,512]{1,0:T(8,128)}, bf16[256,2176]{1,0:T(8,128)(2,1)}, bf16[128,2176]{1,0:T(8,128)(2,1)}, bf16[128,2176]{1,0:T(8,128)(2,1)}) custom-call(bf16[1600,512]{1,0:T(8,128)(2,1)} %x.3, s32[8,1,200]{2,1,0:T(1,128)} %reshape.105.mask, bf16[512,2176]{1,0:T(8,128)(2,1)} %pad_maximum_fusion.small.wqkv.wout.refs_3_.refs_2_, ...), custom_call_target="tpu_custom_call" | custom-call | flops 500000000 | bytes 500000 | tf_op jit(solution)/shard_map/attention_backward/pallas_call | solution.py:681
  289.7 0.5 collective-permute-start.15
  290.2 1.7 collective-permute-done.14
  291.8 0.8 collective-permute-done.15
  292.6 1.5 select_convert_fusion
  294.1 7.6 %collective-permute-start.16 = (bf16[128,2176]{1,0:T(8,128)(2,1)S(1)}, bf16[128,2176]{1,0:T(8,128)(2,1)S(1)}, u32[]{:S(2)}, u32[]{:S(2)}) collective-permute-start(bf16[128,2176]{1,0:T(8,128)(2,1)S(1)} %select_convert_fusion), channel_id=1, source_target_pairs={{0,2},{1,3},{2,0},{3,1},{4,6},{5,7},{6,4},{7,5},{8,10},{9,11},{10,... | collective-permute-start | bytes 1671176 | tf_op jit(solution)/shard_map/ppermute | solution.py:859
  301.8 12.9 %collective-permute-done.16 = bf16[128,2176]{1,0:T(8,128)(2,1)S(1)} collective-permute-done((bf16[128,2176]{1,0:T(8,128)(2,1)S(1)}, bf16[128,2176]{1,0:T(8,128)(2,1)S(1)}, u32[]{:S(2)}, u32[]{:S(2)}) %collective-permute-start.16) | collective-permute-done | bytes 557088 | tf_op jit(solution)/shard_map/ppermute | solution.py:859
  314.7 1.2 add_convert_fusion.2
  315.9 9.6 %all-to-all-start.6 = ((bf16[8,16,2176]{2,1,0:T(8,128)(2,1)}), bf16[8,16,2176]{2,1,0:T(8,128)(2,1)S(1)}, u32[]{:S(2)}, u32[]{:S(2)}) async-start(bf16[8,16,2176]{2,1,0:T(8,128)(2,1)} %bitcast.27), calls=%async_computation.6 | async-start | bytes 1114112 | tf_op jit(solution)/shard_map/all_to_all | solution.py:962
  325.4 15.1 %all-to-all-done.6 = bf16[8,16,2176]{2,1,0:T(8,128)(2,1)S(1)} async-done(((bf16[8,16,2176]{2,1,0:T(8,128)(2,1)}), bf16[8,16,2176]{2,1,0:T(8,128)(2,1)S(1)}, u32[]{:S(2)}, u32[]{:S(2)}) %all-to-all-start.6) | async-done | bytes 557088 | tf_op jit(solution)/shard_map/all_to_all | solution.py:962
  340.5 0.1 reduce_sum.12
  340.6 0.8 broadcast_in_dim.34
  341.5 3.6 %all-to-all-start.7 = ((bf16[8,16,2176]{2,1,0:T(8,128)(2,1)}), bf16[8,16,2176]{2,1,0:T(8,128)(2,1)S(1)}, u32[]{:S(2)}, u32[]{:S(2)}) async-start(bf16[8,16,2176]{2,1,0:T(8,128)(2,1)} %broadcast_in_dim.34), calls=%async_computation.7 | async-start | bytes 1114112 | tf_op jit(solution)/shard_map/all_to_all | solution.py:962
  345.1 1.7 convert_add_fusion
  346.8 0.6 fusion.9
  347.3 0.5 constant_dynamic-slice_fusion
  347.9 1.5 slice_bitcast_fusion
  349.3 11.0 %combine.1 = bf16[1600,512]{1,0:T(8,128)(2,1)} custom-call(s32[1600,2]{1,0:T(8,128)} %get-tuple-element.73.slot, f32[1600,512]{1,0:T(8,128)} %get-tuple-element.80.residual, bf16[8,2,208,512]{3,2,1,0:T(8,128)(2,1)} %bitcast.47, bf16[8,192,512]{2,1,0:T(8,128)(2,1)} %copy-done.4), custom_call_target="tpu_custom_call" | custom-call | flops 100000000 | bytes 100000 | tf_op jit(solution)/shard_map/combine/pallas_call | solution.py:738
  360.5 0.8 copy-done.7
  361.3 2.0 unpack.1
  (47 shorter events, 0.3 us)
Async XLA Ops:
  3.3 34.5 %copy-start.12 = (bf16[128,2176]{1,0:T(8,128)(2,1)S(1)}, bf16[128,2176]{1,0:T(8,128)(2,1)}, u32[]{:S(2)}) copy-start(bf16[128,2176]{1,0:T(8,128)(2,1)} %get-tuple-element.74) | copy-start | bytes 1671172
  3.3 26.4 %collective-permute-start = (bf16[128,2176]{1,0:T(8,128)(2,1)}, bf16[128,2176]{1,0:T(8,128)(2,1)S(1)}, u32[]{:S(2)}, u32[]{:S(2)}) collective-permute-start(bf16[128,2176]{1,0:T(8,128)(2,1)} %get-tuple-element.74), channel_id=1, source_target_pairs={{0,2},{1,3},{2,0},{3,1},{4,6},{5,7},{6,4},{7,5},{8,10},{9,11},{10,... | collective-permute-start | bytes 1671176 | tf_op jit(solution)/shard_map/ppermute | solution.py:859
  6.3 12.4 %collective-permute-start.2 = (bf16[480,512]{1,0:T(8,128)(2,1)}, bf16[480,512]{1,0:T(8,128)(2,1)S(1)}, u32[]{:S(2)}, u32[]{:S(2)}) collective-permute-start(bf16[480,512]{1,0:T(8,128)(2,1)} %get-tuple-element.76), channel_id=1, source_target_pairs={{2,18},{3,19},{6,22},{7,23},{8,24},{9,25},{12,28},{13,29},{18,2},{... | collective-permute-start | bytes 1474568 | tf_op jit(solution)/shard_map/ppermute | solution.py:859
  7.0 22.7 %collective-permute-start.1 = (bf16[480,512]{1,0:T(8,128)(2,1)}, bf16[480,512]{1,0:T(8,128)(2,1)S(1)}, u32[]{:S(2)}, u32[]{:S(2)}) collective-permute-start(bf16[480,512]{1,0:T(8,128)(2,1)} %get-tuple-element.76), channel_id=1, source_target_pairs={{0,18},{1,19},{2,0},{3,1},{4,22},{5,23},{6,4},{7,5},{8,10},{9,11},... | collective-permute-start | bytes 1474568 | tf_op jit(solution)/shard_map/ppermute | solution.py:859
  10.8 27.0 %collective-permute-start.3 = (bf16[128,2176]{1,0:T(8,128)(2,1)}, bf16[128,2176]{1,0:T(8,128)(2,1)S(1)}, u32[]{:S(2)}, u32[]{:S(2)}) collective-permute-start(bf16[128,2176]{1,0:T(8,128)(2,1)} %get-tuple-element.74), channel_id=1, source_target_pairs={{0,1},{1,0},{2,3},{3,2},{4,5},{5,4},{6,7},{7,6},{8,9},{9,8},{10,11... | collective-permute-start | bytes 1671176 | tf_op jit(solution)/shard_map/ppermute | solution.py:859
  18.7 11.0 %copy-start.13 = (bf16[480,512]{1,0:T(8,128)(2,1)}, bf16[480,512]{1,0:T(8,128)(2,1)S(1)}, u32[]{:S(2)}) copy-start(bf16[480,512]{1,0:T(8,128)(2,1)S(1)} %collective-permute-done.2) | copy-start | bytes 1474564
  29.7 0.8 copy-start.14
  30.5 7.3 %collective-permute-start.4 = (bf16[128,2176]{1,0:T(8,128)(2,1)S(1)}, bf16[128,2176]{1,0:T(8,128)(2,1)S(1)}, u32[]{:S(2)}, u32[]{:S(2)}) collective-permute-start(bf16[128,2176]{1,0:T(8,128)(2,1)S(1)} %collective-permute-done), channel_id=1, source_target_pairs={{0,1},{1,0},{2,3},{3,2},{4,5},{5,4},{6,7},{7,6},{8,9},{9,8},{10,11... | collective-permute-start | bytes 1671176 | tf_op jit(solution)/shard_map/ppermute | solution.py:859
  39.6 7.6 %copy-start.9 = (bf16[560,512]{1,0:T(8,128)(2,1)S(1)}, bf16[560,512]{1,0:T(8,128)(2,1)}, u32[]{:S(2)}) copy-start(bf16[560,512]{1,0:T(8,128)(2,1)} %get-tuple-element.83) | copy-start | bytes 1720324
  39.6 44.6 %all-to-all-start = ((bf16[8,224,512]{2,1,0:T(8,128)(2,1)}), bf16[8,224,512]{2,1,0:T(8,128)(2,1)S(1)}, u32[]{:S(2)}, u32[]{:S(2)}) async-start(bf16[8,224,512]{2,1,0:T(8,128)(2,1)} %dispatch.3), calls=%async_computation | async-start | bytes 3670016 | tf_op jit(solution)/shard_map/all_to_all | solution.py:878
  47.3 30.5 %collective-permute-start.6 = (bf16[560,512]{1,0:T(8,128)(2,1)S(1)}, bf16[560,512]{1,0:T(8,128)(2,1)S(1)}, u32[]{:S(2)}, u32[]{:S(2)}) collective-permute-start(bf16[560,512]{1,0:T(8,128)(2,1)S(1)} %copy-done.9), channel_id=1, source_target_pairs={{2,18},{3,19},{6,22},{7,23},{8,24},{9,25},{12,28},{13,29},{18,2},{... | collective-permute-start | bytes 1720328 | tf_op jit(solution)/shard_map/ppermute | solution.py:859
  48.0 36.2 %collective-permute-start.5 = (bf16[560,512]{1,0:T(8,128)(2,1)S(1)}, bf16[560,512]{1,0:T(8,128)(2,1)S(1)}, u32[]{:S(2)}, u32[]{:S(2)}) collective-permute-start(bf16[560,512]{1,0:T(8,128)(2,1)S(1)} %copy-done.9), channel_id=1, source_target_pairs={{0,18},{1,19},{2,0},{3,1},{4,22},{5,23},{6,4},{7,5},{8,10},{9,11},... | collective-permute-start | bytes 1720328 | tf_op jit(solution)/shard_map/ppermute | solution.py:859
  77.8 6.4 %copy-start.10 = (bf16[560,512]{1,0:T(8,128)(2,1)}, bf16[560,512]{1,0:T(8,128)(2,1)S(1)}, u32[]{:S(2)}) copy-start(bf16[560,512]{1,0:T(8,128)(2,1)S(1)} %collective-permute-done.6) | copy-start | bytes 1720324
  84.2 0.8 copy-start.11
  84.2 8.8 %copy-start.2 = (bf16[8,224,512]{2,1,0:T(8,128)(2,1)}, bf16[8,224,512]{2,1,0:T(8,128)(2,1)S(1)}, u32[]{:S(2)}) copy-start(bf16[8,224,512]{2,1,0:T(8,128)(2,1)S(1)} %all-to-all-done.refs_1_) | copy-start | bytes 5505028
  85.0 28.2 %all-to-all-start.1 = ((bf16[8,208,512]{2,1,0:T(8,128)(2,1)}), bf16[8,208,512]{2,1,0:T(8,128)(2,1)S(1)}, u32[]{:S(2)}, u32[]{:S(2)}) async-start(bf16[8,208,512]{2,1,0:T(8,128)(2,1)} %dispatch.4), calls=%async_computation.1 | async-start | bytes 3407872 | tf_op jit(solution)/shard_map/all_to_all | solution.py:878
  93.1 12.9 %collective-permute-start.9 = (bf16[560,512]{1,0:T(8,128)(2,1)}, bf16[560,512]{1,0:T(8,128)(2,1)S(1)}, u32[]{:S(2)}, u32[]{:S(2)}) collective-permute-start(bf16[560,512]{1,0:T(8,128)(2,1)} %get-tuple-element.144), channel_id=1, source_target_pairs={{0,1},{1,0},{2,3},{3,2},{4,5},{5,4},{6,7},{7,6},{8,9},{9,8},{10,11... | collective-permute-start | bytes 1720328 | tf_op jit(solution)/shard_map/ppermute | solution.py:859
  93.1 12.9 %collective-permute-start.10 = (bf16[560,512]{1,0:T(8,128)(2,1)}, bf16[560,512]{1,0:T(8,128)(2,1)S(1)}, u32[]{:S(2)}, u32[]{:S(2)}) collective-permute-start(bf16[560,512]{1,0:T(8,128)(2,1)} %get-tuple-element.145), channel_id=1, source_target_pairs={{0,1},{1,0},{2,3},{3,2},{4,5},{5,4},{6,7},{7,6},{8,9},{9,8},{10,11... | collective-permute-start | bytes 1720328 | tf_op jit(solution)/shard_map/ppermute | solution.py:859
  94.8 12.5 %collective-permute-start.7 = (bf16[480,512]{1,0:T(8,128)(2,1)S(1)}, bf16[480,512]{1,0:T(8,128)(2,1)}, u32[]{:S(2)}, u32[]{:S(2)}) collective-permute-start(bf16[480,512]{1,0:T(8,128)(2,1)S(1)} %get-tuple-element.146), channel_id=1, source_target_pairs={{0,1},{1,0},{2,3},{3,2},{4,5},{5,4},{6,7},{7,6},{8,9},{9,8},{10,11... | collective-permute-start | bytes 1474568 | tf_op jit(solution)/shard_map/ppermute | solution.py:859
  94.9 12.4 %collective-permute-start.8 = (bf16[480,512]{1,0:T(8,128)(2,1)S(1)}, bf16[480,512]{1,0:T(8,128)(2,1)}, u32[]{:S(2)}, u32[]{:S(2)}) collective-permute-start(bf16[480,512]{1,0:T(8,128)(2,1)S(1)} %get-tuple-element.147), channel_id=1, source_target_pairs={{0,1},{1,0},{2,3},{3,2},{4,5},{5,4},{6,7},{7,6},{8,9},{9,8},{10,11... | collective-permute-start | bytes 1474568 | tf_op jit(solution)/shard_map/ppermute | solution.py:859
  113.2 1.2 copy-start.3
  114.5 47.8 %all-to-all-start.2 = ((bf16[8,400,512]{2,1,0:T(8,128)(2,1)}), bf16[8,400,512]{2,1,0:T(8,128)(2,1)S(1)}, u32[]{:S(2)}, u32[]{:S(2)}) async-start(bf16[8,400,512]{2,1,0:T(8,128)(2,1)} %dispatch.5), calls=%async_computation.2 | async-start | bytes 6553600 | tf_op jit(solution)/shard_map/all_to_all | solution.py:878
  162.3 1.7 copy-start.1
  164.0 48.9 %all-to-all-start.3 = ((bf16[8,416,512]{2,1,0:T(8,128)(2,1)}), bf16[8,416,512]{2,1,0:T(8,128)(2,1)S(1)}, u32[]{:S(2)}, u32[]{:S(2)}) async-start(bf16[8,416,512]{2,1,0:T(8,128)(2,1)} %get-tuple-element.100), calls=%async_computation.3 | async-start | bytes 6815744 | tf_op jit(solution)/shard_map/all_to_all | solution.py:878
  209.1 9.6 %collective-permute-start.11 = (bf16[2,1040,512]{2,1,0:T(8,128)(2,1)}, bf16[2,1040,512]{2,1,0:T(8,128)(2,1)}, u32[]{:S(2)}, u32[]{:S(2)}) collective-permute-start(bf16[2,1040,512]{2,1,0:T(8,128)(2,1)} %get-tuple-element.108), channel_id=1, source_target_pairs={{0,1},{1,0},{2,3},{3,2},{4,5},{5,4},{6,7},{7,6},{8,9},{9,8},{10,11... | collective-permute-start | bytes 6389768 | tf_op jit(solution)/shard_map/ppermute | solution.py:859
  212.9 10.2 %copy-start = (bf16[8,416,512]{2,1,0:T(8,128)(2,1)}, bf16[8,416,512]{2,1,0:T(8,128)(2,1)S(1)}, u32[]{:S(2)}) copy-start(bf16[8,416,512]{2,1,0:T(8,128)(2,1)S(1)} %all-to-all-done.3) | copy-start | bytes 10223620
  212.9 25.6 %all-to-all-start.4 = ((bf16[8,192,512]{2,1,0:T(8,128)(2,1)}), bf16[8,192,512]{2,1,0:T(8,128)(2,1)}, u32[]{:S(2)}, u32[]{:S(2)}) async-start(bf16[8,192,512]{2,1,0:T(8,128)(2,1)} %get-tuple-element.105), calls=%async_computation.4 | async-start | bytes 3145728 | tf_op jit(solution)/shard_map/all_to_all | solution.py:878
  238.5 51.1 %collective-permute-start.12 = (bf16[1040,512]{1,0:T(8,128)(2,1)}, bf16[1040,512]{1,0:T(8,128)(2,1)S(1)}, u32[]{:S(2)}, u32[]{:S(2)}) collective-permute-start(bf16[1040,512]{1,0:T(8,128)(2,1)} %get-tuple-element.114), channel_id=1, source_target_pairs={{18,0},{19,1},{0,2},{1,3},{22,4},{23,5},{4,6},{5,7},{10,8},{11,9},... | collective-permute-start | bytes 3194888 | tf_op jit(solution)/shard_map/ppermute | solution.py:859
  238.9 50.7 %collective-permute-start.13 = (bf16[1040,512]{1,0:T(8,128)(2,1)}, bf16[1040,512]{1,0:T(8,128)(2,1)}, u32[]{:S(2)}, u32[]{:S(2)}) collective-permute-start(bf16[1040,512]{1,0:T(8,128)(2,1)} %get-tuple-element.115), channel_id=1, source_target_pairs={{2,18},{3,19},{6,22},{7,23},{8,24},{9,25},{12,28},{13,29},{18,2},{... | collective-permute-start | bytes 3194888 | tf_op jit(solution)/shard_map/ppermute | solution.py:859
  240.6 75.3 %all-to-all-start.5 = ((bf16[8,192,512]{2,1,0:T(8,128)(2,1)}), bf16[8,192,512]{2,1,0:T(8,128)(2,1)S(1)}, u32[]{:S(2)}, u32[]{:S(2)}) async-start(bf16[8,192,512]{2,1,0:T(8,128)(2,1)} %get-tuple-element.119), calls=%async_computation.5 | async-start | bytes 3145728 | tf_op jit(solution)/shard_map/all_to_all | solution.py:878
  289.6 25.2 %copy-start.5 = (bf16[256,2176]{1,0:T(8,128)(2,1)S(1)}, bf16[256,2176]{1,0:T(8,128)(2,1)}, u32[]{:S(2)}) copy-start(bf16[256,2176]{1,0:T(8,128)(2,1)} %get-tuple-element.116) | copy-start | bytes 3342340
  289.6 25.1 %copy-start.8 = (bf16[1040,512]{1,0:T(8,128)(2,1)}, bf16[1040,512]{1,0:T(8,128)(2,1)S(1)}, u32[]{:S(2)}) copy-start(bf16[1040,512]{1,0:T(8,128)(2,1)S(1)} %collective-permute-done.12) | copy-start | bytes 3194884
  289.6 2.2 collective-permute-start.14
  289.7 3.0 collective-permute-start.15
  294.1 20.6 %collective-permute-start.16 = (bf16[128,2176]{1,0:T(8,128)(2,1)S(1)}, bf16[128,2176]{1,0:T(8,128)(2,1)S(1)}, u32[]{:S(2)}, u32[]{:S(2)}) collective-permute-start(bf16[128,2176]{1,0:T(8,128)(2,1)S(1)} %select_convert_fusion), channel_id=1, source_target_pairs={{0,2},{1,3},{2,0},{3,1},{4,6},{5,7},{6,4},{7,5},{8,10},{9,11},{10,... | collective-permute-start | bytes 1671176 | tf_op jit(solution)/shard_map/ppermute | solution.py:859
  315.9 29.2 %copy-start.6 = (bf16[1040,512]{1,0:T(8,128)(2,1)S(1)}, bf16[1040,512]{1,0:T(8,128)(2,1)}, u32[]{:S(2)}) copy-start(bf16[1040,512]{1,0:T(8,128)(2,1)} %get-tuple-element.130) | copy-start | bytes 3194884
  315.9 30.9 %copy-start.4 = (bf16[8,192,512]{2,1,0:T(8,128)(2,1)}, bf16[8,192,512]{2,1,0:T(8,128)(2,1)S(1)}, u32[]{:S(2)}) copy-start(bf16[8,192,512]{2,1,0:T(8,128)(2,1)S(1)} %all-to-all-done.5.ret_b) | copy-start | bytes 4718596
  315.9 24.6 %all-to-all-start.6 = ((bf16[8,16,2176]{2,1,0:T(8,128)(2,1)}), bf16[8,16,2176]{2,1,0:T(8,128)(2,1)S(1)}, u32[]{:S(2)}, u32[]{:S(2)}) async-start(bf16[8,16,2176]{2,1,0:T(8,128)(2,1)} %bitcast.27), calls=%async_computation.6 | async-start | bytes 1114112 | tf_op jit(solution)/shard_map/all_to_all | solution.py:962
  341.5 19.0 %all-to-all-start.7 = ((bf16[8,16,2176]{2,1,0:T(8,128)(2,1)}), bf16[8,16,2176]{2,1,0:T(8,128)(2,1)S(1)}, u32[]{:S(2)}, u32[]{:S(2)}) async-start(bf16[8,16,2176]{2,1,0:T(8,128)(2,1)} %broadcast_in_dim.34), calls=%async_computation.7 | async-start | bytes 1114112 | tf_op jit(solution)/shard_map/all_to_all | solution.py:962
  360.5 0.8 copy-start.7
